TPU v7x, 32 devices: a whole 2x2x4 slice. The times are simulated.
32 devices in a mesh: win: 2 (over x), tile: 16 (over z, y, core).
Axes of the slice: x: 2, y: 2, z: 4, core: 2. Of those that a mesh axis runs over, the one named last changes fastest.
Arguments:
- mask: float32 [512, 4096], P('win', 'tile'), parts along dimension 0, may hold values from -1 to 1
- target: float32 [512, 4096], P('win', 'tile'), parts along dimension 0, may hold values from 0 to 1
- kernel_table: float32 [4, 2, 2, 64, 64], replicated, may hold values from -48 to 48
- kernel_weight: float32 [4, 2], replicated, may hold values from 0.25 to 1
- dose_table: float32 [4], replicated, may hold values from 0.7 to 1.4
- condition_index: int32 [2], replicated, may hold values from 0 to 3, as said below
Outputs:
- resist: float32 [2, 512, 4096], P(None, 'win', 'tile'), parts along dimension 1
- gradient: float32 [512, 4096], P('win', 'tile'), parts along dimension 0
There are 2 independent parts, one for each index of `win`. A program takes and returns all parts, laid end to end along the dimension named above; an argument that names none is the same for every part. Nothing has to cross between parts.
Inputs may be any that keep to these rules, and one draw needn't show every extreme that they name: `condition_index`: the 2 entries are distinct table indices.
All inputs are finite; a program needn't handle non-finite values.
Results may differ from a plain program's by a relative error of at most 0.00015.
Values sent between devices are 32-bit elements; how exact they have to be, the bound alone decides.
No kernel may reach another device: no remote copies, remote signals or barrier semaphores. Data moves between devices by JAX's collectives and lax.ppermute only.
A program may use at most 64 MiB of HBM per device.

v0:
```python
import math

import jax
import jax.numpy as jnp
from jax import lax
from jax.sharding import PartitionSpec as P

NPAD = 512
MARGIN = 128
BAND = 64
CONDS = 2
TABLE = 4
CORE = 256


highest = lax.Precision.HIGHEST
steepness = 6.0
threshold = 0.3


def extended_2(x, sides, width):
    for axis, dim in sides:
        size, length = (lax.axis_size(axis), x.shape[dim])
        up = [(i, (i + 1) % size) for i in range(size - 1)]
        down = [(j, i) for i, j in up]
        last = lax.slice_in_dim(x, length - width, length, axis=dim)
        first = lax.slice_in_dim(x, 0, width, axis=dim)
        before = lax.ppermute(last, axis, up)
        after = lax.ppermute(first, axis, down)
        x = jnp.concatenate([before, x, after], axis=dim)
    return x


def from_behind(x, axis, by):
    length = lax.axis_size(axis)
    pairs = [(i, i + by) for i in range(length) if 0 <= i + by < length]
    return lax.ppermute(x, axis, pairs)


def product(left, right):
    return jnp.matmul(left, right, precision=highest)


def band_tables():
    frequency = jnp.arange(BAND, dtype=jnp.int32) - BAND // 2
    position = jnp.arange(NPAD, dtype=jnp.int32)
    phase = (frequency[:, None] * position[None, :] % NPAD).astype(jnp.float32) * (
        2.0 * math.pi / NPAD
    )
    return (jnp.cos(phase), -jnp.sin(phase))


def select_conditions(kernel_table, kernel_weight, dose_table, condition_index):
    selector = (condition_index[:, None] == jnp.arange(TABLE, dtype=jnp.int32)[None, :]).astype(
        jnp.float32
    )
    kernels = jnp.einsum("ct,tkrab->ckrab", selector, kernel_table, precision=highest)
    return (kernels, product(selector, kernel_weight), product(selector, dose_table))


def column_pass(frames, cosine, sine):
    return (product(frames, cosine.T), product(frames, sine.T))


def row_pass(real, imaginary, cosine, sine):
    first = product(cosine, real) - product(sine, imaginary)
    second = product(cosine, imaginary) + product(sine, real)
    return (first / NPAD, second / NPAD)


def analyze_complex(real, imaginary, cosine, sine):
    first = product(real, cosine.T) - product(imaginary, sine.T)
    second = product(real, sine.T) + product(imaginary, cosine.T)
    return row_pass(first, second, cosine, sine)


def synthesize(real, imaginary, cosine, sine):
    first = product(real, cosine) + product(imaginary, sine)
    second = product(imaginary, cosine) - product(real, sine)
    out_real = (product(cosine.T, first) + product(sine.T, second)) / NPAD
    out_imaginary = (product(cosine.T, second) - product(sine.T, first)) / NPAD
    return (out_real, out_imaginary)


def synthesize_real(real, imaginary, cosine, sine, column_cosine, column_sine):
    first = product(real, column_cosine) + product(imaginary, column_sine)
    second = product(imaginary, column_cosine) - product(real, column_sine)
    return (product(cosine.T, first) + product(sine.T, second)) / NPAD


def stack_frames(extended):
    return jnp.stack([extended])


def fold_rows(frames, tiles):
    folded = jnp.zeros((tiles * CORE + 2 * MARGIN, frames.shape[2]), jnp.float32)
    folded = folded.at[0:NPAD].add(frames[0])
    return folded[MARGIN : MARGIN + tiles * CORE]


def local(mask, target, kernel_table, kernel_weight, dose_table, condition_index):
    cosine, sine = band_tables()
    core_cosine = cosine[:, MARGIN : MARGIN + CORE]
    core_sine = sine[:, MARGIN : MARGIN + CORE]
    kernels, weights, doses = select_conditions(
        kernel_table, kernel_weight, dose_table, condition_index
    )
    tiles = mask.shape[0] // CORE
    widened = extended_2(mask, (("tile", 1),), MARGIN)
    frames = stack_frames(jnp.pad(widened, ((MARGIN, MARGIN), (0, 0))))
    spec_real, spec_imaginary = row_pass(*column_pass(frames, cosine, sine), cosine, sine)
    goals = target.reshape(tiles, CORE, CORE)
    grad_real = jnp.zeros_like(spec_real)
    grad_imaginary = jnp.zeros_like(spec_imaginary)
    printed = []
    for condition in range(CONDS):
        kernel_real = kernels[condition, :, 0]
        kernel_imaginary = kernels[condition, :, 1]
        mixed_real = kernel_real * spec_real[:, None] - kernel_imaginary * spec_imaginary[:, None]
        mixed_imaginary = (
            kernel_real * spec_imaginary[:, None] + kernel_imaginary * spec_real[:, None]
        )
        field_real, field_imaginary = synthesize(
            mixed_real, mixed_imaginary, core_cosine, core_sine
        )
        power = field_real * field_real + field_imaginary * field_imaginary
        intensity = jnp.einsum("k,tkmn->tmn", weights[condition], power, precision=highest)
        inner = jax.nn.sigmoid(steepness * (doses[condition] * intensity - threshold))
        printed.append(inner.reshape(tiles * CORE, CORE))
        misfit = 4.0 * (inner - goals)
        drive = misfit * (steepness * doses[condition]) * inner * (1.0 - inner)
        scaled = 2.0 * weights[condition][None, :, None, None] * drive[:, None]
        back_real, back_imaginary = analyze_complex(
            scaled * field_real, scaled * field_imaginary, core_cosine, core_sine
        )
        grad_real = grad_real + jnp.sum(
            kernel_real * back_real + kernel_imaginary * back_imaginary, axis=1
        )
        grad_imaginary = grad_imaginary + jnp.sum(
            kernel_real * back_imaginary - kernel_imaginary * back_real, axis=1
        )
    resist = jnp.stack(printed)
    whole = fold_rows(synthesize_real(grad_real, grad_imaginary, cosine, sine, cosine, sine), tiles)
    own = whole[:, MARGIN : MARGIN + CORE]
    from_left = from_behind(whole[:, MARGIN + CORE :], "tile", 1)
    from_right = from_behind(whole[:, :MARGIN], "tile", -1)
    gradient = own.at[:, :MARGIN].add(from_left).at[:, CORE - MARGIN :].add(from_right)
    return (resist, gradient)


def solution(mesh):
    return jax.shard_map(
        local,
        mesh=mesh,
        in_specs=(P("win", "tile"), P("win", "tile"), P(), P(), P(), P()),
        out_specs=(P(None, "win", "tile"), P("win", "tile")),
        check_vma=False,
    )
```

profile of v0, /device:TPU:21, one launch (start us, length us, event | category | flops | bytes accessed | tf_op | source)
XLA Modules:
  0.0 59.7 jit_solution(17255362934043514294)
XLA Ops:
  0.6 1.0 %fusion.184 = (f32[256,128]{1,0:T(8,128)S(1)}, f32[256,128]{1,0:T(8,128)S(1)}) fusion(f32[256,256]{1,0:T(8,128)} %param.14), kind=kLoop, calls=%fused_computation.228 | loop fusion | bytes 524288 | tf_op jit(solution)/shard_map/slice | solution.py:26
  1.7 3.7 %collective-permute-start = (f32[256,128]{1,0:T(8,128)S(1)}, f32[256,128]{1,0:T(8,128)S(1)}, u32[]{:S(2)}, u32[]{:S(2)}) collective-permute-start(f32[256,128]{1,0:T(8,128)S(1)} %get-tuple-element.60), channel_id=1, source_target_pairs={{0,1},{1,2},{2,3},{3,4},{4,5},{5,6},{6,7},{7,8},{8,9},{9,10},{10,1... | collective-permute-start | bytes 393224 | tf_op jit(solution)/shard_map/ppermute | solution.py:28
  5.4 1.9 %collective-permute-start.1 = (f32[256,128]{1,0:T(8,128)S(1)}, f32[256,128]{1,0:T(8,128)S(1)}, u32[]{:S(2)}, u32[]{:S(2)}) collective-permute-start(f32[256,128]{1,0:T(8,128)S(1)} %get-tuple-element.61), channel_id=1, source_target_pairs={{1,0},{2,1},{3,2},{4,3},{5,4},{6,5},{7,6},{8,7},{9,8},{10,9},{11,1... | collective-permute-start | bytes 393224 | tf_op jit(solution)/shard_map/ppermute | solution.py:29
  7.4 0.6 sine_negate_fusion
  8.0 0.9 %fusion.32 = f32[2,2,2,64,64]{4,0,3,2,1:T(2,128)S(1)} fusion(f32[4,2,2,64,64]{4,3,2,1,0:T(8,128)S(1)} %copy-done, s32[2]{0:T(128)S(1)} %copy-done.4), kind=kOutput, calls=%fused_computation.63 | convolution fusion | flops 1572872 | bytes 393224 | tf_op jit(solution)/shard_map/ct,tkrab->ckrab/dot_general | solution.py:57
  8.9 0.2 fusion.183
  9.1 0.5 copy-done.5
  9.8 0.5 copy-done.6
  10.4 0.6 fusion.185
  12.4 0.2 collective-permute-done.1
  12.6 1.3 %fusion.20 = f32[512,64]{0,1:T(8,128)S(1)} fusion(f32[256,128]{1,0:T(8,128)S(1)} %collective-permute-done.1, f32[256,256]{1,0:T(8,128)S(1)} %copy-done.2, f32[256,128]{1,0:T(8,128)S(1)} %collective-permute-done, s32[64]{0:T(128)S(1)} %iota_add_fusion), kind=kOutput, calls=%fused_computation.50 | convolution fusion | flops 203882496 | bytes 655616 | tf_op jit(solution)/shard_map/dot_general | solution.py:41
  13.9 0.8 %fusion.95 = f32[64,64]{1,0:T(8,128)S(1)} fusion(f32[512,64]{0,1:T(8,128)S(1)} %fusion.20, s32[64]{0:T(128)S(1)} %iota_add_fusion), kind=kOutput, calls=%fused_computation.136 | convolution fusion | flops 25624576 | bytes 147712 | tf_op jit(solution)/shard_map/dot_general | solution.py:41
  14.7 1.3 %fusion.21 = f32[512,64]{0,1:T(8,128)S(1)} fusion(f32[256,128]{1,0:T(8,128)S(1)} %collective-permute-done.1, f32[256,256]{1,0:T(8,128)S(1)} %copy-done.2, f32[256,128]{1,0:T(8,128)S(1)} %collective-permute-done, s32[64]{0:T(128)S(1)} %iota_add_fusion), kind=kOutput, calls=%fused_computation.51 | convolution fusion | flops 203915264 | bytes 655616 | tf_op jit(solution)/shard_map/dot_general | solution.py:41
  16.1 0.8 %fusion.93 = f32[64,64]{1,0:T(8,128)S(1)} fusion(f32[512,64]{0,1:T(8,128)S(1)} %fusion.21, s32[64]{0:T(128)S(1)} %iota_add_fusion), kind=kOutput, calls=%fused_computation.135 | convolution fusion | flops 25624576 | bytes 147712 | tf_op jit(solution)/shard_map/dot_general | solution.py:41
  16.9 0.8 %fusion.18 = f32[64,64]{1,0:T(8,128)S(1)} fusion(f32[64,64]{1,0:T(8,128)S(1)} %fusion.95, f32[512,64]{0,1:T(8,128)S(1)} %fusion.21, s32[64]{0:T(128)S(1)} %iota_add_fusion), kind=kOutput, calls=%fused_computation.41 | convolution fusion | flops 25665536 | bytes 164096 | tf_op jit(solution)/shard_map/dot_general | solution.py:41
  17.7 0.8 %fusion.17 = f32[64,64]{1,0:T(8,128)S(1)} fusion(f32[64,64]{1,0:T(8,128)S(1)} %fusion.93, f32[512,64]{0,1:T(8,128)S(1)} %fusion.20, s32[64]{0:T(128)S(1)} %iota_add_fusion), kind=kOutput, calls=%fused_computation.39 | convolution fusion | flops 25665536 | bytes 164096 | tf_op jit(solution)/shard_map/dot_general | solution.py:41
  18.5 0.3 fusion.170
  18.8 0.3 fusion.171
  19.1 0.3 fusion.172
  19.3 0.3 fusion.173
  19.6 0.3 convolution_add_fusion.7
  19.8 0.6 %fusion.181 = f32[256,2,256]{2,0,1:T(8,128)S(1)} fusion(f32[2,64,256]{2,1,0:T(8,128)S(1)} %convolution_add_fusion.7, f32[64,512]{1,0:T(8,128)S(1)} %get-tuple-element.67), kind=kOutput, calls=%fused_computation.225 | convolution fusion | flops 100663296 | bytes 720896 | tf_op jit(solution)/shard_map/dot_general | solution.py:41
  20.5 0.3 convolution_subtract_fusion.6
  20.7 0.6 %fusion.180 = f32[256,2,256]{2,0,1:T(8,128)S(1)} fusion(f32[2,64,256]{2,1,0:T(8,128)S(1)} %convolution_subtract_fusion.6, f32[64,512]{1,0:T(8,128)S(1)} %get-tuple-element.67), kind=kOutput, calls=%fused_computation.224 | convolution fusion | flops 100663296 | bytes 720896 | tf_op jit(solution)/shard_map/dot_general | solution.py:41
  21.4 0.6 %fusion.2 = f32[1,2,256,256]{3,2,1,0:T(8,128)S(1)} fusion(f32[256,2,256]{2,0,1:T(8,128)S(1)} %fusion.181, f32[2,64,256]{2,1,0:T(8,128)S(1)} %convolution_subtract_fusion.6, f32[64,512]{1,0:T(8,128)S(1)} %get-tuple-element.66), kind=kOutput, calls=%fused_computation.9 | convolution fusion | flops 100925440 | bytes 1245184 | tf_op jit(solution)/shard_map/dot_general | solution.py:41
  22.0 0.6 %fusion.4 = f32[1,2,256,256]{3,2,1,0:T(8,128)S(1)} fusion(f32[256,2,256]{2,0,1:T(8,128)S(1)} %fusion.180, f32[2,64,256]{2,1,0:T(8,128)S(1)} %convolution_add_fusion.7, f32[64,512]{1,0:T(8,128)S(1)} %get-tuple-element.66), kind=kOutput, calls=%fused_computation.11 | convolution fusion | flops 100925440 | bytes 1245184 | tf_op jit(solution)/shard_map/dot_general | solution.py:41
  22.7 2.0 %fusion.36 = f32[1,256,256]{2,0,1:T(1,128)S(1)} fusion(f32[2,256,256]{2,1,0:T(8,128)S(1)} %add_bitcast_fusion.1, f32[2,2]{1,0:T(2,128)S(1)} %fusion.103), kind=kOutput, calls=%fused_computation.69 | convolution fusion | flops 1572864 | bytes 786944 | tf_op jit(solution)/shard_map/k,tkmn->tmn/dot_general | solution.py:127
  24.8 0.4 convolution_add_fusion.6
  25.2 0.6 %fusion.179 = f32[256,2,256]{2,0,1:T(8,128)S(1)} fusion(f32[2,64,256]{2,1,0:T(8,128)S(1)} %convolution_add_fusion.6, f32[64,512]{1,0:T(8,128)S(1)} %get-tuple-element.67), kind=kOutput, calls=%fused_computation.223 | convolution fusion | flops 100663296 | bytes 720896 | tf_op jit(solution)/shard_map/dot_general | solution.py:41
  25.8 0.3 convolution_subtract_fusion.5
  26.1 0.6 %fusion.178 = f32[256,2,256]{2,0,1:T(8,128)S(1)} fusion(f32[2,64,256]{2,1,0:T(8,128)S(1)} %convolution_subtract_fusion.5, f32[64,512]{1,0:T(8,128)S(1)} %get-tuple-element.67), kind=kOutput, calls=%fused_computation.222 | convolution fusion | flops 100663296 | bytes 720896 | tf_op jit(solution)/shard_map/dot_general | solution.py:41
  26.7 0.6 %fusion.6 = f32[1,2,256,256]{3,2,1,0:T(8,128)S(1)} fusion(f32[256,2,256]{2,0,1:T(8,128)S(1)} %fusion.179, f32[2,64,256]{2,1,0:T(8,128)S(1)} %convolution_subtract_fusion.5, f32[64,512]{1,0:T(8,128)S(1)} %get-tuple-element.66), kind=kOutput, calls=%fused_computation.13 | convolution fusion | flops 100925440 | bytes 1245184 | tf_op jit(solution)/shard_map/dot_general | solution.py:41
  27.4 0.6 %fusion.8 = f32[1,2,256,256]{3,2,1,0:T(8,128)S(1)} fusion(f32[256,2,256]{2,0,1:T(8,128)S(1)} %fusion.178, f32[2,64,256]{2,1,0:T(8,128)S(1)} %convolution_add_fusion.6, f32[64,512]{1,0:T(8,128)S(1)} %get-tuple-element.66), kind=kOutput, calls=%fused_computation.15 | convolution fusion | flops 100925440 | bytes 1245184 | tf_op jit(solution)/shard_map/dot_general | solution.py:41
  28.1 2.0 %fusion.34 = f32[1,256,256]{2,0,1:T(1,128)S(1)} fusion(f32[2,256,256]{2,1,0:T(8,128)S(1)} %add_bitcast_fusion, f32[2,2]{1,0:T(2,128)S(1)} %fusion.103), kind=kOutput, calls=%fused_computation.67 | convolution fusion | flops 1572864 | bytes 786944 | tf_op jit(solution)/shard_map/k,tkmn->tmn/dot_general | solution.py:127
  30.1 1.5 %subtract_multiply_fusion = (f32[256,256]{1,0:T(8,128)S(1)}, f32[1,256,256]{2,1,0:T(8,128)S(1)}, f32[256,256]{1,0:T(8,128)S(1)}, f32[1,256,256]{2,1,0:T(8,128)S(1)}) fusion(f32[256,256]{1,0:T(8,128)S(1)} %copy-done.3, f32[]{:T(128)S(6)} %mul.653, f32[1,256,256]{2,0,1:T(1,128)S(1)} %fusion.34, f32[]{:T(128)} %bitcast.18, f32[]{:T(128)S(6)} %mul.640, ...), kind=kLoop, calls=%fused_computation.93 | loop fusion | flops 1441792 | bytes 1835024 | tf_op jit(solution)/shard_map/mul | solution.py:131
  31.7 0.7 %fusion.42 = f32[2,256,64]{1,2,0:T(8,128)S(1)} fusion(f32[1,2,256,256]{3,2,1,0:T(8,128)S(1)} %fusion.6, f32[256,256]{1,0:T(8,128)S(1)} %get-tuple-element.52, f32[2]{0:T(128)S(1)} %get-tuple-element.62, f32[64,512]{1,0:T(8,128)S(1)} %get-tuple-element.67), kind=kOutput, calls=%fused_computation.72 | convolution fusion | flops 100925440 | bytes 983552 | tf_op jit(solution)/shard_map/dot_general | solution.py:41
  32.4 0.7 %fusion.40 = f32[2,256,64]{1,2,0:T(8,128)S(1)} fusion(f32[1,2,256,256]{3,2,1,0:T(8,128)S(1)} %fusion.6, f32[256,256]{1,0:T(8,128)S(1)} %get-tuple-element.52, f32[2]{0:T(128)S(1)} %get-tuple-element.62, f32[64,512]{1,0:T(8,128)S(1)} %get-tuple-element.66), kind=kOutput, calls=%fused_computation.71 | convolution fusion | flops 100925440 | bytes 983552 | tf_op jit(solution)/shard_map/dot_general | solution.py:41
  33.1 0.7 %fusion.48 = f32[2,256,64]{1,2,0:T(8,128)S(1)} fusion(f32[1,2,256,256]{3,2,1,0:T(8,128)S(1)} %fusion.2, f32[256,256]{1,0:T(8,128)S(1)} %get-tuple-element.54, f32[2]{0:T(128)S(1)} %get-tuple-element.63, f32[64,512]{1,0:T(8,128)S(1)} %get-tuple-element.67), kind=kOutput, calls=%fused_computation.74 | convolution fusion | flops 100925440 | bytes 983552 | tf_op jit(solution)/shard_map/dot_general | solution.py:41
  33.9 0.7 %fusion.46 = f32[2,256,64]{1,2,0:T(8,128)S(1)} fusion(f32[1,2,256,256]{3,2,1,0:T(8,128)S(1)} %fusion.2, f32[256,256]{1,0:T(8,128)S(1)} %get-tuple-element.54, f32[2]{0:T(128)S(1)} %get-tuple-element.63, f32[64,512]{1,0:T(8,128)S(1)} %get-tuple-element.66), kind=kOutput, calls=%fused_computation.73 | convolution fusion | flops 100925440 | bytes 983552 | tf_op jit(solution)/shard_map/dot_general | solution.py:41
  34.6 0.7 %convolution_subtract_fusion.2 = f32[2,256,64]{1,2,0:T(8,128)S(1)} fusion(f32[2,256,64]{1,2,0:T(8,128)S(1)} %fusion.42, f32[1,2,256,256]{3,2,1,0:T(8,128)S(1)} %fusion.8, f32[256,256]{1,0:T(8,128)S(1)} %get-tuple-element.52, f32[2]{0:T(128)S(1)} %get-tuple-element.62, f32[64,512]{1,0:T(8,128)S(1)} %get-tuple-element.66), kind=kOutput, calls=%fused_computation.17 | convolution fusion | flops 100958208 | bytes 1114624 | tf_op jit(solution)/shard_map/dot_general | solution.py:41
  35.4 0.3 fusion.175
  35.7 0.7 %convolution_add_fusion.3 = f32[2,256,64]{1,2,0:T(8,128)S(1)} fusion(f32[2,256,64]{1,2,0:T(8,128)S(1)} %fusion.40, f32[1,2,256,256]{3,2,1,0:T(8,128)S(1)} %fusion.8, f32[256,256]{1,0:T(8,128)S(1)} %get-tuple-element.52, f32[2]{0:T(128)S(1)} %get-tuple-element.62, f32[64,512]{1,0:T(8,128)S(1)} %get-tuple-element.67), kind=kOutput, calls=%fused_computation.16 | convolution fusion | flops 100958208 | bytes 1114624 | tf_op jit(solution)/shard_map/dot_general | solution.py:41
  36.4 0.3 fusion.174
  36.8 0.3 fusion.10
  37.1 0.7 %convolution_subtract_fusion.3 = f32[2,256,64]{1,2,0:T(8,128)S(1)} fusion(f32[2,256,64]{1,2,0:T(8,128)S(1)} %fusion.48, f32[1,2,256,256]{3,2,1,0:T(8,128)S(1)} %fusion.4, f32[256,256]{1,0:T(8,128)S(1)} %get-tuple-element.54, f32[2]{0:T(128)S(1)} %get-tuple-element.63, f32[64,512]{1,0:T(8,128)S(1)} %get-tuple-element.66), kind=kOutput, calls=%fused_computation.19 | convolution fusion | flops 100958208 | bytes 1114624 | tf_op jit(solution)/shard_map/dot_general | solution.py:41
  37.8 0.3 fusion.177
  38.1 0.7 %convolution_add_fusion.4 = f32[2,256,64]{1,2,0:T(8,128)S(1)} fusion(f32[2,256,64]{1,2,0:T(8,128)S(1)} %fusion.46, f32[1,2,256,256]{3,2,1,0:T(8,128)S(1)} %fusion.4, f32[256,256]{1,0:T(8,128)S(1)} %get-tuple-element.54, f32[2]{0:T(128)S(1)} %get-tuple-element.63, f32[64,512]{1,0:T(8,128)S(1)} %get-tuple-element.67), kind=kOutput, calls=%fused_computation.18 | convolution fusion | flops 100958208 | bytes 1114624 | tf_op jit(solution)/shard_map/dot_general | solution.py:41
  38.9 0.3 fusion.176
  39.2 0.3 fusion.14
  39.5 0.3 subtract_reduce_fusion
  39.9 0.3 subtract_reduce_fusion.1
  40.2 0.8 %fusion.87 = f32[64,512]{1,0:T(8,128)S(1)} fusion(s32[64]{0:T(128)S(1)} %iota_add_fusion, f32[64,64]{1,0:T(8,128)S(1)} %get-tuple-element.48, f32[64,64]{1,0:T(8,128)S(1)} %get-tuple-element.46), kind=kOutput, calls=%fused_computation.132 | convolution fusion | flops 25628672 | bytes 164096 | tf_op jit(solution)/shard_map/dot_general | solution.py:41
  41.0 0.8 %fusion.91 = f32[64,512]{1,0:T(8,128)S(1)} fusion(s32[64]{0:T(128)S(1)} %iota_add_fusion, f32[64,64]{1,0:T(8,128)S(1)} %get-tuple-element.49, f32[64,64]{1,0:T(8,128)S(1)} %get-tuple-element.47), kind=kOutput, calls=%fused_computation.134 | convolution fusion | flops 25628672 | bytes 164096 | tf_op jit(solution)/shard_map/dot_general | solution.py:41
  41.8 1.0 %convolution_subtract_fusion.4 = f32[64,512]{1,0:T(8,128)S(1)} fusion(f32[64,512]{1,0:T(8,128)S(1)} %fusion.87, s32[64]{0:T(128)S(1)} %iota_add_fusion, f32[64,64]{1,0:T(8,128)S(1)} %get-tuple-element.49, f32[64,64]{1,0:T(8,128)S(1)} %get-tuple-element.47), kind=kOutput, calls=%fused_computation.20 | convolution fusion | flops 25694208 | bytes 295168 | tf_op jit(solution)/shard_map/dot_general | solution.py:41
  42.9 0.8 %convolution_add_fusion.5 = f32[64,512]{1,0:T(8,128)S(1)} fusion(f32[64,512]{1,0:T(8,128)S(1)} %fusion.91, s32[64]{0:T(128)S(1)} %iota_add_fusion, f32[64,64]{1,0:T(8,128)S(1)} %get-tuple-element.48, f32[64,64]{1,0:T(8,128)S(1)} %get-tuple-element.46), kind=kOutput, calls=%fused_computation.21 | convolution fusion | flops 25694208 | bytes 295168 | tf_op jit(solution)/shard_map/dot_general | solution.py:41
  43.7 1.5 %fusion.89 = f32[512,512]{1,0:T(8,128)S(1)} fusion(f32[64,512]{1,0:T(8,128)S(1)} %convolution_add_fusion.5, s32[64]{0:T(128)S(1)} %iota_add_fusion), kind=kOutput, calls=%fused_computation.133 | convolution fusion | flops 201785344 | bytes 1179904 | tf_op jit(solution)/shard_map/dot_general | solution.py:41
  45.2 1.5 %fusion = f32[512,512]{1,0:T(8,128)S(1)} fusion(f32[512,512]{1,0:T(8,128)S(1)} %fusion.89, f32[64,512]{1,0:T(8,128)S(1)} %convolution_subtract_fusion.4, s32[64]{0:T(128)S(1)} %iota_add_fusion), kind=kOutput, calls=%fused_computation.3 | convolution fusion | flops 202342400 | bytes 2228480 | tf_op jit(solution)/shard_map/dot_general | solution.py:41
  46.8 4.3 %collective-permute-start.2 = (f32[256,128]{1,0:T(8,128)S(1)}, f32[256,128]{1,0:T(8,128)S(1)}, u32[]{:S(2)}, u32[]{:S(2)}) collective-permute-start(f32[256,128]{1,0:T(8,128)S(1)} %get-tuple-element.51), channel_id=1, source_target_pairs={{0,1},{1,2},{2,3},{3,4},{4,5},{5,6},{6,7},{7,8},{8,9},{9,10},{10,1... | collective-permute-start | bytes 393224 | tf_op jit(solution)/shard_map/ppermute | solution.py:37
  51.1 0.6 %compare_reduce_fusion = pred[]{:T(512)} fusion(), kind=kLoop, calls=%fused_computation.142 | loop fusion | flops 5 | bytes 1 | tf_op jit(solution)/shard_map/reduce.4
  51.8 1.9 %collective-permute-start.3 = (f32[256,128]{1,0:T(8,128)S(1)}, f32[256,128]{1,0:T(8,128)S(1)}, u32[]{:S(2)}, u32[]{:S(2)}) collective-permute-start(f32[256,128]{1,0:T(8,128)S(1)} %get-tuple-element.50), channel_id=1, source_target_pairs={{1,0},{2,1},{3,2},{4,3},{5,4},{6,5},{7,6},{8,7},{9,8},{10,9},{11,1... | collective-permute-start | bytes 393224 | tf_op jit(solution)/shard_map/ppermute | solution.py:37
  53.7 0.8 %pad_maximum_fusion = f32[2,256,256]{2,1,0:T(8,128)} fusion(f32[1,256,256]{2,1,0:T(8,128)S(1)} %get-tuple-element.53, f32[1,256,256]{2,1,0:T(8,128)S(1)} %get-tuple-element.55), kind=kLoop, calls=%fused_computation.62 | loop fusion | flops 131072 | bytes 1048576 | tf_op jit(solution)/shard_map/stack | solution.py:142
  54.6 0.7 %fusion.81 = f32[256,256]{1,0:T(8,128)S(1)} fusion(f32[256,256]{1,0:T(8,128)S(1)} %slice.189, f32[256,128]{1,0:T(8,128)S(1)} %collective-permute-done.2, f32[512,512]{1,0:T(8,128)S(1)} %fusion, pred[]{:T(512)} %compare_reduce_fusion), kind=kLoop, calls=%fused_computation.114 | loop fusion | flops 65536 | bytes 393217 | tf_op jit(solution)/shard_map/scatter-add | solution.py:147
  55.2 3.7 %collective-permute-done.3 = f32[256,128]{1,0:T(8,128)S(1)} collective-permute-done((f32[256,128]{1,0:T(8,128)S(1)}, f32[256,128]{1,0:T(8,128)S(1)}, u32[]{:S(2)}, u32[]{:S(2)}) %collective-permute-start.3) | collective-permute-done | bytes 131104 | tf_op jit(solution)/shard_map/ppermute | solution.py:37
  59.0 0.7 %copy-done.1 = f32[256,256]{1,0:T(8,128)} copy-done((f32[256,256]{1,0:T(8,128)}, f32[256,256]{1,0:T(8,128)S(1)}, u32[]{:S(2)}) %copy-start.1) | copy-done | bytes 262168
  (22 shorter events, 0.7 us)
Async XLA Ops:
  0.6 7.3 %copy-start = (f32[4,2,2,64,64]{4,3,2,1,0:T(8,128)S(1)}, f32[4,2,2,64,64]{4,3,2,1,0:T(8,128)}, u32[]{:S(2)}) copy-start(f32[4,2,2,64,64]{4,3,2,1,0:T(8,128)} %param.16) | copy-start | bytes 786436
  1.7 10.7 %collective-permute-start = (f32[256,128]{1,0:T(8,128)S(1)}, f32[256,128]{1,0:T(8,128)S(1)}, u32[]{:S(2)}, u32[]{:S(2)}) collective-permute-start(f32[256,128]{1,0:T(8,128)S(1)} %get-tuple-element.60), channel_id=1, source_target_pairs={{0,1},{1,2},{2,3},{3,4},{4,5},{5,6},{6,7},{7,8},{8,9},{9,10},{10,1... | collective-permute-start | bytes 393224 | tf_op jit(solution)/shard_map/ppermute | solution.py:28
  5.4 7.2 %collective-permute-start.1 = (f32[256,128]{1,0:T(8,128)S(1)}, f32[256,128]{1,0:T(8,128)S(1)}, u32[]{:S(2)}, u32[]{:S(2)}) collective-permute-start(f32[256,128]{1,0:T(8,128)S(1)} %get-tuple-element.61), channel_id=1, source_target_pairs={{1,0},{2,1},{3,2},{4,3},{5,4},{6,5},{7,6},{8,7},{9,8},{10,9},{11,1... | collective-permute-start | bytes 393224 | tf_op jit(solution)/shard_map/ppermute | solution.py:29
  7.3 0.7 %copy-start.4 = (s32[2]{0:T(128)S(1)}, s32[2]{0:T(128)}, u32[]{:S(2)}) copy-start(s32[2]{0:T(128)} %param.19) | copy-start | bytes 28
  8.9 0.7 %copy-start.5 = (f32[4,2]{0,1:T(2,128)S(1)}, f32[4,2]{0,1:T(2,128)}, u32[]{:S(2)}) copy-start(f32[4,2]{0,1:T(2,128)} %param.17) | copy-start | bytes 100
  8.9 3.7 %copy-start.2 = (f32[256,256]{1,0:T(8,128)S(1)}, f32[256,256]{1,0:T(8,128)}, u32[]{:S(2)}) copy-start(f32[256,256]{1,0:T(8,128)} %param.14) | copy-start | bytes 786436
  9.6 0.7 %copy-start.6 = (f32[4]{0:T(128)S(1)}, f32[4]{0:T(128)}, u32[]{:S(2)}) copy-start(f32[4]{0:T(128)} %param.18) | copy-start | bytes 52
  28.1 2.1 %copy-start.3 = (f32[256,256]{1,0:T(8,128)S(1)}, f32[256,256]{1,0:T(8,128)}, u32[]{:S(2)}) copy-start(f32[256,256]{1,0:T(8,128)} %param.15) | copy-start | bytes 786436
  46.8 7.8 %collective-permute-start.2 = (f32[256,128]{1,0:T(8,128)S(1)}, f32[256,128]{1,0:T(8,128)S(1)}, u32[]{:S(2)}, u32[]{:S(2)}) collective-permute-start(f32[256,128]{1,0:T(8,128)S(1)} %get-tuple-element.51), channel_id=1, source_target_pairs={{0,1},{1,2},{2,3},{3,4},{4,5},{5,6},{6,7},{7,8},{8,9},{9,10},{10,1... | collective-permute-start | bytes 393224 | tf_op jit(solution)/shard_map/ppermute | solution.py:37
  51.8 7.2 %collective-permute-start.3 = (f32[256,128]{1,0:T(8,128)S(1)}, f32[256,128]{1,0:T(8,128)S(1)}, u32[]{:S(2)}, u32[]{:S(2)}) collective-permute-start(f32[256,128]{1,0:T(8,128)S(1)} %get-tuple-element.50), channel_id=1, source_target_pairs={{1,0},{2,1},{3,2},{4,3},{5,4},{6,5},{7,6},{8,7},{9,8},{10,9},{11,1... | collective-permute-start | bytes 393224 | tf_op jit(solution)/shard_map/ppermute | solution.py:37
  59.0 0.7 %copy-start.1 = (f32[256,256]{1,0:T(8,128)}, f32[256,256]{1,0:T(8,128)S(1)}, u32[]{:S(2)}) copy-start(f32[256,256]{1,0:T(8,128)S(1)} %fusion.82) | copy-start | bytes 786436
where the time goes:
time: 60 us; the launch traced here: 59.7 us
  matrix products  33.5 us (56%)
  starting transfers between devices  11.9 us (20%)
  other arithmetic  4.42 us (7%)
  waiting for transfers between devices  3.99 us (7%)
  local copies, waits for them, and re-layouts  3.56 us (6%)
  between operations  2.36 us (4%)
    dot_general x46, matrix products, product(): return jnp.matmul(left, right, precision=highest)  28.6 us
    ppermute x2, starting transfers between devices, from_behind(): return lax.ppermute(x, axis, pairs)  6.24 us
    dot_general x2, matrix products, local(): jnp.einsum('k,tkmn->tmn', weights[condition], power, precision=highest)  4.06 us
    ppermute x2, waiting for transfers between devices, from_behind(): return lax.ppermute(x, axis, pairs)  3.75 us
    ppermute x1, starting transfers between devices, extended_2(): before = lax.ppermute(last, axis, up)  3.71 us
    ppermute x1, starting transfers between devices, extended_2(): after = lax.ppermute(first, axis, down)  1.92 us
    unnamed x14, local copies, waits for them, and re-layouts  1.69 us
    mul x1, other arithmetic, local(): drive = misfit * (steepness * doses[condition]) * inner * (1.0 - inner)  1.51 us
  transfers between devices with their start and end apart: 4, of which 2 were waited for; matrix products, arithmetic and copies ran while one was open for 8% of the time, Pallas kernels for 0%

commit v1 on v0

v1 whole, which is shorter than its diff:
```python
import math

import jax
import jax.numpy as jnp
import ml_dtypes
import numpy as np
from jax import lax
from jax.experimental import pallas as pl
from jax.experimental.pallas import tpu as pltpu
from jax.sharding import PartitionSpec as P

NPAD = 512
MARGIN = 128
BAND = 64
KERN = 2
CONDS = 2
CORE = 256
PAIRS = CONDS * KERN
WIDE = 2 * BAND

steepness = 6.0
threshold = 0.3


def parts(table):
    high = table.astype(ml_dtypes.bfloat16)
    low = (table - high.astype(np.float64)).astype(ml_dtypes.bfloat16)
    return high, low


def tables():
    frequency = np.arange(BAND)[:, None] - BAND // 2
    position = np.arange(MARGIN, MARGIN + CORE)[None, :]
    phase = (frequency * position % NPAD) * (2.0 * math.pi / NPAD)
    cosine, sine = np.cos(phase), -np.sin(phase)
    rows = np.concatenate([cosine, sine], 0)
    half = CORE // 2
    split = np.zeros((CORE, CORE))
    split[:half, :WIDE] = rows[:, :half].T
    split[half:, WIDE:] = rows[:, half:].T
    out = np.block([[cosine, -sine], [sine, cosine]])
    back = np.block([[cosine.T, sine.T], [-sine.T, cosine.T]])
    return rows, split, out, back


def side_by_side(pair, axis):
    return np.concatenate(pair, axis)


def halves(x):
    high = x.astype(jnp.bfloat16)
    return high, (x - high.astype(jnp.float32)).astype(jnp.bfloat16)


def dot(a, b):
    return jnp.dot(a, b, preferred_element_type=jnp.float32)


def turn(x):
    lane = lax.broadcasted_iota(jnp.int32, x.shape, 1)
    rolled = pltpu.roll(x, BAND, 1)
    return jnp.where(lane < BAND, -rolled, rolled)


def signs(shape):
    lane = lax.broadcasted_iota(jnp.int32, shape, 1)
    return jnp.where(lane % 2 == 0, 1.0, -1.0).astype(jnp.float32)


def stacked(x):
    return jnp.concatenate([x, -turn(x)], 0)


def analyze_kernel(mask, rows, split_high, split_low, own, even_out, odd_out):
    odd = lax.axis_index("tile") % 2 == 1
    high, low = halves(mask[...])
    both = dot(rows[...], high)
    z = both[:WIDE] + both[WIDE:] + dot(rows[:WIDE], low)
    z_high, z_low = halves(z)
    w = (
        dot(z_high, split_high[...])
        + dot(z_low, split_high[...])
        + dot(z_high, split_low[...])
    )
    left = w[:BAND, :WIDE] + turn(w[BAND:, :WIDE])
    right = w[:BAND, WIDE:] + turn(w[BAND:, WIDE:])
    own[...] = left + right
    sign = signs(left.shape)
    left = left * sign
    right = right * sign
    even_out[...] = jnp.where(odd, left, right)
    odd_out[...] = jnp.where(odd, right, left)


def prepare_kernel(index, weight, dose, table, mixed):
    for condition in range(CONDS):
        entry = index[condition]
        for k in range(KERN):
            scale = jnp.sqrt(
                jnp.full((1, WIDE), 0.5 * steepness * dose[entry] * weight[entry, k])
            ) * (1.0 / (NPAD * NPAD))
            for part in range(2):
                kernel = table[entry, k, part]
                doubled = jnp.concatenate([kernel, kernel], 1)
                mixed[condition * KERN + k, part] = doubled * scale


def window_kernel(
    own, even_in, odd_in, target, mixed, rows_t, rows, out_high, out_low, back_both, back_high,
    resist, grad, field,
):
    tile, tiles = lax.axis_index("tile"), lax.axis_size("tile")
    alone = jnp.logical_or(tile == 0, tile == tiles - 1)
    spec = own[...] + even_in[...] + jnp.where(alone, 0.0, odd_in[...])
    turned = turn(spec)
    stack = jnp.concatenate(
        [stacked(mixed[i, 0] * spec + mixed[i, 1] * turned) for i in range(PAIRS)], 1
    )
    high, low = halves(stack)
    first = dot(rows_t[...], jnp.concatenate([high, high], 0)) + dot(rows_t[:, :WIDE], low)
    y_high, y_low = halves(first)
    half = CORE // 2
    q_parts = [[None, None] for _ in range(PAIRS)]
    for condition in range(CONDS):
        for part in range(2):
            r = slice(part * half, (part + 1) * half)
            cols = [slice((condition * KERN + k) * WIDE, (condition * KERN + k + 1) * WIDE) for k in range(KERN)]
            a = jnp.concatenate([y_high[r, c] for c in cols], 0)
            b = jnp.concatenate([y_low[r, c] for c in cols], 0)
            f = dot(jnp.concatenate([a, b], 1), out_high[...]) + dot(a, out_low[...])
            squares = f * f
            power = squares[:half, :CORE] + squares[:half, CORE:] + squares[half:, :CORE] + squares[half:, CORE:]
            t = jnp.tanh(power - 0.5 * steepness * threshold)
            resist[condition, r] = 0.5 + 0.5 * t
            drive = (t + (1.0 - 2.0 * target[r])) * (2.0 - 2.0 * (t * t))
            scaled = jnp.concatenate([drive, drive], 1)
            scaled = jnp.concatenate([scaled, scaled], 0) * f
            s_high, s_low = halves(scaled)
            both = dot(s_high, back_both[...])
            q = both[:, :WIDE] + both[:, WIDE:] + dot(s_low, back_high[...])
            for k in range(KERN):
                q_parts[condition * KERN + k][part] = q[k * half : (k + 1) * half]
    q = jnp.concatenate([jnp.concatenate(p, 0) for p in q_parts], 1)
    q_high, q_low = halves(q)
    both = dot(rows[...], q_high)
    u = both[:WIDE] + both[WIDE:] + dot(rows[:WIDE], q_low)
    total = jnp.zeros((BAND, WIDE), jnp.float32)
    for i in range(PAIRS):
        c = slice(i * WIDE, (i + 1) * WIDE)
        back = u[:BAND, c] + turn(u[BAND:, c])
        total = total + mixed[i, 0] * back - mixed[i, 1] * turn(back)
    grad[...] = total


def synthesize_kernel(own, even_in, odd_in, rows_t, split_high, split_low, gradient):
    tile, tiles = lax.axis_index("tile"), lax.axis_size("tile")
    odd = tile % 2 == 1
    alone = jnp.logical_or(tile == 0, tile == tiles - 1)
    sign = signs((BAND, WIDE))
    beside = even_in[...] * sign
    across = jnp.where(alone, 0.0, odd_in[...] * sign)
    left = own[...] + jnp.where(odd, beside, across)
    right = own[...] + jnp.where(odd, across, beside)
    stack = jnp.concatenate([stacked(left), stacked(right)], 1)
    high, low = halves(stack)
    y = dot(rows_t[...], jnp.concatenate([high, high], 0)) + dot(rows_t[:, :WIDE], low)
    y_high, y_low = halves(y)
    gradient[...] = (
        dot(y_high, split_high[...])
        + dot(y_low, split_high[...])
        + dot(y_high, split_low[...])
    )


def call(kernel, outs, scratch=(), smem=0, n=0, flops=0):
    spec = [pl.BlockSpec(memory_space=pltpu.SMEM)] * smem + [
        pl.BlockSpec(memory_space=pltpu.VMEM)
    ] * (n - smem)
    shapes = [jax.ShapeDtypeStruct(o, jnp.float32) for o in outs]
    return pl.pallas_call(
        kernel,
        out_shape=shapes if len(shapes) > 1 else shapes[0],
        in_specs=spec,
        out_specs=[pl.BlockSpec(memory_space=pltpu.VMEM)] * len(outs)
        if len(outs) > 1
        else pl.BlockSpec(memory_space=pltpu.VMEM),
        scratch_shapes=list(scratch),
        compiler_params=pltpu.CompilerParams(vmem_limit_bytes=16 << 20),
        cost_estimate=pl.CostEstimate(flops=flops, bytes_accessed=1 << 20, transcendentals=0),
    )


def partners(windows, tiles):
    even = [(w * tiles + i, w * tiles + (i ^ 1)) for w in range(windows) for i in range(tiles)]
    odd = []
    for w in range(windows):
        base = w * tiles
        for i in range(1, tiles - 1, 2):
            odd += [(base + i, base + i + 1), (base + i + 1, base + i)]
        other = w ^ 1 if (w ^ 1) < windows else w
        for i in (0, tiles - 1):
            odd.append((base + i, other * tiles + i))
    return even, odd


def local(mask, target, kernel_table, kernel_weight, dose_table, condition_index):
    rows, split, out, back = tables()
    rows_high, rows_low = parts(rows)
    rows_both = side_by_side((rows_high, rows_low), 0)
    rows_t = np.ascontiguousarray(rows_both.T)
    split_high, split_low = parts(split)
    split_t_high, split_t_low = (np.ascontiguousarray(s.T) for s in (split_high, split_low))
    out_high, out_low = parts(out)
    back_high, back_low = parts(back)
    out_twice = side_by_side((out_high, out_high), 0)
    back_both = side_by_side((back_high, back_low), 1)
    even, odd = partners(lax.axis_size("win"), lax.axis_size("tile"))

    def swap(x, y):
        over = ("win", "tile")
        b = lax.ppermute(y, over, odd)
        a = lax.ppermute(x, over, even)
        return a, b

    small = (BAND, WIDE)
    own, to_even, to_odd = call(analyze_kernel, [small] * 3, n=4, flops=10**8)(
        mask, rows_both, split_high, split_low
    )
    mixed = call(prepare_kernel, [(PAIRS, 2, BAND, WIDE)], smem=3, n=4, flops=10**6)(
        condition_index, kernel_weight, dose_table, kernel_table
    )
    from_even, from_odd = swap(to_even, to_odd)
    resist, grad = call(
        window_kernel,
        [(CONDS, CORE, CORE), small],
        scratch=[pltpu.VMEM((8, 128), jnp.float32)],
        n=11,
        flops=10**9,
    )(own, from_even, from_odd, target, mixed, rows_t, rows_both, out_twice, out_low, back_both, back_high)
    from_even, from_odd = swap(grad, grad)
    gradient = call(synthesize_kernel, [(CORE, CORE)], n=6, flops=10**8)(
        grad, from_even, from_odd, rows_t, split_t_high, split_t_low
    )
    return (resist, gradient)


def solution(mesh):
    return jax.shard_map(
        local,
        mesh=mesh,
        in_specs=(P("win", "tile"), P("win", "tile"), P(), P(), P(), P()),
        out_specs=(P(None, "win", "tile"), P("win", "tile")),
        check_vma=False,
    )
```

time: 60 us -> 20.7 us (0.34)
  the two profiles are of different devices: /device:TPU:21 before, /device:TPU:5 now
where the time goes in v1:
time: 20.7 us; the launch traced here: 20.4 us
  local copies, waits for them, and re-layouts  5.71 us (28%)
  Pallas kernels  5.64 us (27%)
  waiting for transfers between devices  5.11 us (25%)
  starting transfers between devices  3.23 us (16%)
  between operations  0.75 us (4%)
    unnamed x35, local copies, waits for them, and re-layouts  5.71 us
    ppermute x2, waiting for transfers between devices, swap(): b = lax.ppermute(y, over, odd)  5.11 us
    pallas_call x1, Pallas kernels, local(): call(window_kernel, [(CONDS, CORE, CORE), small], scratch=[pltpu.VMEM((8,...  3.12 us
    ppermute x2, starting transfers between devices, swap(): b = lax.ppermute(y, over, odd)  2.48 us
    pallas_call x1, Pallas kernels, local(): call(synthesize_kernel, [(CORE, CORE)], n=6, flops=10 ** 8)  1.29 us
    ppermute x2, starting transfers between devices, swap(): a = lax.ppermute(x, over, even)  0.74 us
    pallas_call x1, Pallas kernels, local(): call(prepare_kernel, [(PAIRS, 2, BAND, WIDE)], smem=3, n=4, flops=10 ** 6)  0.71 us
    pallas_call x1, Pallas kernels, local(): call(analyze_kernel, [small] * 3, n=4, flops=10 ** 8)  0.51 us
  transfers between devices with their start and end apart: 4, of which 2 were waited for; matrix products, arithmetic and copies ran while one was open for 0% of the time, Pallas kernels for 3%

profile of v1, /device:TPU:5, one launch (start us, length us, event | category | flops | bytes accessed | tf_op | source)
XLA Modules:
  0.0 20.4 jit_solution(15535572133064737054)
XLA Ops:
  0.6 0.0 copy-start
  0.6 0.0 copy-start.1
  0.6 1.0 %copy-done.1 = f32[256,256]{1,0:T(8,128)S(1)} copy-done((f32[256,256]{1,0:T(8,128)S(1)}, f32[256,256]{1,0:T(8,128)}, u32[]{:S(2)}) %copy-start.1) | copy-done | bytes 262168
  1.6 0.0 copy-start.2
  1.6 0.9 %copy-done.2 = bf16[256,256]{1,0:T(8,128)(2,1)S(1)} copy-done((bf16[256,256]{1,0:T(8,128)(2,1)S(1)}, bf16[256,256]{1,0:T(8,128)(2,1)}, u32[]{:S(2)}) %copy-start.2) | copy-done | bytes 131096
  2.6 0.0 copy-start.4
  2.6 0.9 %copy-done.4 = bf16[256,256]{1,0:T(8,128)(2,1)S(1)} copy-done((bf16[256,256]{1,0:T(8,128)(2,1)S(1)}, bf16[256,256]{1,0:T(8,128)(2,1)}, u32[]{:S(2)}) %copy-start.4) | copy-done | bytes 131096
  3.5 0.0 copy-start.5
  3.5 0.9 %copy-done.5 = bf16[256,256]{1,0:T(8,128)(2,1)S(1)} copy-done((bf16[256,256]{1,0:T(8,128)(2,1)S(1)}, bf16[256,256]{1,0:T(8,128)(2,1)}, u32[]{:S(2)}) %copy-start.5) | copy-done | bytes 131096
  4.4 0.0 copy-start.14
  4.4 0.5 %shard_map.167 = (f32[64,128]{1,0:T(8,128)S(1)}, f32[64,128]{1,0:T(8,128)S(1)}, f32[64,128]{1,0:T(8,128)S(1)}) custom-call(f32[256,256]{1,0:T(8,128)S(1)} %copy-done.1, bf16[256,256]{1,0:T(8,128)(2,1)S(1)} %copy-done.2, bf16[256,256]{1,0:T(8,128)(2,1)S(1)} %copy-done.5, bf16[256,256]{1,0:T(8,128)(2,1)S(1)} %copy-done.4), custom_call_target="tpu_custom_call" | custom-call | flops 100000000 | bytes 1048576 | tf_op jit(solution)/shard_map/pallas_call | solution.py:226
  4.9 0.0 copy-start.16
  4.9 0.7 %collective-permute-start = (f32[64,128]{1,0:T(8,128)S(1)}, f32[64,128]{1,0:T(8,128)S(1)}, u32[]{:S(2)}, u32[]{:S(2)}) collective-permute-start(f32[64,128]{1,0:T(8,128)S(1)} %get-tuple-element.8), channel_id=1, source_target_pairs={{0,1},{1,0},{2,3},{3,2},{4,5},{5,4},{6,7},{7,6},{8,9},{9,8},{10,11... | collective-permute-start | bytes 98312 | tf_op jit(solution)/shard_map/ppermute | solution.py:222
  5.6 0.0 copy-start.9
  5.6 0.0 copy-start.10
  5.6 1.2 %collective-permute-start.1 = (f32[64,128]{1,0:T(8,128)S(1)}, f32[64,128]{1,0:T(8,128)S(1)}, u32[]{:S(2)}, u32[]{:S(2)}) collective-permute-start(f32[64,128]{1,0:T(8,128)S(1)} %get-tuple-element.9), channel_id=1, source_target_pairs={{1,2},{2,1},{3,4},{4,3},{5,6},{6,5},{7,8},{8,7},{9,10},{10,9},{11,... | collective-permute-start | bytes 98312 | tf_op jit(solution)/shard_map/ppermute | solution.py:221
  6.9 0.0 copy-done.16
  6.9 0.1 copy.18.weight
  7.0 0.0 copy-done
  7.0 0.0 copy-done.9
  7.0 0.0 copy-done.10
  7.0 0.0 copy-start.3
  7.0 0.0 copy-start.6
  7.0 0.0 copy-start.11
  7.0 0.0 copy-start.12
  7.0 0.7 %shard_map.168.mixed = f32[4,2,64,128]{3,2,1,0:T(8,128)S(1)} custom-call(s32[2]{0:T(128)S(1)} %copy-done.9, f32[4,2]{1,0:T(4,128)S(1)} %copy.18.weight, f32[4]{0:T(128)S(1)} %copy-done.10, f32[4,2,2,64,64]{4,3,2,1,0:T(8,128)S(1)} %copy-done), custom_call_target="tpu_custom_call" | custom-call | flops 1000000 | bytes 1048576 | tf_op jit(solution)/shard_map/pallas_call | solution.py:229
  7.7 0.0 collective-permute-done.even_in
  7.7 2.1 %collective-permute-done.1.odd_in = f32[64,128]{1,0:T(8,128)S(1)} collective-permute-done((f32[64,128]{1,0:T(8,128)S(1)}, f32[64,128]{1,0:T(8,128)S(1)}, u32[]{:S(2)}, u32[]{:S(2)}) %collective-permute-start.1) | collective-permute-done | bytes 32800 | tf_op jit(solution)/shard_map/ppermute | solution.py:221
  9.9 0.0 copy-done.14
  9.9 0.0 copy-done.3
  9.9 0.0 copy-done.6
  9.9 0.0 copy-done.11
  9.9 0.0 copy-done.12
  9.9 0.0 copy-start.13
  9.9 0.9 %copy-done.13 = bf16[256,512]{1,0:T(8,128)(2,1)S(1)} copy-done((bf16[256,512]{1,0:T(8,128)(2,1)S(1)}, bf16[256,512]{1,0:T(8,128)(2,1)}, u32[]{:S(2)}) %copy-start.13) | copy-done | bytes 262168
  10.9 0.0 copy-start.15
  10.9 0.9 %copy-done.15 = bf16[128,512]{1,0:T(8,128)(2,1)S(1)} copy-done((bf16[128,512]{1,0:T(8,128)(2,1)S(1)}, bf16[128,512]{1,0:T(8,128)(2,1)}, u32[]{:S(2)}) %copy-start.15) | copy-done | bytes 131096
  11.8 0.0 copy-start.7
  11.8 0.0 copy-start.8
  11.8 3.1 %shard_map.169 = (f32[2,256,256]{2,1,0:T(8,128)}, f32[64,128]{1,0:T(8,128)S(1)}) custom-call(f32[64,128]{1,0:T(8,128)S(1)} %get-tuple-element.7.own, f32[64,128]{1,0:T(8,128)S(1)} %collective-permute-done.even_in, f32[64,128]{1,0:T(8,128)S(1)} %collective-permute-done.1.odd_in, f32[256,256]{1,0:T(8,128)S(1)} %copy-done.11, ...), custom_call_target="tpu_custom_call" | custom-call | flops 1000000000 | bytes 1048576 | tf_op jit(solution)/shard_map/pallas_call | solution.py:233
  14.9 1.3 %collective-permute-start.3 = (f32[64,128]{1,0:T(8,128)S(1)}, f32[64,128]{1,0:T(8,128)S(1)}, u32[]{:S(2)}, u32[]{:S(2)}) collective-permute-start(f32[64,128]{1,0:T(8,128)S(1)} %get-tuple-element.11.own), channel_id=1, source_target_pairs={{1,2},{2,1},{3,4},{4,3},{5,6},{6,5},{7,8},{8,7},{9,10},{10,9},{11,... | collective-permute-start | bytes 98312 | tf_op jit(solution)/shard_map/ppermute | solution.py:221
  16.2 0.0 collective-permute-start.2
  16.2 3.0 %collective-permute-done.3.odd_in = f32[64,128]{1,0:T(8,128)S(1)} collective-permute-done((f32[64,128]{1,0:T(8,128)S(1)}, f32[64,128]{1,0:T(8,128)S(1)}, u32[]{:S(2)}, u32[]{:S(2)}) %collective-permute-start.3) | collective-permute-done | bytes 32800 | tf_op jit(solution)/shard_map/ppermute | solution.py:221
  19.1 0.0 collective-permute-done.2.even_in
  19.1 0.0 copy-done.7
  19.1 0.0 copy-done.8
  19.1 1.3 %shard_map.170 = f32[256,256]{1,0:T(8,128)} custom-call(f32[64,128]{1,0:T(8,128)S(1)} %get-tuple-element.11.own, f32[64,128]{1,0:T(8,128)S(1)} %collective-permute-done.2.even_in, f32[64,128]{1,0:T(8,128)S(1)} %collective-permute-done.3.odd_in, bf16[256,256]{1,0:T(8,128)(2,1)S(1)} %copy-done.6, bf16[256,256]{1,0:T(8,128)(2,1)S(1)} %copy-done.8, ...), custom_call_target="tpu_custom_call" | custom-call | flops 100000000 | bytes 1048576 | tf_op jit(solution)/shard_map/pallas_call | solution.py:241
Async XLA Ops:
  0.6 6.3 %copy-start = (f32[4,2,2,64,64]{4,3,2,1,0:T(8,128)S(1)}, f32[4,2,2,64,64]{4,3,2,1,0:T(8,128)}, u32[]{:S(2)}) copy-start(f32[4,2,2,64,64]{4,3,2,1,0:T(8,128)} %table.1) | copy-start | bytes 786436
  0.6 1.0 %copy-start.1 = (f32[256,256]{1,0:T(8,128)S(1)}, f32[256,256]{1,0:T(8,128)}, u32[]{:S(2)}) copy-start(f32[256,256]{1,0:T(8,128)} %mask.1) | copy-start | bytes 786436
  1.6 0.9 %copy-start.2 = (bf16[256,256]{1,0:T(8,128)(2,1)S(1)}, bf16[256,256]{1,0:T(8,128)(2,1)}, u32[]{:S(2)}) copy-start(bf16[256,256]{1,0:T(8,128)(2,1)} %constant.20.clone.rows) | copy-start | bytes 393220
  2.6 0.9 %copy-start.4 = (bf16[256,256]{1,0:T(8,128)(2,1)S(1)}, bf16[256,256]{1,0:T(8,128)(2,1)}, u32[]{:S(2)}) copy-start(bf16[256,256]{1,0:T(8,128)(2,1)} %constant.22.clone.split_low) | copy-start | bytes 393220
  3.5 0.9 %copy-start.5 = (bf16[256,256]{1,0:T(8,128)(2,1)S(1)}, bf16[256,256]{1,0:T(8,128)(2,1)}, u32[]{:S(2)}) copy-start(bf16[256,256]{1,0:T(8,128)(2,1)} %constant.21.clone.split_high) | copy-start | bytes 393220
  4.4 5.5 %copy-start.14 = (bf16[512,128]{1,0:T(8,128)(2,1)S(1)}, bf16[512,128]{1,0:T(8,128)(2,1)}, u32[]{:S(2)}) copy-start(bf16[512,128]{1,0:T(8,128)(2,1)} %constant.27.clone.back_high) | copy-start | bytes 393220
  4.9 2.0 %copy-start.16 = (f32[4,2]{0,1:T(2,128)S(1)}, f32[4,2]{0,1:T(2,128)}, u32[]{:S(2)}) copy-start(f32[4,2]{0,1:T(2,128)} %param.19) | copy-start | bytes 100
  4.9 2.8 %collective-permute-start = (f32[64,128]{1,0:T(8,128)S(1)}, f32[64,128]{1,0:T(8,128)S(1)}, u32[]{:S(2)}, u32[]{:S(2)}) collective-permute-start(f32[64,128]{1,0:T(8,128)S(1)} %get-tuple-element.8), channel_id=1, source_target_pairs={{0,1},{1,0},{2,3},{3,2},{4,5},{5,4},{6,7},{7,6},{8,9},{9,8},{10,11... | collective-permute-start | bytes 98312 | tf_op jit(solution)/shard_map/ppermute | solution.py:222
  5.6 1.3 %copy-start.9 = (s32[2]{0:T(128)S(1)}, s32[2]{0:T(128)}, u32[]{:S(2)}) copy-start(s32[2]{0:T(128)} %index.1) | copy-start | bytes 28
  5.6 1.3 %copy-start.10 = (f32[4]{0:T(128)S(1)}, f32[4]{0:T(128)}, u32[]{:S(2)}) copy-start(f32[4]{0:T(128)} %dose.1) | copy-start | bytes 52
  5.6 4.2 %collective-permute-start.1 = (f32[64,128]{1,0:T(8,128)S(1)}, f32[64,128]{1,0:T(8,128)S(1)}, u32[]{:S(2)}, u32[]{:S(2)}) collective-permute-start(f32[64,128]{1,0:T(8,128)S(1)} %get-tuple-element.9), channel_id=1, source_target_pairs={{1,2},{2,1},{3,4},{4,3},{5,6},{6,5},{7,8},{8,7},{9,10},{10,9},{11,... | collective-permute-start | bytes 98312 | tf_op jit(solution)/shard_map/ppermute | solution.py:221
  7.0 2.9 %copy-start.3 = (bf16[256,256]{1,0:T(8,128)(2,1)S(1)}, bf16[256,256]{1,0:T(8,128)(2,1)}, u32[]{:S(2)}) copy-start(bf16[256,256]{1,0:T(8,128)(2,1)} %constant.20.clone.rows) | copy-start | bytes 393220
  7.0 2.9 %copy-start.6 = (bf16[256,256]{1,0:T(8,128)(2,1)S(1)}, bf16[256,256]{1,0:T(8,128)(2,1)}, u32[]{:S(2)}) copy-start(bf16[256,256]{1,0:T(8,128)(2,1)} %constant.23.clone.rows_t) | copy-start | bytes 393220
  7.0 2.9 %copy-start.11 = (f32[256,256]{1,0:T(8,128)S(1)}, f32[256,256]{1,0:T(8,128)}, u32[]{:S(2)}) copy-start(f32[256,256]{1,0:T(8,128)} %target.1) | copy-start | bytes 786436
  7.0 2.9 %copy-start.12 = (bf16[512,256]{1,0:T(8,128)(2,1)S(1)}, bf16[512,256]{1,0:T(8,128)(2,1)}, u32[]{:S(2)}) copy-start(bf16[512,256]{1,0:T(8,128)(2,1)} %constant.26.clone.back_both) | copy-start | bytes 786436
  9.9 1.0 %copy-start.13 = (bf16[256,512]{1,0:T(8,128)(2,1)S(1)}, bf16[256,512]{1,0:T(8,128)(2,1)}, u32[]{:S(2)}) copy-start(bf16[256,512]{1,0:T(8,128)(2,1)} %constant.24.clone.out_high) | copy-start | bytes 786436
  10.9 0.9 %copy-start.15 = (bf16[128,512]{1,0:T(8,128)(2,1)S(1)}, bf16[128,512]{1,0:T(8,128)(2,1)}, u32[]{:S(2)}) copy-start(bf16[128,512]{1,0:T(8,128)(2,1)} %constant.25.clone.out_low) | copy-start | bytes 393220
  11.8 7.4 %copy-start.7 = (bf16[256,256]{1,0:T(8,128)(2,1)S(1)}, bf16[256,256]{1,0:T(8,128)(2,1)}, u32[]{:S(2)}) copy-start(bf16[256,256]{1,0:T(8,128)(2,1)} %constant.29.clone.split_low) | copy-start | bytes 393220
  11.8 7.4 %copy-start.8 = (bf16[256,256]{1,0:T(8,128)(2,1)S(1)}, bf16[256,256]{1,0:T(8,128)(2,1)}, u32[]{:S(2)}) copy-start(bf16[256,256]{1,0:T(8,128)(2,1)} %constant.28.clone.split_high) | copy-start | bytes 393220
  14.9 4.2 %collective-permute-start.3 = (f32[64,128]{1,0:T(8,128)S(1)}, f32[64,128]{1,0:T(8,128)S(1)}, u32[]{:S(2)}, u32[]{:S(2)}) collective-permute-start(f32[64,128]{1,0:T(8,128)S(1)} %get-tuple-element.11.own), channel_id=1, source_target_pairs={{1,2},{2,1},{3,4},{4,3},{5,6},{6,5},{7,8},{8,7},{9,10},{10,9},{11,... | collective-permute-start | bytes 98312 | tf_op jit(solution)/shard_map/ppermute | solution.py:221
  16.2 3.0 %collective-permute-start.2 = (f32[64,128]{1,0:T(8,128)S(1)}, f32[64,128]{1,0:T(8,128)S(1)}, u32[]{:S(2)}, u32[]{:S(2)}) collective-permute-start(f32[64,128]{1,0:T(8,128)S(1)} %get-tuple-element.11.own), channel_id=1, source_target_pairs={{0,1},{1,0},{2,3},{3,2},{4,5},{5,4},{6,7},{7,6},{8,9},{9,8},{10,11... | collective-permute-start | bytes 98312 | tf_op jit(solution)/shard_map/ppermute | solution.py:222

commit v2 on v1

v2 whole, which is shorter than its diff:
```python
import math

import jax
import jax.numpy as jnp
import ml_dtypes
import numpy as np
from jax import lax
from jax.experimental import pallas as pl
from jax.experimental.pallas import tpu as pltpu
from jax.sharding import PartitionSpec as P

NPAD = 512
MARGIN = 128
BAND = 64
KERN = 2
CONDS = 2
CORE = 256
PAIRS = CONDS * KERN
WIDE = 2 * BAND

steepness = 6.0
threshold = 0.3


def parts(table):
    high = table.astype(ml_dtypes.bfloat16)
    low = (table - high.astype(np.float64)).astype(ml_dtypes.bfloat16)
    return high, low


def tables():
    frequency = np.arange(BAND)[:, None] - BAND // 2
    position = np.arange(MARGIN, MARGIN + CORE)[None, :]
    phase = (frequency * position % NPAD) * (2.0 * math.pi / NPAD)
    cosine, sine = np.cos(phase), -np.sin(phase)
    rows = np.concatenate([cosine, sine], 0)
    out = np.block([[cosine, -sine], [sine, cosine]])
    back = np.block([[cosine.T, sine.T], [-sine.T, cosine.T]])
    return rows, out, back


def halves(x):
    high = x.astype(jnp.bfloat16)
    return high, (x - high.astype(jnp.float32)).astype(jnp.bfloat16)


def dot(a, b):
    return jnp.dot(a, b, preferred_element_type=jnp.float32)


def turn(x):
    lane = lax.broadcasted_iota(jnp.int32, x.shape, 1)
    rolled = pltpu.roll(x, BAND, 1)
    return jnp.where(lane < BAND, -rolled, rolled)


def signs(shape):
    lane = lax.broadcasted_iota(jnp.int32, shape, 1)
    return jnp.where(lane % 2 == 0, 1.0, -1.0).astype(jnp.float32)


def stacked(x):
    return jnp.concatenate([x, -turn(x)], 0)


def copies(pairs, sems):
    moves = [pltpu.make_async_copy(a, b, sems.at[i]) for i, (a, b) in enumerate(pairs)]
    for move in moves:
        move.start()
    return moves


def place():
    tile, tiles = lax.axis_index("tile"), lax.axis_size("tile")
    return tile % 2 == 1, jnp.logical_or(tile == 0, tile == tiles - 1)


def analyze_kernel(mask_hbm, rows_hbm, rows_t_hbm, own, even_out, odd_out, rows, rows_t, mask, sems):
    moves = copies([(mask_hbm, mask), (rows_hbm, rows), (rows_t_hbm, rows_t)], sems)
    for move in moves:
        move.wait()
    odd, _ = place()
    high, low = halves(mask[...])
    both = dot(rows[...], high)
    z = both[:WIDE] + both[WIDE:] + dot(rows[:WIDE], low)
    z_high, z_low = halves(z)
    z_both = jnp.concatenate([z_high, z_low], 0)
    sides = []
    for side in range(2):
        c = slice(side * MARGIN, (side + 1) * MARGIN)
        both = dot(z_both[:, c], rows_t[c, :WIDE])
        w = both[:WIDE] + both[WIDE:] + dot(z_high[:, c], rows_t[c, WIDE:])
        sides.append(w[:BAND] + turn(w[BAND:]))
    left, right = sides
    own[...] = left + right
    sign = signs(left.shape)
    left = left * sign
    right = right * sign
    even_out[...] = jnp.where(odd, left, right)
    odd_out[...] = jnp.where(odd, right, left)


def prepare_kernel(
    index, weight, dose, after, table_hbm, target_hbm, out_high_hbm, out_low_hbm, back_hbm,
    mixed, target, out_high, out_low, back, table, sems,
):
    moves = copies(
        [(table_hbm.at[index[c]], table.at[c]) for c in range(CONDS)]
        + [
            (target_hbm, target),
            (out_high_hbm, out_high),
            (out_low_hbm, out_low),
            (back_hbm, back),
        ],
        sems,
    )
    for condition in range(CONDS):
        entry = index[condition]
        moves[condition].wait()
        for k in range(KERN):
            scale = jnp.sqrt(
                jnp.full((1, WIDE), 0.5 * steepness * dose[entry] * weight[k, entry])
            ) * (1.0 / (NPAD * NPAD))
            for part in range(2):
                kernel = table[condition, k, part]
                doubled = jnp.concatenate([kernel, kernel], 1)
                mixed[condition * KERN + k, part] = doubled * scale
    for move in moves[CONDS:]:
        move.wait()


def window_kernel(
    own, even_in, odd_in, target, mixed, rows_t, rows, out_high, out_low, back_both,
    resist, grad,
):
    _, alone = place()
    spec = own[...] + even_in[...] + jnp.where(alone, 0.0, odd_in[...])
    turned = turn(spec)
    stack = jnp.concatenate(
        [stacked(mixed[i, 0] * spec + mixed[i, 1] * turned) for i in range(PAIRS)], 1
    )
    high, low = halves(stack)
    first = dot(rows_t[...], jnp.concatenate([high, high], 0)) + dot(rows_t[:, :WIDE], low)
    y_high, y_low = halves(first)
    out_twice = jnp.concatenate([out_high[...], out_high[...]], 0)
    half = CORE // 2
    q_parts = [[None, None] for _ in range(PAIRS)]
    for condition in range(CONDS):
        for part in range(2):
            r = slice(part * half, (part + 1) * half)
            group = [condition * KERN + k for k in range(KERN)]
            cols = [slice(i * WIDE, (i + 1) * WIDE) for i in group]
            a = jnp.concatenate([y_high[r, c] for c in cols], 0)
            b = jnp.concatenate([y_low[r, c] for c in cols], 0)
            f = dot(jnp.concatenate([a, b], 1), out_twice) + dot(a, out_low[...])
            squares = f * f
            power = sum(
                squares[k * half : (k + 1) * half, :CORE] + squares[k * half : (k + 1) * half, CORE:]
                for k in range(KERN)
            )
            t = jnp.tanh(power - 0.5 * steepness * threshold)
            resist[condition, r] = 0.5 + 0.5 * t
            drive = (t + (1.0 - 2.0 * target[r])) * (2.0 - 2.0 * (t * t))
            drive = jnp.concatenate([drive, drive], 1)
            scaled = jnp.concatenate([drive] * KERN, 0) * f
            s_high, s_low = halves(scaled)
            both = dot(s_high, back_both[...])
            q = both[:, :WIDE] + both[:, WIDE:] + dot(s_low, back_both[:, :WIDE])
            for k in range(KERN):
                q_parts[group[k]][part] = q[k * half : (k + 1) * half]
    q = jnp.concatenate([jnp.concatenate(p, 0) for p in q_parts], 1)
    q_high, q_low = halves(q)
    both = dot(rows[...], q_high)
    u = both[:WIDE] + both[WIDE:] + dot(rows[:WIDE], q_low)
    total = jnp.zeros((BAND, WIDE), jnp.float32)
    for i in range(PAIRS):
        c = slice(i * WIDE, (i + 1) * WIDE)
        back = u[:BAND, c] + turn(u[BAND:, c])
        total = total + mixed[i, 0] * back - mixed[i, 1] * turn(back)
    grad[...] = total


def synthesize(spec, rows, rows_t, side, out):
    high, low = halves(stacked(spec))
    y = dot(rows_t[...], jnp.concatenate([high, high], 0)) + dot(rows_t[:, :WIDE], low)
    y_high, y_low = halves(y)
    c = pl.ds(pl.multiple_of(side * MARGIN, MARGIN), MARGIN)
    both = dot(jnp.concatenate([y_high, y_low], 0), rows[:WIDE, c])
    out[...] = both[:CORE] + both[CORE:] + dot(y_high, rows[WIDE:, c])


def beside_kernel(own, even_in, rows, rows_t, resist, resist_hbm, gradient_hbm, out, sems):
    odd, _ = place()
    side = jnp.where(odd, 0, 1)
    first = copies([(resist, resist_hbm)], sems)[0]
    synthesize(own[...] + even_in[...] * signs((BAND, WIDE)), rows, rows_t, side, out)
    c = pl.ds(pl.multiple_of(side * MARGIN, MARGIN), MARGIN)
    second = pltpu.make_async_copy(out, gradient_hbm.at[:, c], sems.at[1])
    second.start()
    first.wait()
    second.wait()


def across_kernel(own, odd_in, rows, rows_t, half_hbm, gradient_hbm, out, sems):
    odd, alone = place()
    side = jnp.where(odd, 1, 0)
    extra = jnp.where(alone, 0.0, odd_in[...] * signs((BAND, WIDE)))
    synthesize(own[...] + extra, rows, rows_t, side, out)
    c = pl.ds(pl.multiple_of(side * MARGIN, MARGIN), MARGIN)
    move = pltpu.make_async_copy(out, gradient_hbm.at[:, c], sems.at[0])
    move.start()
    move.wait()


def pinned(*arrays):
    return [pltpu.with_memory_space_constraint(jnp.asarray(a), pltpu.HBM) for a in arrays]


SPACES = {"v": pltpu.VMEM, "h": pltpu.HBM, "s": pltpu.SMEM}


def call(kernel, ins, outs, scratch=(), aliases=None, flops=10**6):
    shapes = [jax.ShapeDtypeStruct(shape, dtype) for _, shape, dtype in outs]
    specs = [pl.BlockSpec(memory_space=SPACES[o[0]]) for o in outs]
    return pl.pallas_call(
        kernel,
        out_shape=shapes if len(shapes) > 1 else shapes[0],
        in_specs=[pl.BlockSpec(memory_space=SPACES[i]) for i in ins],
        out_specs=specs if len(specs) > 1 else specs[0],
        scratch_shapes=list(scratch),
        input_output_aliases=aliases or {},
        compiler_params=pltpu.CompilerParams(vmem_limit_bytes=16 << 20),
        cost_estimate=pl.CostEstimate(flops=flops, bytes_accessed=1 << 16, transcendentals=0),
    )


def partners(windows, tiles):
    even = [(w * tiles + i, w * tiles + (i ^ 1)) for w in range(windows) for i in range(tiles)]
    odd = []
    for w in range(windows):
        base = w * tiles
        for i in range(1, tiles - 1, 2):
            odd += [(base + i, base + i + 1), (base + i + 1, base + i)]
        other = w ^ 1 if (w ^ 1) < windows else w
        for i in (0, tiles - 1):
            odd.append((base + i, other * tiles + i))
    return even, odd


def local(mask, target, kernel_table, kernel_weight, dose_table, condition_index):
    rows, out, back = tables()
    rows_table = np.concatenate(parts(rows), 0)
    rows_t_table = np.ascontiguousarray(rows_table.T)
    out_high, out_low = parts(out)
    back_table = np.concatenate(parts(back), 1)
    even, odd = partners(lax.axis_size("win"), lax.axis_size("tile"))

    def swap(x, y):
        over = ("win", "tile")
        b = lax.ppermute(y, over, odd)
        a = lax.ppermute(x, over, even)
        return a, b

    f32, bf16 = jnp.float32, jnp.bfloat16
    small = ("v", (BAND, WIDE), f32)
    square = (CORE, CORE)
    dma = pltpu.SemaphoreType.DMA
    own, to_even, to_odd, rows, rows_t = call(
        analyze_kernel,
        "hhh",
        [small] * 3 + [("v", square, bf16)] * 2,
        [pltpu.VMEM(square, f32), dma((3,))],
    )(*pinned(mask, rows_table, rows_t_table))
    mixed, goal, out_high, out_low, back = call(
        prepare_kernel,
        "sss" + "v" + "hhhhh",
        [
            ("v", (PAIRS, 2, BAND, WIDE), f32),
            ("v", square, f32),
            ("v", out_high.shape, bf16),
            ("v", out_low.shape, bf16),
            ("v", back_table.shape, bf16),
        ],
        [pltpu.VMEM((CONDS, KERN, 2, BAND, BAND), f32), dma((CONDS + 4,))],
    )(
        condition_index, kernel_weight.T, dose_table, own,
        *pinned(kernel_table, target, out_high, out_low, back_table),
    )
    from_even, from_odd = swap(to_even, to_odd)
    resist, grad = call(
        window_kernel, "v" * 10, [("v", (CONDS, CORE, CORE), f32), small]
    )(own, from_even, from_odd, goal, mixed, rows_t, rows, out_high, out_low, back)
    from_even, from_odd = swap(grad, grad)
    strip = pltpu.VMEM((CORE, MARGIN), f32)
    resist, gradient = call(
        beside_kernel,
        "v" * 5,
        [("h", (CONDS, CORE, CORE), f32), ("h", square, f32)],
        [strip, dma((2,))],
    )(grad, from_even, rows, rows_t, resist)
    gradient = call(
        across_kernel, "vvvvh", [("h", square, f32)], [strip, dma((1,))], {4: 0}
    )(grad, from_odd, rows, rows_t, gradient)
    return (resist, gradient)


def solution(mesh):
    return jax.shard_map(
        local,
        mesh=mesh,
        in_specs=(P("win", "tile"), P("win", "tile"), P(), P(), P(), P()),
        out_specs=(P(None, "win", "tile"), P("win", "tile")),
        check_vma=False,
    )
```

time: 20.7 us -> 16 us (0.77)
  the two profiles are of different devices: /device:TPU:5 before, /device:TPU:0 now
where the time goes in v2:
time: 16 us; the launch traced here: 15.9 us
  Pallas kernels  8.44 us (53%)
  starting transfers between devices  4.78 us (30%)
  waiting for transfers between devices  1.26 us (8%)
  between operations  0.69 us (4%)
  local copies, waits for them, and re-layouts  0.68 us (4%)
    ppermute x2, starting transfers between devices, swap(): b = lax.ppermute(y, over, odd)  4.04 us
    pallas_call x1, Pallas kernels, local(): call(window_kernel, 'v' * 10, [('v', (CONDS, CORE, CORE), f32), small])  2.67 us
    pallas_call x1, Pallas kernels, local(): call(prepare_kernel, 'sss' + 'v' + 'hhhhh', [('v', (PAIRS, 2, BAND, WIDE)...  1.85 us
    pallas_call x1, Pallas kernels, local(): call(analyze_kernel, 'hhh', [small] * 3 + [('v', square, bf16)] * 2, [plt...  1.6 us
    ppermute x2, waiting for transfers between devices, swap(): b = lax.ppermute(y, over, odd)  1.26 us
    pallas_call x1, Pallas kernels, local(): call(beside_kernel, 'v' * 5, [('h', (CONDS, CORE, CORE), f32), ('h', squa...  1.17 us
    pallas_call x1, Pallas kernels, local(): call(across_kernel, 'vvvvh', [('h', square, f32)], [strip, dma((1,))], {4...  1.15 us
    ppermute x2, starting transfers between devices, swap(): a = lax.ppermute(x, over, even)  0.73 us
  transfers between devices with their start and end apart: 4, of which 1 were waited for; matrix products, arithmetic and copies ran while one was open for 0% of the time, Pallas kernels for 19%

profile of v2, /device:TPU:0, one launch (start us, length us, event | category | flops | bytes accessed | tf_op | source)
XLA Modules:
  0.0 15.9 jit_solution(14325545332711828649)
XLA Ops:
  0.6 1.6 %shard_map.122 = (f32[64,128]{1,0:T(8,128)S(1)}, f32[64,128]{1,0:T(8,128)S(1)}, f32[64,128]{1,0:T(8,128)S(1)}, bf16[256,256]{1,0:T(8,128)(2,1)S(1)}, bf16[256,256]{1,0:T(8,128)(2,1)S(1)}) custom-call(f32[256,256]{1,0:T(8,128)} %mask_hbm.1, bf16[256,256]{1,0:T(8,128)(2,1)} %constant.10.clone.rows_hbm, bf16[256,256]{1,0:T(8,128)(2,1)} %constant.11.clone.rows_t_hbm), custom_call_target="tpu_custom_call" | custom-call | flops 1000000 | bytes 65536 | tf_op jit(solution)/shard_map/pallas_call | solution.py:268
  2.2 0.0 copy-start.2
  2.2 0.5 %collective-permute-start = (f32[64,128]{1,0:T(8,128)S(1)}, f32[64,128]{1,0:T(8,128)S(1)}, u32[]{:S(2)}, u32[]{:S(2)}) collective-permute-start(f32[64,128]{1,0:T(8,128)S(1)} %get-tuple-element.17), channel_id=1, source_target_pairs={{0,1},{1,0},{2,3},{3,2},{4,5},{5,4},{6,7},{7,6},{8,9},{9,8},{10,11... | collective-permute-start | bytes 98312 | tf_op jit(solution)/shard_map/ppermute | solution.py:261
  2.8 2.6 %collective-permute-start.1 = (f32[64,128]{1,0:T(8,128)S(1)}, f32[64,128]{1,0:T(8,128)S(1)}, u32[]{:S(2)}, u32[]{:S(2)}) collective-permute-start(f32[64,128]{1,0:T(8,128)S(1)} %get-tuple-element.18), channel_id=1, source_target_pairs={{1,2},{2,1},{3,4},{4,3},{5,6},{6,5},{7,8},{8,7},{9,10},{10,9},{11,... | collective-permute-start | bytes 98312 | tf_op jit(solution)/shard_map/ppermute | solution.py:260
  5.3 0.0 copy-start
  5.3 0.0 copy-start.1
  5.3 0.0 copy-done.2
  5.3 0.7 %copy-done = f32[4,2]{0,1:T(2,128)S(1)} copy-done((f32[4,2]{0,1:T(2,128)S(1)}, f32[4,2]{0,1:T(2,128)}, u32[]{:S(2)}) %copy-start) | copy-done | bytes 56
  6.0 0.0 copy-done.1
  6.0 1.9 %shard_map.123 = (f32[4,2,64,128]{3,2,1,0:T(8,128)S(1)}, f32[256,256]{1,0:T(8,128)S(1)}, bf16[128,512]{1,0:T(8,128)(2,1)S(1)}, bf16[128,512]{1,0:T(8,128)(2,1)S(1)}, bf16[512,256]{1,0:T(8,128)(2,1)S(1)}) custom-call(s32[2]{0:T(128)S(1)} %copy-done.1, f32[2,4]{1,0:T(2,128)S(1)} %bitcast.1, f32[4]{0:T(128)S(1)} %copy-done.2, ...), custom_call_target="tpu_custom_call" | custom-call | flops 1000000 | bytes 65536 | tf_op jit(solution)/shard_map/pallas_call | solution.py:274
  7.9 0.0 collective-permute-done.even_in
  7.9 0.0 collective-permute-done.1.odd_in
  7.9 2.7 %shard_map.124 = (f32[2,256,256]{2,1,0:T(8,128)S(1)}, f32[64,128]{1,0:T(8,128)S(1)}) custom-call(f32[64,128]{1,0:T(8,128)S(1)} %get-tuple-element.16.after.own, f32[64,128]{1,0:T(8,128)S(1)} %collective-permute-done.even_in, f32[64,128]{1,0:T(8,128)S(1)} %collective-permute-done.1.odd_in, f32[256,256]{1,0:T(8,128)S(1)} %get-tuple-element.19.target, ...), custom_call_target="tpu_custom_call" | custom-call | flops 1000000 | bytes 65536 | tf_op jit(solution)/shard_map/pallas_call | solution.py:290
  10.6 0.2 %collective-permute-start.2 = (f32[64,128]{1,0:T(8,128)S(1)}, f32[64,128]{1,0:T(8,128)S(1)}, u32[]{:S(2)}, u32[]{:S(2)}) collective-permute-start(f32[64,128]{1,0:T(8,128)S(1)} %get-tuple-element.26.own), channel_id=1, source_target_pairs={{0,1},{1,0},{2,3},{3,2},{4,5},{5,4},{6,7},{7,6},{8,9},{9,8},{10,11... | collective-permute-start | bytes 98312 | tf_op jit(solution)/shard_map/ppermute | solution.py:261
  10.8 1.5 %collective-permute-start.3 = (f32[64,128]{1,0:T(8,128)S(1)}, f32[64,128]{1,0:T(8,128)S(1)}, u32[]{:S(2)}, u32[]{:S(2)}) collective-permute-start(f32[64,128]{1,0:T(8,128)S(1)} %get-tuple-element.26.own), channel_id=1, source_target_pairs={{1,2},{2,1},{3,4},{4,3},{5,6},{6,5},{7,8},{8,7},{9,10},{10,9},{11,... | collective-permute-start | bytes 98312 | tf_op jit(solution)/shard_map/ppermute | solution.py:260
  12.3 0.0 collective-permute-done.2.even_in
  12.3 1.2 %shard_map.125 = (f32[2,256,256]{2,1,0:T(8,128)}, f32[256,256]{1,0:T(8,128)}) custom-call(f32[64,128]{1,0:T(8,128)S(1)} %get-tuple-element.26.own, f32[64,128]{1,0:T(8,128)S(1)} %collective-permute-done.2.even_in, bf16[256,256]{1,0:T(8,128)(2,1)S(1)} %get-tuple-element.22.rows, bf16[256,256]{1,0:T(8,128)(2,1)S(1)} %get-tuple-element.21.rows_t, ...), custom_call_target="tpu_custom_call" | custom-call | flops 1000000 | bytes 65536 | tf_op jit(solution)/shard_map/pallas_call | solution.py:295
  13.4 1.3 %collective-permute-done.3.odd_in = f32[64,128]{1,0:T(8,128)S(1)} collective-permute-done((f32[64,128]{1,0:T(8,128)S(1)}, f32[64,128]{1,0:T(8,128)S(1)}, u32[]{:S(2)}, u32[]{:S(2)}) %collective-permute-start.3) | collective-permute-done | bytes 32800 | tf_op jit(solution)/shard_map/ppermute | solution.py:260
  14.7 1.2 %shard_map.126 = f32[256,256]{1,0:T(8,128)} custom-call(f32[64,128]{1,0:T(8,128)S(1)} %get-tuple-element.26.own, f32[64,128]{1,0:T(8,128)S(1)} %collective-permute-done.3.odd_in, bf16[256,256]{1,0:T(8,128)(2,1)S(1)} %get-tuple-element.22.rows, bf16[256,256]{1,0:T(8,128)(2,1)S(1)} %get-tuple-element.21.rows_t, ...), custom_call_target="tpu_custom_call", output_to_operand_aliasing={{}: (4, {})} | custom-call | flops 1000000 | bytes 65536 | tf_op jit(solution)/shard_map/pallas_call | solution.py:301
Async XLA Ops:
  2.2 3.1 %copy-start.2 = (f32[4]{0:T(128)S(1)}, f32[4]{0:T(128)}, u32[]{:S(2)}) copy-start(f32[4]{0:T(128)} %dose.1) | copy-start | bytes 52
  2.2 5.6 %collective-permute-start = (f32[64,128]{1,0:T(8,128)S(1)}, f32[64,128]{1,0:T(8,128)S(1)}, u32[]{:S(2)}, u32[]{:S(2)}) collective-permute-start(f32[64,128]{1,0:T(8,128)S(1)} %get-tuple-element.17), channel_id=1, source_target_pairs={{0,1},{1,0},{2,3},{3,2},{4,5},{5,4},{6,7},{7,6},{8,9},{9,8},{10,11... | collective-permute-start | bytes 98312 | tf_op jit(solution)/shard_map/ppermute | solution.py:261
  2.8 5.1 %collective-permute-start.1 = (f32[64,128]{1,0:T(8,128)S(1)}, f32[64,128]{1,0:T(8,128)S(1)}, u32[]{:S(2)}, u32[]{:S(2)}) collective-permute-start(f32[64,128]{1,0:T(8,128)S(1)} %get-tuple-element.18), channel_id=1, source_target_pairs={{1,2},{2,1},{3,4},{4,3},{5,6},{6,5},{7,8},{8,7},{9,10},{10,9},{11,... | collective-permute-start | bytes 98312 | tf_op jit(solution)/shard_map/ppermute | solution.py:260
  5.3 0.7 %copy-start = (f32[4,2]{0,1:T(2,128)S(1)}, f32[4,2]{0,1:T(2,128)}, u32[]{:S(2)}) copy-start(f32[4,2]{0,1:T(2,128)} %param.14) | copy-start | bytes 100
  5.3 0.7 %copy-start.1 = (s32[2]{0:T(128)S(1)}, s32[2]{0:T(128)}, u32[]{:S(2)}) copy-start(s32[2]{0:T(128)} %index.1) | copy-start | bytes 28
  10.6 1.7 %collective-permute-start.2 = (f32[64,128]{1,0:T(8,128)S(1)}, f32[64,128]{1,0:T(8,128)S(1)}, u32[]{:S(2)}, u32[]{:S(2)}) collective-permute-start(f32[64,128]{1,0:T(8,128)S(1)} %get-tuple-element.26.own), channel_id=1, source_target_pairs={{0,1},{1,0},{2,3},{3,2},{4,5},{5,4},{6,7},{7,6},{8,9},{9,8},{10,11... | collective-permute-start | bytes 98312 | tf_op jit(solution)/shard_map/ppermute | solution.py:261
  10.8 3.9 %collective-permute-start.3 = (f32[64,128]{1,0:T(8,128)S(1)}, f32[64,128]{1,0:T(8,128)S(1)}, u32[]{:S(2)}, u32[]{:S(2)}) collective-permute-start(f32[64,128]{1,0:T(8,128)S(1)} %get-tuple-element.26.own), channel_id=1, source_target_pairs={{1,2},{2,1},{3,4},{4,3},{5,6},{6,5},{7,8},{8,7},{9,10},{10,9},{11,... | collective-permute-start | bytes 98312 | tf_op jit(solution)/shard_map/ppermute | solution.py:260

commit v3 on v2

--- a/solution.py
+++ b/solution.py
@@ -13,10 +13,12 @@
 MARGIN = 128
 BAND = 64
 KERN = 2
+TABLE = 4
 CONDS = 2
 CORE = 256
 PAIRS = CONDS * KERN
 WIDE = 2 * BAND
+CHUNK = 64
 
 steepness = 6.0
 threshold = 0.3
@@ -34,9 +36,7 @@
     phase = (frequency * position % NPAD) * (2.0 * math.pi / NPAD)
     cosine, sine = np.cos(phase), -np.sin(phase)
     rows = np.concatenate([cosine, sine], 0)
-    out = np.block([[cosine, -sine], [sine, cosine]])
-    back = np.block([[cosine.T, sine.T], [-sine.T, cosine.T]])
-    return rows, out, back
+    return rows
 
 
 def halves(x):
@@ -75,7 +75,14 @@
     return tile % 2 == 1, jnp.logical_or(tile == 0, tile == tiles - 1)
 
 
-def analyze_kernel(mask_hbm, rows_hbm, rows_t_hbm, own, even_out, odd_out, rows, rows_t, mask, sems):
+def half_spectrum(z_high, z_low, rows_t, side):
+    r = pl.ds(pl.multiple_of(side * MARGIN, MARGIN), MARGIN)
+    both = dot(jnp.concatenate([z_high, z_low], 0), rows_t[r, :WIDE])
+    w = both[:WIDE] + both[WIDE:] + dot(z_high, rows_t[r, WIDE:])
+    return (w[:BAND] + turn(w[BAND:])) * signs((BAND, WIDE))
+
+
+def analyze_kernel(mask_hbm, rows_hbm, rows_t_hbm, odd_out, rest, rows, rows_t, mask, sems):
     moves = copies([(mask_hbm, mask), (rows_hbm, rows), (rows_t_hbm, rows_t)], sems)
     for move in moves:
         move.wait()
@@ -83,91 +90,76 @@
     high, low = halves(mask[...])
     both = dot(rows[...], high)
     z = both[:WIDE] + both[WIDE:] + dot(rows[:WIDE], low)
-    z_high, z_low = halves(z)
-    z_both = jnp.concatenate([z_high, z_low], 0)
-    sides = []
-    for side in range(2):
-        c = slice(side * MARGIN, (side + 1) * MARGIN)
-        both = dot(z_both[:, c], rows_t[c, :WIDE])
-        w = both[:WIDE] + both[WIDE:] + dot(z_high[:, c], rows_t[c, WIDE:])
-        sides.append(w[:BAND] + turn(w[BAND:]))
-    left, right = sides
-    own[...] = left + right
-    sign = signs(left.shape)
-    left = left * sign
-    right = right * sign
-    even_out[...] = jnp.where(odd, left, right)
-    odd_out[...] = jnp.where(odd, right, left)
+    z_left, z_right = z[:, :MARGIN], z[:, MARGIN:]
+    rest[...] = jnp.where(odd, z_left, z_right)
+    odd_out[...] = half_spectrum(*halves(jnp.where(odd, z_right, z_left)), rows_t, jnp.where(odd, 1, 0))
 
 
 def prepare_kernel(
-    index, weight, dose, after, table_hbm, target_hbm, out_high_hbm, out_low_hbm, back_hbm,
-    mixed, target, out_high, out_low, back, table, sems,
+    rest, odd_out, rows_t, index_hbm, weight_hbm, dose_hbm, table_hbm, target_hbm,
+    even_out, own, mixed, target, table, index, weight, dose, sems,
 ):
     moves = copies(
-        [(table_hbm.at[index[c]], table.at[c]) for c in range(CONDS)]
-        + [
+        [
+            (index_hbm, index),
+            (weight_hbm, weight),
+            (dose_hbm, dose),
+            (table_hbm, table),
             (target_hbm, target),
-            (out_high_hbm, out_high),
-            (out_low_hbm, out_low),
-            (back_hbm, back),
         ],
         sems,
     )
+    odd, _ = place()
+    even = half_spectrum(*halves(rest[...]), rows_t, jnp.where(odd, 0, 1))
+    even_out[...] = even
+    own[...] = (even + odd_out[...]) * signs((BAND, WIDE))
+    for move in moves:
+        move.wait()
     for condition in range(CONDS):
         entry = index[condition]
-        moves[condition].wait()
         for k in range(KERN):
             scale = jnp.sqrt(
                 jnp.full((1, WIDE), 0.5 * steepness * dose[entry] * weight[k, entry])
             ) * (1.0 / (NPAD * NPAD))
             for part in range(2):
-                kernel = table[condition, k, part]
+                kernel = table[entry, k, part]
                 doubled = jnp.concatenate([kernel, kernel], 1)
                 mixed[condition * KERN + k, part] = doubled * scale
-    for move in moves[CONDS:]:
-        move.wait()
-
-
-def window_kernel(
-    own, even_in, odd_in, target, mixed, rows_t, rows, out_high, out_low, back_both,
-    resist, grad,
-):
+
+
+def join_kernel(own, odd_in, joined):
     _, alone = place()
-    spec = own[...] + even_in[...] + jnp.where(alone, 0.0, odd_in[...])
+    joined[...] = own[...] + jnp.where(alone, 0.0, odd_in[...])
+
+
+def window_kernel(joined, even_in, target, mixed, rows_t, rows, resist, grad):
+    spec = joined[...] + even_in[...]
     turned = turn(spec)
     stack = jnp.concatenate(
         [stacked(mixed[i, 0] * spec + mixed[i, 1] * turned) for i in range(PAIRS)], 1
     )
     high, low = halves(stack)
     first = dot(rows_t[...], jnp.concatenate([high, high], 0)) + dot(rows_t[:, :WIDE], low)
-    y_high, y_low = halves(first)
-    out_twice = jnp.concatenate([out_high[...], out_high[...]], 0)
-    half = CORE // 2
-    q_parts = [[None, None] for _ in range(PAIRS)]
+    rows_twice = jnp.concatenate([rows[:WIDE], rows[:WIDE]], 0)
+    q_parts = [[] for _ in range(PAIRS)]
     for condition in range(CONDS):
-        for part in range(2):
-            r = slice(part * half, (part + 1) * half)
-            group = [condition * KERN + k for k in range(KERN)]
-            cols = [slice(i * WIDE, (i + 1) * WIDE) for i in group]
-            a = jnp.concatenate([y_high[r, c] for c in cols], 0)
-            b = jnp.concatenate([y_low[r, c] for c in cols], 0)
-            f = dot(jnp.concatenate([a, b], 1), out_twice) + dot(a, out_low[...])
+        group = [condition * KERN + k for k in range(KERN)]
+        for start in range(0, CORE, CHUNK):
+            r = slice(start, start + CHUNK)
+            y = jnp.concatenate([first[r, i * WIDE : (i + 1) * WIDE] for i in group], 0)
+            y_high, y_low = halves(jnp.concatenate([y, -turn(y)], 0))
+            f = dot(jnp.concatenate([y_high, y_low], 1), rows_twice) + dot(y_high, rows[WIDE:])
             squares = f * f
-            power = sum(
-                squares[k * half : (k + 1) * half, :CORE] + squares[k * half : (k + 1) * half, CORE:]
-                for k in range(KERN)
-            )
+            power = sum(squares[i * CHUNK : (i + 1) * CHUNK] for i in range(2 * KERN))
             t = jnp.tanh(power - 0.5 * steepness * threshold)
             resist[condition, r] = 0.5 + 0.5 * t
             drive = (t + (1.0 - 2.0 * target[r])) * (2.0 - 2.0 * (t * t))
-            drive = jnp.concatenate([drive, drive], 1)
-            scaled = jnp.concatenate([drive] * KERN, 0) * f
-            s_high, s_low = halves(scaled)
-            both = dot(s_high, back_both[...])
-            q = both[:, :WIDE] + both[:, WIDE:] + dot(s_low, back_both[:, :WIDE])
+            s_high, s_low = halves(jnp.concatenate([drive] * (2 * KERN), 0) * f)
+            both = dot(s_high, rows_t[...])
+            u = both[:, :WIDE] + both[:, WIDE:] + dot(s_low, rows_t[:, :WIDE])
+            q = u[: KERN * CHUNK] + turn(u[KERN * CHUNK :])
             for k in range(KERN):
-                q_parts[group[k]][part] = q[k * half : (k + 1) * half]
+                q_parts[group[k]].append(q[k * CHUNK : (k + 1) * CHUNK])
     q = jnp.concatenate([jnp.concatenate(p, 0) for p in q_parts], 1)
     q_high, q_low = halves(q)
     both = dot(rows[...], q_high)
@@ -248,49 +240,43 @@
 
 
 def local(mask, target, kernel_table, kernel_weight, dose_table, condition_index):
-    rows, out, back = tables()
-    rows_table = np.concatenate(parts(rows), 0)
+    rows_table = np.concatenate(parts(tables()), 0)
     rows_t_table = np.ascontiguousarray(rows_table.T)
-    out_high, out_low = parts(out)
-    back_table = np.concatenate(parts(back), 1)
     even, odd = partners(lax.axis_size("win"), lax.axis_size("tile"))
-
-    def swap(x, y):
-        over = ("win", "tile")
-        b = lax.ppermute(y, over, odd)
-        a = lax.ppermute(x, over, even)
-        return a, b
-
+    over = ("win", "tile")
     f32, bf16 = jnp.float32, jnp.bfloat16
     small = ("v", (BAND, WIDE), f32)
     square = (CORE, CORE)
-    dma = pltpu.SemaphoreType.DMA
-    own, to_even, to_odd, rows, rows_t = call(
+    dma, smem = pltpu.SemaphoreType.DMA, pltpu.SMEM
+    to_odd, rest, rows, rows_t = call(
         analyze_kernel,
         "hhh",
-        [small] * 3 + [("v", square, bf16)] * 2,
+        [small, ("v", (WIDE, MARGIN), f32)] + [("v", square, bf16)] * 2,
         [pltpu.VMEM(square, f32), dma((3,))],
     )(*pinned(mask, rows_table, rows_t_table))
-    mixed, goal, out_high, out_low, back = call(
+    from_odd = lax.ppermute(to_odd, over, odd)
+    to_even, own, mixed, goal = call(
         prepare_kernel,
-        "sss" + "v" + "hhhhh",
+        "vvvhhhhh",
+        [small, small, ("v", (PAIRS, 2, BAND, WIDE), f32), ("v", square, f32)],
         [
-            ("v", (PAIRS, 2, BAND, WIDE), f32),
-            ("v", square, f32),
-            ("v", out_high.shape, bf16),
-            ("v", out_low.shape, bf16),
-            ("v", back_table.shape, bf16),
+            pltpu.VMEM((TABLE, KERN, 2, BAND, BAND), f32),
+            smem((CONDS,), jnp.int32),
+            smem((KERN, TABLE), f32),
+            smem((TABLE,), f32),
+            dma((5,)),
         ],
-        [pltpu.VMEM((CONDS, KERN, 2, BAND, BAND), f32), dma((CONDS + 4,))],
     )(
-        condition_index, kernel_weight.T, dose_table, own,
-        *pinned(kernel_table, target, out_high, out_low, back_table),
-    )
-    from_even, from_odd = swap(to_even, to_odd)
+        rest, to_odd, rows_t,
+        *pinned(condition_index, kernel_weight.T, dose_table, kernel_table, target),
+    )
+    from_even = lax.ppermute(to_even, over, even)
+    joined = call(join_kernel, "vv", [small])(own, from_odd)
     resist, grad = call(
-        window_kernel, "v" * 10, [("v", (CONDS, CORE, CORE), f32), small]
-    )(own, from_even, from_odd, goal, mixed, rows_t, rows, out_high, out_low, back)
-    from_even, from_odd = swap(grad, grad)
+        window_kernel, "v" * 6, [("v", (CONDS, CORE, CORE), f32), small]
+    )(joined, from_even, goal, mixed, rows_t, rows)
+    from_odd = lax.ppermute(grad, over, odd)
+    from_even = lax.ppermute(grad, over, even)
     strip = pltpu.VMEM((CORE, MARGIN), f32)
     resist, gradient = call(
         beside_kernel,

time: 16 us -> 15.6 us (0.975)
  waiting for transfers between devices: 1.26 us -> 2.32 us
  Pallas kernels: 8.44 us -> 7.54 us
  local copies, waits for them, and re-layouts: 0.68 us -> 0 us
    ppermute x4, waiting for transfers between devices: 1.26 us -> 2.32 us  [the longest x1 1.27 us: local(): from_odd = lax.ppermute(grad, over, odd)]
    pallas_call x3 -> x4, Pallas kernels: 6.12 us -> 5.22 us  [the longest x1 2.37 us: local(): call(window_kernel, 'v' * 6, [('v', (CONDS, CORE, CORE), f32), small])]
    unnamed x6 -> x0, local copies, waits for them, and re-layouts: 0.68 us -> none
  transfers between devices with their start and end apart: 4 -> 4, of which waited for: 1 -> 3; matrix products, arithmetic and copies ran while one was open for 0% -> 0% of each run, Pallas kernels for 19% -> 16%
where the time goes in v3:
time: 15.6 us; the launch traced here: 15.4 us
  Pallas kernels  7.54 us (48%)
  starting transfers between devices  4.91 us (31%)
  waiting for transfers between devices  2.32 us (15%)
  between operations  0.66 us (4%)
    ppermute x1, starting transfers between devices, local(): from_odd = lax.ppermute(to_odd, over, odd)  3 us
    pallas_call x1, Pallas kernels, local(): call(window_kernel, 'v' * 6, [('v', (CONDS, CORE, CORE), f32), small])  2.37 us
    pallas_call x1, Pallas kernels, local(): call(analyze_kernel, 'hhh', [small, ('v', (WIDE, MARGIN), f32)] + [('v',...  1.54 us
    ppermute x1, starting transfers between devices, local(): from_odd = lax.ppermute(grad, over, odd)  1.47 us
    pallas_call x1, Pallas kernels, local(): call(prepare_kernel, 'vvvhhhhh', [small, small, ('v', (PAIRS, 2, BAND, WI...  1.3 us
    ppermute x1, waiting for transfers between devices, local(): from_odd = lax.ppermute(grad, over, odd)  1.27 us
    pallas_call x1, Pallas kernels, local(): call(beside_kernel, 'v' * 5, [('h', (CONDS, CORE, CORE), f32), ('h', squa...  1.17 us
    pallas_call x1, Pallas kernels, local(): call(across_kernel, 'vvvvh', [('h', square, f32)], [strip, dma((1,))], {4...  1.16 us
  transfers between devices with their start and end apart: 4, of which 3 were waited for; matrix products, arithmetic and copies ran while one was open for 0% of the time, Pallas kernels for 16%

profile of v3, /device:TPU:0, one launch (start us, length us, event | category | flops | bytes accessed | tf_op | source)
XLA Modules:
  0.0 15.4 jit_solution(15898659009145854931)
XLA Ops:
  0.6 1.5 %shard_map.95 = (f32[64,128]{1,0:T(8,128)S(1)}, f32[128,128]{1,0:T(8,128)S(1)}, bf16[256,256]{1,0:T(8,128)(2,1)S(1)}, bf16[256,256]{1,0:T(8,128)(2,1)S(1)}) custom-call(f32[256,256]{1,0:T(8,128)} %mask_hbm.1, bf16[256,256]{1,0:T(8,128)(2,1)} %constant.4.clone.rows_hbm, bf16[256,256]{1,0:T(8,128)(2,1)} %constant.5.clone.rows_t_hbm), custom_call_target="tpu_custom_call" | custom-call | flops 1000000 | bytes 65536 | tf_op jit(solution)/shard_map/pallas_call | solution.py:251
  2.2 3.0 %collective-permute-start = (f32[64,128]{1,0:T(8,128)S(1)}, f32[64,128]{1,0:T(8,128)S(1)}, u32[]{:S(2)}, u32[]{:S(2)}) collective-permute-start(f32[64,128]{1,0:T(8,128)S(1)} %get-tuple-element.15.odd_out), channel_id=1, source_target_pairs={{1,2},{2,1},{3,4},{4,3},{5,6},{6,5},{7,8},{8,7},{9,10},{10,9},{11,... | collective-permute-start | bytes 98312 | tf_op jit(solution)/shard_map/ppermute | solution.py:257
  5.2 1.3 %shard_map.96 = (f32[64,128]{1,0:T(8,128)S(1)}, f32[64,128]{1,0:T(8,128)S(1)}, f32[4,2,64,128]{3,2,1,0:T(8,128)S(1)}, f32[256,256]{1,0:T(8,128)S(1)}) custom-call(f32[128,128]{1,0:T(8,128)S(1)} %get-tuple-element.14.rest, f32[64,128]{1,0:T(8,128)S(1)} %get-tuple-element.15.odd_out, bf16[256,256]{1,0:T(8,128)(2,1)S(1)} %get-tuple-element.16.rows_t, ...), custom_call_target="tpu_custom_call" | custom-call | flops 1000000 | bytes 65536 | tf_op jit(solution)/shard_map/pallas_call | solution.py:258
  6.5 0.2 %collective-permute-start.1 = (f32[64,128]{1,0:T(8,128)S(1)}, f32[64,128]{1,0:T(8,128)S(1)}, u32[]{:S(2)}, u32[]{:S(2)}) collective-permute-start(f32[64,128]{1,0:T(8,128)S(1)} %get-tuple-element.18), channel_id=1, source_target_pairs={{0,1},{1,0},{2,3},{3,2},{4,5},{5,4},{6,7},{7,6},{8,9},{9,8},{10,11... | collective-permute-start | bytes 98312 | tf_op jit(solution)/shard_map/ppermute | solution.py:273
  6.7 0.4 %collective-permute-done.odd_in = f32[64,128]{1,0:T(8,128)S(1)} collective-permute-done((f32[64,128]{1,0:T(8,128)S(1)}, f32[64,128]{1,0:T(8,128)S(1)}, u32[]{:S(2)}, u32[]{:S(2)}) %collective-permute-start) | collective-permute-done | bytes 32800 | tf_op jit(solution)/shard_map/ppermute | solution.py:257
  7.1 0.7 %collective-permute-done.1.even_in = f32[64,128]{1,0:T(8,128)S(1)} collective-permute-done((f32[64,128]{1,0:T(8,128)S(1)}, f32[64,128]{1,0:T(8,128)S(1)}, u32[]{:S(2)}, u32[]{:S(2)}) %collective-permute-start.1) | collective-permute-done | bytes 32800 | tf_op jit(solution)/shard_map/ppermute | solution.py:273
  7.8 2.4 %shard_map.98 = (f32[2,256,256]{2,1,0:T(8,128)S(1)}, f32[64,128]{1,0:T(8,128)S(1)}) custom-call(f32[64,128]{1,0:T(8,128)S(1)} %shard_map.97.joined, f32[64,128]{1,0:T(8,128)S(1)} %collective-permute-done.1.even_in, f32[256,256]{1,0:T(8,128)S(1)} %get-tuple-element.19.target, f32[4,2,64,128]{3,2,1,0:T(8,128)S(1)} %get-tuple-element.20.mixed, ...), custom_call_target="tpu_custom_call" | custom-call | flops 1000000 | bytes 65536 | tf_op jit(solution)/shard_map/pallas_call | solution.py:275
  10.1 0.2 %collective-permute-start.2 = (f32[64,128]{1,0:T(8,128)S(1)}, f32[64,128]{1,0:T(8,128)S(1)}, u32[]{:S(2)}, u32[]{:S(2)}) collective-permute-start(f32[64,128]{1,0:T(8,128)S(1)} %get-tuple-element.22.own), channel_id=1, source_target_pairs={{0,1},{1,0},{2,3},{3,2},{4,5},{5,4},{6,7},{7,6},{8,9},{9,8},{10,11... | collective-permute-start | bytes 98312 | tf_op jit(solution)/shard_map/ppermute | solution.py:279
  10.4 1.5 %collective-permute-start.3 = (f32[64,128]{1,0:T(8,128)S(1)}, f32[64,128]{1,0:T(8,128)S(1)}, u32[]{:S(2)}, u32[]{:S(2)}) collective-permute-start(f32[64,128]{1,0:T(8,128)S(1)} %get-tuple-element.22.own), channel_id=1, source_target_pairs={{1,2},{2,1},{3,4},{4,3},{5,6},{6,5},{7,8},{8,7},{9,10},{10,9},{11,... | collective-permute-start | bytes 98312 | tf_op jit(solution)/shard_map/ppermute | solution.py:278
  11.8 0.0 collective-permute-done.2.even_in
  11.8 1.2 %shard_map.99 = (f32[2,256,256]{2,1,0:T(8,128)}, f32[256,256]{1,0:T(8,128)}) custom-call(f32[64,128]{1,0:T(8,128)S(1)} %get-tuple-element.22.own, f32[64,128]{1,0:T(8,128)S(1)} %collective-permute-done.2.even_in, bf16[256,256]{1,0:T(8,128)(2,1)S(1)} %get-tuple-element.21.rows, bf16[256,256]{1,0:T(8,128)(2,1)S(1)} %get-tuple-element.16.rows_t, ...), custom_call_target="tpu_custom_call" | custom-call | flops 1000000 | bytes 65536 | tf_op jit(solution)/shard_map/pallas_call | solution.py:281
  13.0 1.3 %collective-permute-done.3.odd_in = f32[64,128]{1,0:T(8,128)S(1)} collective-permute-done((f32[64,128]{1,0:T(8,128)S(1)}, f32[64,128]{1,0:T(8,128)S(1)}, u32[]{:S(2)}, u32[]{:S(2)}) %collective-permute-start.3) | collective-permute-done | bytes 32800 | tf_op jit(solution)/shard_map/ppermute | solution.py:278
  14.3 1.2 %shard_map.100 = f32[256,256]{1,0:T(8,128)} custom-call(f32[64,128]{1,0:T(8,128)S(1)} %get-tuple-element.22.own, f32[64,128]{1,0:T(8,128)S(1)} %collective-permute-done.3.odd_in, bf16[256,256]{1,0:T(8,128)(2,1)S(1)} %get-tuple-element.21.rows, bf16[256,256]{1,0:T(8,128)(2,1)S(1)} %get-tuple-element.16.rows_t, ...), custom_call_target="tpu_custom_call", output_to_operand_aliasing={{}: (4, {})} | custom-call | flops 1000000 | bytes 65536 | tf_op jit(solution)/shard_map/pallas_call | solution.py:287
  (1 shorter events, 0.0 us)
Async XLA Ops:
  2.2 4.9 %collective-permute-start = (f32[64,128]{1,0:T(8,128)S(1)}, f32[64,128]{1,0:T(8,128)S(1)}, u32[]{:S(2)}, u32[]{:S(2)}) collective-permute-start(f32[64,128]{1,0:T(8,128)S(1)} %get-tuple-element.15.odd_out), channel_id=1, source_target_pairs={{1,2},{2,1},{3,4},{4,3},{5,6},{6,5},{7,8},{8,7},{9,10},{10,9},{11,... | collective-permute-start | bytes 98312 | tf_op jit(solution)/shard_map/ppermute | solution.py:257
  6.5 1.3 %collective-permute-start.1 = (f32[64,128]{1,0:T(8,128)S(1)}, f32[64,128]{1,0:T(8,128)S(1)}, u32[]{:S(2)}, u32[]{:S(2)}) collective-permute-start(f32[64,128]{1,0:T(8,128)S(1)} %get-tuple-element.18), channel_id=1, source_target_pairs={{0,1},{1,0},{2,3},{3,2},{4,5},{5,4},{6,7},{7,6},{8,9},{9,8},{10,11... | collective-permute-start | bytes 98312 | tf_op jit(solution)/shard_map/ppermute | solution.py:273
  10.1 1.7 %collective-permute-start.2 = (f32[64,128]{1,0:T(8,128)S(1)}, f32[64,128]{1,0:T(8,128)S(1)}, u32[]{:S(2)}, u32[]{:S(2)}) collective-permute-start(f32[64,128]{1,0:T(8,128)S(1)} %get-tuple-element.22.own), channel_id=1, source_target_pairs={{0,1},{1,0},{2,3},{3,2},{4,5},{5,4},{6,7},{7,6},{8,9},{9,8},{10,11... | collective-permute-start | bytes 98312 | tf_op jit(solution)/shard_map/ppermute | solution.py:279
  10.4 3.9 %collective-permute-start.3 = (f32[64,128]{1,0:T(8,128)S(1)}, f32[64,128]{1,0:T(8,128)S(1)}, u32[]{:S(2)}, u32[]{:S(2)}) collective-permute-start(f32[64,128]{1,0:T(8,128)S(1)} %get-tuple-element.22.own), channel_id=1, source_target_pairs={{1,2},{2,1},{3,4},{4,3},{5,6},{6,5},{7,8},{8,7},{9,10},{10,9},{11,... | collective-permute-start | bytes 98312 | tf_op jit(solution)/shard_map/ppermute | solution.py:278

commit v4 on v3

--- a/solution.py
+++ b/solution.py
@@ -14,11 +14,14 @@
 BAND = 64
 KERN = 2
 TABLE = 4
+TABLES = 7
 CONDS = 2
 CORE = 256
 PAIRS = CONDS * KERN
 WIDE = 2 * BAND
-CHUNK = 64
+CHUNK = 128
+COARSE = 2 * BAND
+STEP = NPAD // COARSE
 
 steepness = 6.0
 threshold = 0.3
@@ -30,13 +33,22 @@
     return high, low
 
 
-def tables():
+def waves(positions):
     frequency = np.arange(BAND)[:, None] - BAND // 2
-    position = np.arange(MARGIN, MARGIN + CORE)[None, :]
-    phase = (frequency * position % NPAD) * (2.0 * math.pi / NPAD)
-    cosine, sine = np.cos(phase), -np.sin(phase)
-    rows = np.concatenate([cosine, sine], 0)
-    return rows
+    phase = (frequency * positions[None, :] % NPAD) * (2.0 * math.pi / NPAD)
+    return np.concatenate([np.cos(phase), -np.sin(phase)], 0)
+
+
+def interpolation():
+    apart = np.arange(MARGIN, MARGIN + CORE)[:, None] - STEP * np.arange(COARSE)[None, :]
+    frequency = np.arange(1, COARSE // 2)[:, None, None]
+    total = 1.0 + 2.0 * np.cos((frequency * apart % NPAD) * (2.0 * math.pi / NPAD)).sum(0)
+    total = total + np.cos((COARSE // 2 * apart % NPAD) * (2.0 * math.pi / NPAD))
+    return total / COARSE
+
+
+def side_by_side(table):
+    return np.concatenate(parts(table), 1)
 
 
 def halves(x):
@@ -95,10 +107,19 @@
     odd_out[...] = half_spectrum(*halves(jnp.where(odd, z_right, z_left)), rows_t, jnp.where(odd, 1, 0))
 
 
+def own_kernel(rest, odd_out, rows_t, even_out, own):
+    odd, _ = place()
+    even = half_spectrum(*halves(rest[...]), rows_t, jnp.where(odd, 0, 1))
+    even_out[...] = even
+    own[...] = (even + odd_out[...]) * signs((BAND, WIDE))
+
+
 def prepare_kernel(
-    rest, odd_out, rows_t, index_hbm, weight_hbm, dose_hbm, table_hbm, target_hbm,
-    even_out, own, mixed, target, table, index, weight, dose, sems,
+    after, index_hbm, weight_hbm, dose_hbm, table_hbm, target_hbm, *refs
 ):
+    hbm, refs = refs[:TABLES], refs[TABLES:]
+    mixed, goal, tables = refs[0], refs[1], refs[2 : 2 + TABLES]
+    target, table, index, weight, dose, sems = refs[2 + TABLES :]
     moves = copies(
         [
             (index_hbm, index),
@@ -106,13 +127,10 @@
             (dose_hbm, dose),
             (table_hbm, table),
             (target_hbm, target),
+            *zip(hbm, tables),
         ],
         sems,
     )
-    odd, _ = place()
-    even = half_spectrum(*halves(rest[...]), rows_t, jnp.where(odd, 0, 1))
-    even_out[...] = even
-    own[...] = (even + odd_out[...]) * signs((BAND, WIDE))
     for move in moves:
         move.wait()
     for condition in range(CONDS):
@@ -125,6 +143,7 @@
                 kernel = table[entry, k, part]
                 doubled = jnp.concatenate([kernel, kernel], 1)
                 mixed[condition * KERN + k, part] = doubled * scale
+    goal[...] = 1.0 - 2.0 * target[...]
 
 
 def join_kernel(own, odd_in, joined):
@@ -132,44 +151,87 @@
     joined[...] = own[...] + jnp.where(alone, 0.0, odd_in[...])
 
 
-def window_kernel(joined, even_in, target, mixed, rows_t, rows, resist, grad):
+def window_kernel(
+    joined, even_in, goal, mixed, points, points_t, out_high, out_low, back_both, finer, finer_t,
+    resist, grad,
+):
     spec = joined[...] + even_in[...]
     turned = turn(spec)
-    stack = jnp.concatenate(
-        [stacked(mixed[i, 0] * spec + mixed[i, 1] * turned) for i in range(PAIRS)], 1
-    )
-    high, low = halves(stack)
-    first = dot(rows_t[...], jnp.concatenate([high, high], 0)) + dot(rows_t[:, :WIDE], low)
-    rows_twice = jnp.concatenate([rows[:WIDE], rows[:WIDE]], 0)
-    q_parts = [[] for _ in range(PAIRS)]
-    for condition in range(CONDS):
-        group = [condition * KERN + k for k in range(KERN)]
-        for start in range(0, CORE, CHUNK):
-            r = slice(start, start + CHUNK)
-            y = jnp.concatenate([first[r, i * WIDE : (i + 1) * WIDE] for i in group], 0)
-            y_high, y_low = halves(jnp.concatenate([y, -turn(y)], 0))
-            f = dot(jnp.concatenate([y_high, y_low], 1), rows_twice) + dot(y_high, rows[WIDE:])
-            squares = f * f
-            power = sum(squares[i * CHUNK : (i + 1) * CHUNK] for i in range(2 * KERN))
-            t = jnp.tanh(power - 0.5 * steepness * threshold)
-            resist[condition, r] = 0.5 + 0.5 * t
-            drive = (t + (1.0 - 2.0 * target[r])) * (2.0 - 2.0 * (t * t))
-            s_high, s_low = halves(jnp.concatenate([drive] * (2 * KERN), 0) * f)
-            both = dot(s_high, rows_t[...])
-            u = both[:, :WIDE] + both[:, WIDE:] + dot(s_low, rows_t[:, :WIDE])
-            q = u[: KERN * CHUNK] + turn(u[KERN * CHUNK :])
-            for k in range(KERN):
-                q_parts[group[k]].append(q[k * CHUNK : (k + 1) * CHUNK])
-    q = jnp.concatenate([jnp.concatenate(p, 0) for p in q_parts], 1)
-    q_high, q_low = halves(q)
-    both = dot(rows[...], q_high)
-    u = both[:WIDE] + both[WIDE:] + dot(rows[:WIDE], q_low)
-    total = jnp.zeros((BAND, WIDE), jnp.float32)
+    out_twice = jnp.concatenate([out_high[...], out_high[...]], 0)
+    finer_twice = jnp.concatenate([finer_t[:COARSE], finer_t[:COARSE]], 0)
+    conditions = range(CONDS)
+
+    def coarse_rows(condition):
+        group = range(condition * KERN, (condition + 1) * KERN)
+        top = jnp.concatenate([mixed[i, 0] * spec + mixed[i, 1] * turned for i in group], 1)
+        bottom = jnp.concatenate([mixed[i, 1] * spec - mixed[i, 0] * turned for i in group], 1)
+        high, low = halves(jnp.concatenate([top, bottom], 0))
+        return dot(points_t[...], jnp.concatenate([high, high], 0)) + dot(points_t[:, :WIDE], low)
+
+    def coarse_field(y):
+        y = jnp.concatenate([y[:, k * WIDE : (k + 1) * WIDE] for k in range(KERN)], 0)
+        high, low = halves(y)
+        return dot(jnp.concatenate([high, low], 1), out_twice) + dot(high, out_low[...])
+
+    def finer_rows(f):
+        squares = f * f
+        power = sum(
+            squares[k * COARSE : (k + 1) * COARSE, c]
+            for k in range(KERN)
+            for c in (slice(0, COARSE), slice(COARSE, 2 * COARSE))
+        )
+        high, low = halves(power - 0.5 * steepness * threshold)
+        return dot(finer[...], jnp.concatenate([high, high], 0)) + dot(finer[:, :COARSE], low)
+
+    def finer_columns(z):
+        z_high, z_low = halves(z)
+        return dot(jnp.concatenate([z_high, z_low], 1), finer_twice) + dot(z_high, finer_t[COARSE:])
+
+    def print_and_drive(condition, r, power):
+        t = jnp.tanh(power)
+        resist[condition, r] = 0.5 + 0.5 * t
+        return (t + goal[r]) * (1.0 - t * t)
+
+    def coarser_columns(drive):
+        high, low = halves(drive)
+        both = dot(high, finer[...])
+        return both[:, :COARSE] + both[:, COARSE:] + dot(low, finer[:, :COARSE])
+
+    def coarser_rows(w):
+        high, low = halves(w)
+        both = dot(finer_t[...], high)
+        return both[:COARSE] + both[COARSE:] + dot(finer_t[:COARSE], low)
+
+    def back_columns(drive, f):
+        drive = jnp.concatenate([drive, drive], 1)
+        high, low = halves(jnp.concatenate([drive] * KERN, 0) * f)
+        both = dot(high, back_both[...])
+        q = both[:, :WIDE] + both[:, WIDE:] + dot(low, back_both[:, :WIDE])
+        return jnp.concatenate([q[k * COARSE : (k + 1) * COARSE] for k in range(KERN)], 1)
+
+    def back_rows(q):
+        high, low = halves(q)
+        return dot(points[...], jnp.concatenate([high, high], 0)) + dot(points[:, :COARSE], low)
+
+    y = [coarse_rows(c) for c in conditions]
+    fields = [coarse_field(x) for x in y]
+    z = [finer_rows(f) for f in fields]
+    pieces = [slice(start, start + CHUNK) for start in range(0, CORE, CHUNK)]
+    power = [[finer_columns(z[c][r]) for c in conditions] for r in pieces]
+    drive = [[print_and_drive(c, r, p[c]) for c in conditions] for r, p in zip(pieces, power)]
+    w = [[coarser_columns(d[c]) for c in conditions] for d in drive]
+    w = [jnp.concatenate([x[c] for x in w], 0) for c in conditions]
+    drive = [coarser_rows(x) for x in w]
+    q = [back_columns(drive[c], fields[c]) for c in conditions]
+    u = [back_rows(x) for x in q]
+    straight = jnp.zeros((BAND, WIDE), jnp.float32)
+    crossed = jnp.zeros((BAND, WIDE), jnp.float32)
     for i in range(PAIRS):
-        c = slice(i * WIDE, (i + 1) * WIDE)
-        back = u[:BAND, c] + turn(u[BAND:, c])
-        total = total + mixed[i, 0] * back - mixed[i, 1] * turn(back)
-    grad[...] = total
+        c = slice(i % KERN * WIDE, (i % KERN + 1) * WIDE)
+        top, bottom = u[i // KERN][:BAND, c], u[i // KERN][BAND:, c]
+        straight = straight + (mixed[i, 0] * top + mixed[i, 1] * bottom)
+        crossed = crossed + (mixed[i, 0] * bottom - mixed[i, 1] * top)
+    grad[...] = 2.0 * (straight + turn(crossed))
 
 
 def synthesize(spec, rows, rows_t, side, out):
@@ -240,8 +302,17 @@
 
 
 def local(mask, target, kernel_table, kernel_weight, dose_table, condition_index):
-    rows_table = np.concatenate(parts(tables()), 0)
+    rows_table = np.concatenate(parts(waves(np.arange(MARGIN, MARGIN + CORE))), 0)
     rows_t_table = np.ascontiguousarray(rows_table.T)
+    points = waves(STEP * np.arange(COARSE))
+    cosine, sine = points[:BAND], points[BAND:]
+    out = np.block([[cosine, -sine], [sine, cosine]])
+    back = np.block([[cosine.T, sine.T], [-sine.T, cosine.T]])
+    finer = side_by_side(interpolation())
+    coarse_tables = (
+        side_by_side(points), side_by_side(points.T), *parts(out), side_by_side(back),
+        finer, np.ascontiguousarray(finer.T),
+    )
     even, odd = partners(lax.axis_size("win"), lax.axis_size("tile"))
     over = ("win", "tile")
     f32, bf16 = jnp.float32, jnp.bfloat16
@@ -255,26 +326,29 @@
         [pltpu.VMEM(square, f32), dma((3,))],
     )(*pinned(mask, rows_table, rows_t_table))
     from_odd = lax.ppermute(to_odd, over, odd)
-    to_even, own, mixed, goal = call(
+    to_even, own = call(own_kernel, "vvv", [small, small])(rest, to_odd, rows_t)
+    from_even = lax.ppermute(to_even, over, even)
+    mixed, goal, *coarse = call(
         prepare_kernel,
-        "vvvhhhhh",
-        [small, small, ("v", (PAIRS, 2, BAND, WIDE), f32), ("v", square, f32)],
+        "v" + "h" * (5 + TABLES),
+        [("v", (PAIRS, 2, BAND, WIDE), f32), ("v", square, f32)]
+        + [("v", table.shape, bf16) for table in coarse_tables],
         [
+            pltpu.VMEM(square, f32),
             pltpu.VMEM((TABLE, KERN, 2, BAND, BAND), f32),
             smem((CONDS,), jnp.int32),
             smem((KERN, TABLE), f32),
             smem((TABLE,), f32),
-            dma((5,)),
+            dma((5 + TABLES,)),
         ],
     )(
-        rest, to_odd, rows_t,
-        *pinned(condition_index, kernel_weight.T, dose_table, kernel_table, target),
-    )
-    from_even = lax.ppermute(to_even, over, even)
+        own,
+        *pinned(condition_index, kernel_weight.T, dose_table, kernel_table, target, *coarse_tables),
+    )
     joined = call(join_kernel, "vv", [small])(own, from_odd)
     resist, grad = call(
-        window_kernel, "v" * 6, [("v", (CONDS, CORE, CORE), f32), small]
-    )(joined, from_even, goal, mixed, rows_t, rows)
+        window_kernel, "v" * (4 + TABLES), [("v", (CONDS, CORE, CORE), f32), small]
+    )(joined, from_even, goal, mixed, *coarse)
     from_odd = lax.ppermute(grad, over, odd)
     from_even = lax.ppermute(grad, over, even)
     strip = pltpu.VMEM((CORE, MARGIN), f32)

time: 15.6 us -> 14.8 us (0.949)
  waiting for transfers between devices: 2.32 us -> 1.17 us
  starting transfers between devices: 4.91 us -> 5.22 us
    ppermute x1, waiting for transfers between devices: 0.68 us -> 0.01 us  [local(): from_even = lax.ppermute(to_even, over, even)]
    ppermute x1, waiting for transfers between devices: 0.38 us -> 0.01 us  [local(): from_odd = lax.ppermute(to_odd, over, odd)]
    ppermute x1, starting transfers between devices: 0.22 us -> 0.43 us  [local(): from_even = lax.ppermute(grad, over, even)]
    pallas_call x2 -> x3, Pallas kernels: 3.67 us -> 3.67 us  [the longest x1 1.86 us: local(): call(window_kernel, 'v' * (4 + TABLES), [('v', (CONDS, CORE, CORE), f32),...]
  transfers between devices with their start and end apart: 4 -> 4, of which waited for: 3 -> 1; matrix products, arithmetic and copies ran while one was open for 0% -> 0% of each run, Pallas kernels for 16% -> 20%
where the time goes in v4:
time: 14.8 us; the launch traced here: 14.6 us
  Pallas kernels  7.54 us (51%)
  starting transfers between devices  5.22 us (35%)
  waiting for transfers between devices  1.17 us (8%)
  between operations  0.69 us (5%)
    ppermute x1, starting transfers between devices, local(): from_odd = lax.ppermute(to_odd, over, odd)  3 us
    pallas_call x1, Pallas kernels, local(): call(window_kernel, 'v' * (4 + TABLES), [('v', (CONDS, CORE, CORE), f32),...  1.86 us
    ppermute x1, starting transfers between devices, local(): from_odd = lax.ppermute(grad, over, odd)  1.57 us
    pallas_call x1, Pallas kernels, local(): call(prepare_kernel, 'v' + 'h' * (5 + TABLES), [('v', (PAIRS, 2, BAND, WI...  1.55 us
    pallas_call x1, Pallas kernels, local(): call(analyze_kernel, 'hhh', [small, ('v', (WIDE, MARGIN), f32)] + [('v',...  1.54 us
    ppermute x1, waiting for transfers between devices, local(): from_odd = lax.ppermute(grad, over, odd)  1.17 us
    pallas_call x1, Pallas kernels, local(): call(beside_kernel, 'v' * 5, [('h', (CONDS, CORE, CORE), f32), ('h', squa...  1.17 us
    pallas_call x1, Pallas kernels, local(): call(across_kernel, 'vvvvh', [('h', square, f32)], [strip, dma((1,))], {4...  1.15 us
  transfers between devices with their start and end apart: 4, of which 1 were waited for; matrix products, arithmetic and copies ran while one was open for 0% of the time, Pallas kernels for 20%

profile of v4, /device:TPU:0, one launch (start us, length us, event | category | flops | bytes accessed | tf_op | source)
XLA Modules:
  0.0 14.6 jit_solution(4290424915385708395)
XLA Ops:
  0.6 1.5 %shard_map.158 = (f32[64,128]{1,0:T(8,128)S(1)}, f32[128,128]{1,0:T(8,128)S(1)}, bf16[256,256]{1,0:T(8,128)(2,1)S(1)}, bf16[256,256]{1,0:T(8,128)(2,1)S(1)}) custom-call(f32[256,256]{1,0:T(8,128)} %mask_hbm.1, bf16[256,256]{1,0:T(8,128)(2,1)} %constant.18.clone.rows_hbm, bf16[256,256]{1,0:T(8,128)(2,1)} %constant.19.clone.rows_t_hbm), custom_call_target="tpu_custom_call" | custom-call | flops 1000000 | bytes 65536 | tf_op jit(solution)/shard_map/pallas_call | solution.py:322
  2.2 3.0 %collective-permute-start = (f32[64,128]{1,0:T(8,128)S(1)}, f32[64,128]{1,0:T(8,128)S(1)}, u32[]{:S(2)}, u32[]{:S(2)}) collective-permute-start(f32[64,128]{1,0:T(8,128)S(1)} %get-tuple-element.22.odd_out), channel_id=1, source_target_pairs={{1,2},{2,1},{3,4},{4,3},{5,6},{6,5},{7,8},{8,7},{9,10},{10,9},{11,... | collective-permute-start | bytes 98312 | tf_op jit(solution)/shard_map/ppermute | solution.py:328
  5.2 0.3 %shard_map.159 = (f32[64,128]{1,0:T(8,128)S(1)}, f32[64,128]{1,0:T(8,128)S(1)}) custom-call(f32[128,128]{1,0:T(8,128)S(1)} %get-tuple-element.21.rest, f32[64,128]{1,0:T(8,128)S(1)} %get-tuple-element.22.odd_out, bf16[256,256]{1,0:T(8,128)(2,1)S(1)} %get-tuple-element.23.rows_t), custom_call_target="tpu_custom_call" | custom-call | flops 1000000 | bytes 65536 | tf_op jit(solution)/shard_map/pallas_call | solution.py:329
  5.4 0.2 %collective-permute-start.1 = (f32[64,128]{1,0:T(8,128)S(1)}, f32[64,128]{1,0:T(8,128)S(1)}, u32[]{:S(2)}, u32[]{:S(2)}) collective-permute-start(f32[64,128]{1,0:T(8,128)S(1)} %get-tuple-element.25), channel_id=1, source_target_pairs={{0,1},{1,0},{2,3},{3,2},{4,5},{5,4},{6,7},{7,6},{8,9},{9,8},{10,11... | collective-permute-start | bytes 98312 | tf_op jit(solution)/shard_map/ppermute | solution.py:330
  5.6 1.6 %shard_map.161 = (f32[4,2,64,128]{3,2,1,0:T(8,128)S(1)}, f32[256,256]{1,0:T(8,128)S(1)}, bf16[128,256]{1,0:T(8,128)(2,1)S(1)}, bf16[128,256]{1,0:T(8,128)(2,1)S(...) custom-call(f32[64,128]{1,0:T(8,128)S(1)} %get-tuple-element.24.own., ...), custom_call_target="tpu_custom_call" | custom-call | flops 1000000 | bytes 65536 | tf_op jit(solution)/shard_map/pallas_call | solution.py:331
  7.2 0.0 collective-permute-done.odd_in
  7.2 0.0 collective-permute-done.1.even_in
  7.3 1.9 %shard_map.162 = (f32[2,256,256]{2,1,0:T(8,128)S(1)}, f32[64,128]{1,0:T(8,128)S(1)}) custom-call(f32[64,128]{1,0:T(8,128)S(1)} %shard_map.160.joined, f32[64,128]{1,0:T(8,128)S(1)} %collective-permute-done.1.even_in, f32[256,256]{1,0:T(8,128)S(1)} %get-tuple-element.26.goal, f32[4,2,64,128]{3,2,1,0:T(8,128)S(1)} %get-tuple-element.27.mixed, ...), custom_call_target="tpu_custom_call" | custom-call | flops 1000000 | bytes 65536 | tf_op jit(solution)/shard_map/pallas_call | solution.py:349
  9.1 0.4 %collective-permute-start.2 = (f32[64,128]{1,0:T(8,128)S(1)}, f32[64,128]{1,0:T(8,128)S(1)}, u32[]{:S(2)}, u32[]{:S(2)}) collective-permute-start(f32[64,128]{1,0:T(8,128)S(1)} %get-tuple-element.35.own), channel_id=1, source_target_pairs={{0,1},{1,0},{2,3},{3,2},{4,5},{5,4},{6,7},{7,6},{8,9},{9,8},{10,11... | collective-permute-start | bytes 98312 | tf_op jit(solution)/shard_map/ppermute | solution.py:353
  9.6 1.6 %collective-permute-start.3 = (f32[64,128]{1,0:T(8,128)S(1)}, f32[64,128]{1,0:T(8,128)S(1)}, u32[]{:S(2)}, u32[]{:S(2)}) collective-permute-start(f32[64,128]{1,0:T(8,128)S(1)} %get-tuple-element.35.own), channel_id=1, source_target_pairs={{1,2},{2,1},{3,4},{4,3},{5,6},{6,5},{7,8},{8,7},{9,10},{10,9},{11,... | collective-permute-start | bytes 98312 | tf_op jit(solution)/shard_map/ppermute | solution.py:352
  11.1 0.0 collective-permute-done.2.even_in
  11.1 1.2 %shard_map.163 = (f32[2,256,256]{2,1,0:T(8,128)}, f32[256,256]{1,0:T(8,128)}) custom-call(f32[64,128]{1,0:T(8,128)S(1)} %get-tuple-element.35.own, f32[64,128]{1,0:T(8,128)S(1)} %collective-permute-done.2.even_in, bf16[256,256]{1,0:T(8,128)(2,1)S(1)} %get-tuple-element.36.rows, bf16[256,256]{1,0:T(8,128)(2,1)S(1)} %get-tuple-element.23.rows_t, ...), custom_call_target="tpu_custom_call" | custom-call | flops 1000000 | bytes 65536 | tf_op jit(solution)/shard_map/pallas_call | solution.py:355
  12.3 1.2 %collective-permute-done.3.odd_in = f32[64,128]{1,0:T(8,128)S(1)} collective-permute-done((f32[64,128]{1,0:T(8,128)S(1)}, f32[64,128]{1,0:T(8,128)S(1)}, u32[]{:S(2)}, u32[]{:S(2)}) %collective-permute-start.3) | collective-permute-done | bytes 32800 | tf_op jit(solution)/shard_map/ppermute | solution.py:352
  13.5 1.2 %shard_map.164 = f32[256,256]{1,0:T(8,128)} custom-call(f32[64,128]{1,0:T(8,128)S(1)} %get-tuple-element.35.own, f32[64,128]{1,0:T(8,128)S(1)} %collective-permute-done.3.odd_in, bf16[256,256]{1,0:T(8,128)(2,1)S(1)} %get-tuple-element.36.rows, bf16[256,256]{1,0:T(8,128)(2,1)S(1)} %get-tuple-element.23.rows_t, ...), custom_call_target="tpu_custom_call", output_to_operand_aliasing={{}: (4, {})} | custom-call | flops 1000000 | bytes 65536 | tf_op jit(solution)/shard_map/pallas_call | solution.py:361
  (1 shorter events, 0.0 us)
Async XLA Ops:
  2.2 5.0 %collective-permute-start = (f32[64,128]{1,0:T(8,128)S(1)}, f32[64,128]{1,0:T(8,128)S(1)}, u32[]{:S(2)}, u32[]{:S(2)}) collective-permute-start(f32[64,128]{1,0:T(8,128)S(1)} %get-tuple-element.22.odd_out), channel_id=1, source_target_pairs={{1,2},{2,1},{3,4},{4,3},{5,6},{6,5},{7,8},{8,7},{9,10},{10,9},{11,... | collective-permute-start | bytes 98312 | tf_op jit(solution)/shard_map/ppermute | solution.py:328
  5.4 1.8 %collective-permute-start.1 = (f32[64,128]{1,0:T(8,128)S(1)}, f32[64,128]{1,0:T(8,128)S(1)}, u32[]{:S(2)}, u32[]{:S(2)}) collective-permute-start(f32[64,128]{1,0:T(8,128)S(1)} %get-tuple-element.25), channel_id=1, source_target_pairs={{0,1},{1,0},{2,3},{3,2},{4,5},{5,4},{6,7},{7,6},{8,9},{9,8},{10,11... | collective-permute-start | bytes 98312 | tf_op jit(solution)/shard_map/ppermute | solution.py:330
  9.1 2.0 %collective-permute-start.2 = (f32[64,128]{1,0:T(8,128)S(1)}, f32[64,128]{1,0:T(8,128)S(1)}, u32[]{:S(2)}, u32[]{:S(2)}) collective-permute-start(f32[64,128]{1,0:T(8,128)S(1)} %get-tuple-element.35.own), channel_id=1, source_target_pairs={{0,1},{1,0},{2,3},{3,2},{4,5},{5,4},{6,7},{7,6},{8,9},{9,8},{10,11... | collective-permute-start | bytes 98312 | tf_op jit(solution)/shard_map/ppermute | solution.py:353
  9.6 3.9 %collective-permute-start.3 = (f32[64,128]{1,0:T(8,128)S(1)}, f32[64,128]{1,0:T(8,128)S(1)}, u32[]{:S(2)}, u32[]{:S(2)}) collective-permute-start(f32[64,128]{1,0:T(8,128)S(1)} %get-tuple-element.35.own), channel_id=1, source_target_pairs={{1,2},{2,1},{3,4},{4,3},{5,6},{6,5},{7,8},{8,7},{9,10},{10,9},{11,... | collective-permute-start | bytes 98312 | tf_op jit(solution)/shard_map/ppermute | solution.py:352

commit v5 on v4

--- a/solution.py
+++ b/solution.py
@@ -14,12 +14,13 @@
 BAND = 64
 KERN = 2
 TABLE = 4
-TABLES = 7
+TSPLIT = 2
+CSPLIT = 3
 CONDS = 2
 CORE = 256
 PAIRS = CONDS * KERN
 WIDE = 2 * BAND
-CHUNK = 128
+CHUNK = 256
 COARSE = 2 * BAND
 STEP = NPAD // COARSE
 
@@ -51,6 +52,22 @@
     return np.concatenate(parts(table), 1)
 
 
+def later_tables(rows_table):
+    points = waves(STEP * np.arange(COARSE))
+    cosine, sine = points[:BAND], points[BAND:]
+    out = np.block([[cosine, -sine], [sine, cosine]])
+    back = np.block([[cosine.T, sine.T], [-sine.T, cosine.T]])
+    finer = side_by_side(interpolation())
+    return np.concatenate(
+        [side_by_side(points), side_by_side(points.T), *parts(out), side_by_side(back), finer, finer.T, rows_table.T]
+    )
+
+
+def table_parts(tables):
+    ends = np.cumsum([WIDE, COARSE, WIDE, WIDE, 2 * COARSE, CORE, CORE, CORE])
+    return [tables.at[int(end - size) : int(end)] for end, size in zip(ends, np.diff(ends, prepend=0))]
+
+
 def halves(x):
     high = x.astype(jnp.bfloat16)
     return high, (x - high.astype(jnp.float32)).astype(jnp.bfloat16)
@@ -73,6 +90,13 @@
 
 def stacked(x):
     return jnp.concatenate([x, -turn(x)], 0)
+
+
+def strips(source, target, rows):
+    return [
+        (source.at[start : start + rows], target.at[start : start + rows])
+        for start in range(0, source.shape[0], rows)
+    ]
 
 
 def copies(pairs, sems):
@@ -87,16 +111,21 @@
     return tile % 2 == 1, jnp.logical_or(tile == 0, tile == tiles - 1)
 
 
-def half_spectrum(z_high, z_low, rows_t, side):
-    r = pl.ds(pl.multiple_of(side * MARGIN, MARGIN), MARGIN)
-    both = dot(jnp.concatenate([z_high, z_low], 0), rows_t[r, :WIDE])
-    w = both[:WIDE] + both[WIDE:] + dot(z_high, rows_t[r, WIDE:])
+def across_lanes(a, b):
+    return lax.dot_general(a, b, (((1,), (1,)), ((), ())), preferred_element_type=jnp.float32)
+
+
+def half_spectrum(z, rows, side):
+    columns = rows[:, pl.ds(pl.multiple_of(side * MARGIN, MARGIN), MARGIN)]
+    both = across_lanes(
+        jnp.concatenate(halves(z), 1), jnp.concatenate([columns, columns], 1)
+    )
+    w = both[:, :WIDE] + both[:, WIDE:]
     return (w[:BAND] + turn(w[BAND:])) * signs((BAND, WIDE))
 
 
-def analyze_kernel(mask_hbm, rows_hbm, rows_t_hbm, odd_out, rest, rows, rows_t, mask, sems):
-    moves = copies([(mask_hbm, mask), (rows_hbm, rows), (rows_t_hbm, rows_t)], sems)
-    for move in moves:
+def analyze_kernel(mask_hbm, rows_hbm, odd_out, rest, rows, mask, sems):
+    for move in copies([(mask_hbm, mask), (rows_hbm, rows)], sems):
         move.wait()
     odd, _ = place()
     high, low = halves(mask[...])
@@ -104,30 +133,28 @@
     z = both[:WIDE] + both[WIDE:] + dot(rows[:WIDE], low)
     z_left, z_right = z[:, :MARGIN], z[:, MARGIN:]
     rest[...] = jnp.where(odd, z_left, z_right)
-    odd_out[...] = half_spectrum(*halves(jnp.where(odd, z_right, z_left)), rows_t, jnp.where(odd, 1, 0))
-
-
-def own_kernel(rest, odd_out, rows_t, even_out, own):
+    odd_out[...] = half_spectrum(jnp.where(odd, z_right, z_left), rows, jnp.where(odd, 1, 0))
+
+
+def own_kernel(rest, odd_out, rows, even_out, own):
     odd, _ = place()
-    even = half_spectrum(*halves(rest[...]), rows_t, jnp.where(odd, 0, 1))
+    even = half_spectrum(rest[...], rows, jnp.where(odd, 0, 1))
     even_out[...] = even
     own[...] = (even + odd_out[...]) * signs((BAND, WIDE))
 
 
 def prepare_kernel(
-    after, index_hbm, weight_hbm, dose_hbm, table_hbm, target_hbm, *refs
+    after, index_hbm, weight_hbm, dose_hbm, table_hbm, target_hbm, tables_hbm,
+    mixed, goal, tables, target, table, index, weight, dose, sems,
 ):
-    hbm, refs = refs[:TABLES], refs[TABLES:]
-    mixed, goal, tables = refs[0], refs[1], refs[2 : 2 + TABLES]
-    target, table, index, weight, dose, sems = refs[2 + TABLES :]
     moves = copies(
         [
             (index_hbm, index),
             (weight_hbm, weight),
             (dose_hbm, dose),
-            (table_hbm, table),
+            *strips(table_hbm, table, TABLE // TSPLIT),
             (target_hbm, target),
-            *zip(hbm, tables),
+            *strips(tables_hbm, tables, tables.shape[0] // CSPLIT),
         ],
         sems,
     )
@@ -151,10 +178,8 @@
     joined[...] = own[...] + jnp.where(alone, 0.0, odd_in[...])
 
 
-def window_kernel(
-    joined, even_in, goal, mixed, points, points_t, out_high, out_low, back_both, finer, finer_t,
-    resist, grad,
-):
+def window_kernel(joined, even_in, goal, mixed, tables, resist, grad):
+    points, points_t, out_high, out_low, back_both, finer, finer_t, _ = table_parts(tables)
     spec = joined[...] + even_in[...]
     turned = turn(spec)
     out_twice = jnp.concatenate([out_high[...], out_high[...]], 0)
@@ -181,7 +206,9 @@
             for c in (slice(0, COARSE), slice(COARSE, 2 * COARSE))
         )
         high, low = halves(power - 0.5 * steepness * threshold)
-        return dot(finer[...], jnp.concatenate([high, high], 0)) + dot(finer[:, :COARSE], low)
+        both = jnp.concatenate([high, low], 1)
+        both = dot(finer[...], jnp.concatenate([both, both], 0))
+        return both[:, :COARSE] + both[:, COARSE:]
 
     def finer_columns(z):
         z_high, z_low = halves(z)
@@ -199,8 +226,8 @@
 
     def coarser_rows(w):
         high, low = halves(w)
-        both = dot(finer_t[...], high)
-        return both[:COARSE] + both[COARSE:] + dot(finer_t[:COARSE], low)
+        both = dot(finer_t[:COARSE], jnp.concatenate([high, low], 1))
+        return both[:, :COARSE] + both[:, COARSE:] + dot(finer_t[COARSE:], high)
 
     def back_columns(drive, f):
         drive = jnp.concatenate([drive, drive], 1)
@@ -235,15 +262,17 @@
 
 
 def synthesize(spec, rows, rows_t, side, out):
-    high, low = halves(stacked(spec))
-    y = dot(rows_t[...], jnp.concatenate([high, high], 0)) + dot(rows_t[:, :WIDE], low)
-    y_high, y_low = halves(y)
+    both = jnp.concatenate(halves(stacked(spec)), 1)
+    y = dot(rows_t[...], jnp.concatenate([both, both], 0))
+    y = jnp.concatenate(halves(y[:, :WIDE] + y[:, WIDE:]), 1)
     c = pl.ds(pl.multiple_of(side * MARGIN, MARGIN), MARGIN)
-    both = dot(jnp.concatenate([y_high, y_low], 0), rows[:WIDE, c])
-    out[...] = both[:CORE] + both[CORE:] + dot(y_high, rows[WIDE:, c])
-
-
-def beside_kernel(own, even_in, rows, rows_t, resist, resist_hbm, gradient_hbm, out, sems):
+    columns = jnp.concatenate([rows[:WIDE, c], rows[WIDE:, c]], 1)
+    both = dot(y, jnp.concatenate([columns, columns], 0))
+    out[...] = both[:, :MARGIN] + both[:, MARGIN:]
+
+
+def beside_kernel(own, even_in, rows, tables, resist, resist_hbm, gradient_hbm, out, sems):
+    rows_t = table_parts(tables)[-1]
     odd, _ = place()
     side = jnp.where(odd, 0, 1)
     first = copies([(resist, resist_hbm)], sems)[0]
@@ -255,7 +284,8 @@
     second.wait()
 
 
-def across_kernel(own, odd_in, rows, rows_t, half_hbm, gradient_hbm, out, sems):
+def across_kernel(own, odd_in, rows, tables, half_hbm, gradient_hbm, out, sems):
+    rows_t = table_parts(tables)[-1]
     odd, alone = place()
     side = jnp.where(odd, 1, 0)
     extra = jnp.where(alone, 0.0, odd_in[...] * signs((BAND, WIDE)))
@@ -303,52 +333,42 @@
 
 def local(mask, target, kernel_table, kernel_weight, dose_table, condition_index):
     rows_table = np.concatenate(parts(waves(np.arange(MARGIN, MARGIN + CORE))), 0)
-    rows_t_table = np.ascontiguousarray(rows_table.T)
-    points = waves(STEP * np.arange(COARSE))
-    cosine, sine = points[:BAND], points[BAND:]
-    out = np.block([[cosine, -sine], [sine, cosine]])
-    back = np.block([[cosine.T, sine.T], [-sine.T, cosine.T]])
-    finer = side_by_side(interpolation())
-    coarse_tables = (
-        side_by_side(points), side_by_side(points.T), *parts(out), side_by_side(back),
-        finer, np.ascontiguousarray(finer.T),
-    )
+    tables = later_tables(rows_table)
     even, odd = partners(lax.axis_size("win"), lax.axis_size("tile"))
     over = ("win", "tile")
     f32, bf16 = jnp.float32, jnp.bfloat16
     small = ("v", (BAND, WIDE), f32)
     square = (CORE, CORE)
     dma, smem = pltpu.SemaphoreType.DMA, pltpu.SMEM
-    to_odd, rest, rows, rows_t = call(
+    to_odd, rest, rows = call(
         analyze_kernel,
-        "hhh",
-        [small, ("v", (WIDE, MARGIN), f32)] + [("v", square, bf16)] * 2,
-        [pltpu.VMEM(square, f32), dma((3,))],
-    )(*pinned(mask, rows_table, rows_t_table))
+        "hh",
+        [small, ("v", (WIDE, MARGIN), f32), ("v", square, bf16)],
+        [pltpu.VMEM(square, f32), dma((2,))],
+    )(*pinned(mask, rows_table))
     from_odd = lax.ppermute(to_odd, over, odd)
-    to_even, own = call(own_kernel, "vvv", [small, small])(rest, to_odd, rows_t)
+    to_even, own = call(own_kernel, "vvv", [small, small])(rest, to_odd, rows)
     from_even = lax.ppermute(to_even, over, even)
-    mixed, goal, *coarse = call(
+    mixed, goal, tables = call(
         prepare_kernel,
-        "v" + "h" * (5 + TABLES),
-        [("v", (PAIRS, 2, BAND, WIDE), f32), ("v", square, f32)]
-        + [("v", table.shape, bf16) for table in coarse_tables],
+        "v" + "h" * 6,
+        [("v", (PAIRS, 2, BAND, WIDE), f32), ("v", square, f32), ("v", tables.shape, bf16)],
         [
             pltpu.VMEM(square, f32),
             pltpu.VMEM((TABLE, KERN, 2, BAND, BAND), f32),
             smem((CONDS,), jnp.int32),
             smem((KERN, TABLE), f32),
             smem((TABLE,), f32),
-            dma((5 + TABLES,)),
+            dma((4 + TSPLIT + CSPLIT,)),
         ],
     )(
         own,
-        *pinned(condition_index, kernel_weight.T, dose_table, kernel_table, target, *coarse_tables),
+        *pinned(condition_index, kernel_weight.T, dose_table, kernel_table, target, tables),
     )
     joined = call(join_kernel, "vv", [small])(own, from_odd)
     resist, grad = call(
-        window_kernel, "v" * (4 + TABLES), [("v", (CONDS, CORE, CORE), f32), small]
-    )(joined, from_even, goal, mixed, *coarse)
+        window_kernel, "v" * 5, [("v", (CONDS, CORE, CORE), f32), small]
+    )(joined, from_even, goal, mixed, tables)
     from_odd = lax.ppermute(grad, over, odd)
     from_even = lax.ppermute(grad, over, even)
     strip = pltpu.VMEM((CORE, MARGIN), f32)
@@ -357,10 +377,10 @@
         "v" * 5,
         [("h", (CONDS, CORE, CORE), f32), ("h", square, f32)],
         [strip, dma((2,))],
-    )(grad, from_even, rows, rows_t, resist)
+    )(grad, from_even, rows, tables, resist)
     gradient = call(
         across_kernel, "vvvvh", [("h", square, f32)], [strip, dma((1,))], {4: 0}
-    )(grad, from_odd, rows, rows_t, gradient)
+    )(grad, from_odd, rows, tables, gradient)
     return (resist, gradient)
 
 

time: 14.8 us -> 14.7 us (level)
  Pallas kernels: 7.54 us -> 7.35 us
where the time goes in v5:
time: 14.7 us; the launch traced here: 14.5 us
  Pallas kernels  7.35 us (50%)
  starting transfers between devices  5.17 us (35%)
  waiting for transfers between devices  1.3 us (9%)
  between operations  0.69 us (5%)
    ppermute x1, starting transfers between devices, local(): from_odd = lax.ppermute(to_odd, over, odd)  3 us
    pallas_call x1, Pallas kernels, local(): call(window_kernel, 'v' * 5, [('v', (CONDS, CORE, CORE), f32), small])  1.87 us
    pallas_call x1, Pallas kernels, local(): call(prepare_kernel, 'v' + 'h' * 6, [('v', (PAIRS, 2, BAND, WIDE), f32),...  1.57 us
    ppermute x1, starting transfers between devices, local(): from_odd = lax.ppermute(grad, over, odd)  1.53 us
    pallas_call x1, Pallas kernels, local(): call(analyze_kernel, 'hh', [small, ('v', (WIDE, MARGIN), f32), ('v', squa...  1.45 us
    ppermute x1, waiting for transfers between devices, local(): from_odd = lax.ppermute(grad, over, odd)  1.29 us
    pallas_call x1, Pallas kernels, local(): call(beside_kernel, 'v' * 5, [('h', (CONDS, CORE, CORE), f32), ('h', squa...  1.09 us
    pallas_call x1, Pallas kernels, local(): call(across_kernel, 'vvvvh', [('h', square, f32)], [strip, dma((1,))], {4...  1.08 us
  transfers between devices with their start and end apart: 4, of which 1 were waited for; matrix products, arithmetic and copies ran while one was open for 0% of the time, Pallas kernels for 20%

profile of v5, /device:TPU:0, one launch (start us, length us, event | category | flops | bytes accessed | tf_op | source)
XLA Modules:
  0.0 14.5 jit_solution(12706038443208377760)
XLA Ops:
  0.6 1.5 %shard_map.95 = (f32[64,128]{1,0:T(8,128)S(1)}, f32[128,128]{1,0:T(8,128)S(1)}, bf16[256,256]{1,0:T(8,128)(2,1)S(1)}) custom-call(f32[256,256]{1,0:T(8,128)} %mask_hbm.1, bf16[256,256]{1,0:T(8,128)(2,1)} %constant.4.clone.rows_hbm), custom_call_target="tpu_custom_call" | custom-call | flops 1000000 | bytes 65536 | tf_op jit(solution)/shard_map/pallas_call | solution.py:343
  2.1 3.0 %collective-permute-start = (f32[64,128]{1,0:T(8,128)S(1)}, f32[64,128]{1,0:T(8,128)S(1)}, u32[]{:S(2)}, u32[]{:S(2)}) collective-permute-start(f32[64,128]{1,0:T(8,128)S(1)} %get-tuple-element.15.odd_out), channel_id=1, source_target_pairs={{1,2},{2,1},{3,4},{4,3},{5,6},{6,5},{7,8},{8,7},{9,10},{10,9},{11,... | collective-permute-start | bytes 98312 | tf_op jit(solution)/shard_map/ppermute | solution.py:349
  5.1 0.3 %shard_map.96 = (f32[64,128]{1,0:T(8,128)S(1)}, f32[64,128]{1,0:T(8,128)S(1)}) custom-call(f32[128,128]{1,0:T(8,128)S(1)} %get-tuple-element.14.rest, f32[64,128]{1,0:T(8,128)S(1)} %get-tuple-element.15.odd_out, bf16[256,256]{1,0:T(8,128)(2,1)S(1)} %get-tuple-element.16.rows), custom_call_target="tpu_custom_call" | custom-call | flops 1000000 | bytes 65536 | tf_op jit(solution)/shard_map/pallas_call | solution.py:350
  5.4 0.2 %collective-permute-start.1 = (f32[64,128]{1,0:T(8,128)S(1)}, f32[64,128]{1,0:T(8,128)S(1)}, u32[]{:S(2)}, u32[]{:S(2)}) collective-permute-start(f32[64,128]{1,0:T(8,128)S(1)} %get-tuple-element.18), channel_id=1, source_target_pairs={{0,1},{1,0},{2,3},{3,2},{4,5},{5,4},{6,7},{7,6},{8,9},{9,8},{10,11... | collective-permute-start | bytes 98312 | tf_op jit(solution)/shard_map/ppermute | solution.py:351
  5.6 1.6 %shard_map.98 = (f32[4,2,64,128]{3,2,1,0:T(8,128)S(1)}, f32[256,256]{1,0:T(8,128)S(1)}, bf16[1536,256]{1,0:T(8,128)(2,1)S(1)}) custom-call(f32[64,128]{1,0:T(8,128)S(1)} %get-tuple-element.17.own.after, s32[2]{0:T(128)} %index_hbm.1, f32[2,4]{1,0:T(2,128)} %bitcast.1, f32[4]{0:T(128)} %dose_hbm.1, f32[4,2,2,64,64]{4,3,2,1,0:T(8,128)} %table_hbm.1, ...), custom_call_target="tpu_custom_call" | custom-call | flops 1000000 | bytes 65536 | tf_op jit(solution)/shard_map/pallas_call | solution.py:352
  7.2 0.0 collective-permute-done.odd_in
  7.2 0.0 collective-permute-done.1.even_in
  7.2 1.9 %shard_map.99 = (f32[2,256,256]{2,1,0:T(8,128)S(1)}, f32[64,128]{1,0:T(8,128)S(1)}) custom-call(f32[64,128]{1,0:T(8,128)S(1)} %shard_map.97.joined, f32[64,128]{1,0:T(8,128)S(1)} %collective-permute-done.1.even_in, f32[256,256]{1,0:T(8,128)S(1)} %get-tuple-element.19.goal, f32[4,2,64,128]{3,2,1,0:T(8,128)S(1)} %get-tuple-element.20.mixed, ...), custom_call_target="tpu_custom_call" | custom-call | flops 1000000 | bytes 65536 | tf_op jit(solution)/shard_map/pallas_call | solution.py:369
  9.1 0.4 %collective-permute-start.2 = (f32[64,128]{1,0:T(8,128)S(1)}, f32[64,128]{1,0:T(8,128)S(1)}, u32[]{:S(2)}, u32[]{:S(2)}) collective-permute-start(f32[64,128]{1,0:T(8,128)S(1)} %get-tuple-element.22.own), channel_id=1, source_target_pairs={{0,1},{1,0},{2,3},{3,2},{4,5},{5,4},{6,7},{7,6},{8,9},{9,8},{10,11... | collective-permute-start | bytes 98312 | tf_op jit(solution)/shard_map/ppermute | solution.py:373
  9.5 1.5 %collective-permute-start.3 = (f32[64,128]{1,0:T(8,128)S(1)}, f32[64,128]{1,0:T(8,128)S(1)}, u32[]{:S(2)}, u32[]{:S(2)}) collective-permute-start(f32[64,128]{1,0:T(8,128)S(1)} %get-tuple-element.22.own), channel_id=1, source_target_pairs={{1,2},{2,1},{3,4},{4,3},{5,6},{6,5},{7,8},{8,7},{9,10},{10,9},{11,... | collective-permute-start | bytes 98312 | tf_op jit(solution)/shard_map/ppermute | solution.py:372
  11.0 0.0 collective-permute-done.2.even_in
  11.0 1.1 %shard_map.100 = (f32[2,256,256]{2,1,0:T(8,128)}, f32[256,256]{1,0:T(8,128)}) custom-call(f32[64,128]{1,0:T(8,128)S(1)} %get-tuple-element.22.own, f32[64,128]{1,0:T(8,128)S(1)} %collective-permute-done.2.even_in, bf16[256,256]{1,0:T(8,128)(2,1)S(1)} %get-tuple-element.16.rows, bf16[1536,256]{1,0:T(8,128)(2,1)S(1)} %get-tuple-element.21.tables, ...), custom_call_target="tpu_custom_call" | custom-call | flops 1000000 | bytes 65536 | tf_op jit(solution)/shard_map/pallas_call | solution.py:375
  12.1 1.3 %collective-permute-done.3.odd_in = f32[64,128]{1,0:T(8,128)S(1)} collective-permute-done((f32[64,128]{1,0:T(8,128)S(1)}, f32[64,128]{1,0:T(8,128)S(1)}, u32[]{:S(2)}, u32[]{:S(2)}) %collective-permute-start.3) | collective-permute-done | bytes 32800 | tf_op jit(solution)/shard_map/ppermute | solution.py:372
  13.4 1.1 %shard_map.101 = f32[256,256]{1,0:T(8,128)} custom-call(f32[64,128]{1,0:T(8,128)S(1)} %get-tuple-element.22.own, f32[64,128]{1,0:T(8,128)S(1)} %collective-permute-done.3.odd_in, bf16[256,256]{1,0:T(8,128)(2,1)S(1)} %get-tuple-element.16.rows, bf16[1536,256]{1,0:T(8,128)(2,1)S(1)} %get-tuple-element.21.tables, ...), custom_call_target="tpu_custom_call", output_to_operand_aliasing={{}: (4, {})} | custom-call | flops 1000000 | bytes 65536 | tf_op jit(solution)/shard_map/pallas_call | solution.py:381
  (1 shorter events, 0.0 us)
Async XLA Ops:
  2.1 5.1 %collective-permute-start = (f32[64,128]{1,0:T(8,128)S(1)}, f32[64,128]{1,0:T(8,128)S(1)}, u32[]{:S(2)}, u32[]{:S(2)}) collective-permute-start(f32[64,128]{1,0:T(8,128)S(1)} %get-tuple-element.15.odd_out), channel_id=1, source_target_pairs={{1,2},{2,1},{3,4},{4,3},{5,6},{6,5},{7,8},{8,7},{9,10},{10,9},{11,... | collective-permute-start | bytes 98312 | tf_op jit(solution)/shard_map/ppermute | solution.py:349
  5.4 1.8 %collective-permute-start.1 = (f32[64,128]{1,0:T(8,128)S(1)}, f32[64,128]{1,0:T(8,128)S(1)}, u32[]{:S(2)}, u32[]{:S(2)}) collective-permute-start(f32[64,128]{1,0:T(8,128)S(1)} %get-tuple-element.18), channel_id=1, source_target_pairs={{0,1},{1,0},{2,3},{3,2},{4,5},{5,4},{6,7},{7,6},{8,9},{9,8},{10,11... | collective-permute-start | bytes 98312 | tf_op jit(solution)/shard_map/ppermute | solution.py:351
  9.1 2.0 %collective-permute-start.2 = (f32[64,128]{1,0:T(8,128)S(1)}, f32[64,128]{1,0:T(8,128)S(1)}, u32[]{:S(2)}, u32[]{:S(2)}) collective-permute-start(f32[64,128]{1,0:T(8,128)S(1)} %get-tuple-element.22.own), channel_id=1, source_target_pairs={{0,1},{1,0},{2,3},{3,2},{4,5},{5,4},{6,7},{7,6},{8,9},{9,8},{10,11... | collective-permute-start | bytes 98312 | tf_op jit(solution)/shard_map/ppermute | solution.py:373
  9.5 3.9 %collective-permute-start.3 = (f32[64,128]{1,0:T(8,128)S(1)}, f32[64,128]{1,0:T(8,128)S(1)}, u32[]{:S(2)}, u32[]{:S(2)}) collective-permute-start(f32[64,128]{1,0:T(8,128)S(1)} %get-tuple-element.22.own), channel_id=1, source_target_pairs={{1,2},{2,1},{3,4},{4,3},{5,6},{6,5},{7,8},{8,7},{9,10},{10,9},{11,... | collective-permute-start | bytes 98312 | tf_op jit(solution)/shard_map/ppermute | solution.py:372

commit v6 on v5

--- a/solution.py
+++ b/solution.py
@@ -20,7 +20,6 @@
 CORE = 256
 PAIRS = CONDS * KERN
 WIDE = 2 * BAND
-CHUNK = 256
 COARSE = 2 * BAND
 STEP = NPAD // COARSE
 
@@ -54,17 +53,19 @@
 
 def later_tables(rows_table):
     points = waves(STEP * np.arange(COARSE))
-    cosine, sine = points[:BAND], points[BAND:]
-    out = np.block([[cosine, -sine], [sine, cosine]])
-    back = np.block([[cosine.T, sine.T], [-sine.T, cosine.T]])
+    core = waves(np.arange(MARGIN, MARGIN + CORE))
+    turned = np.concatenate([-core[BAND:], core[:BAND]], 0)
     finer = side_by_side(interpolation())
     return np.concatenate(
-        [side_by_side(points), side_by_side(points.T), *parts(out), side_by_side(back), finer, finer.T, rows_table.T]
+        [
+            side_by_side(points), side_by_side(points.T), *parts(turned),
+            finer, finer.T, rows_table.T, side_by_side(turned.T),
+        ]
     )
 
 
 def table_parts(tables):
-    ends = np.cumsum([WIDE, COARSE, WIDE, WIDE, 2 * COARSE, CORE, CORE, CORE])
+    ends = np.cumsum([WIDE, COARSE, WIDE, WIDE, CORE, CORE, 2 * CORE])
     return [tables.at[int(end - size) : int(end)] for end, size in zip(ends, np.diff(ends, prepend=0))]
 
 
@@ -178,12 +179,13 @@
     joined[...] = own[...] + jnp.where(alone, 0.0, odd_in[...])
 
 
-def window_kernel(joined, even_in, goal, mixed, tables, resist, grad):
-    points, points_t, out_high, out_low, back_both, finer, finer_t, _ = table_parts(tables)
+def window_kernel(joined, even_in, goal, mixed, rows, tables, resist, grad, odd_out):
+    points, points_t, turned_high, turned_low, finer, finer_t, back_both = table_parts(tables)
     spec = joined[...] + even_in[...]
     turned = turn(spec)
-    out_twice = jnp.concatenate([out_high[...], out_high[...]], 0)
-    finer_twice = jnp.concatenate([finer_t[:COARSE], finer_t[:COARSE]], 0)
+    out_high = jnp.concatenate([rows[:WIDE], turned_high[...]], 1)
+    out_low = jnp.concatenate([rows[WIDE:], turned_low[...]], 1)
+    out_twice = jnp.concatenate([out_high, out_high], 0)
     conditions = range(CONDS)
 
     def coarse_rows(condition):
@@ -196,38 +198,29 @@
     def coarse_field(y):
         y = jnp.concatenate([y[:, k * WIDE : (k + 1) * WIDE] for k in range(KERN)], 0)
         high, low = halves(y)
-        return dot(jnp.concatenate([high, low], 1), out_twice) + dot(high, out_low[...])
+        return dot(jnp.concatenate([high, low], 1), out_twice) + dot(high, out_low)
 
     def finer_rows(f):
         squares = f * f
         power = sum(
             squares[k * COARSE : (k + 1) * COARSE, c]
             for k in range(KERN)
-            for c in (slice(0, COARSE), slice(COARSE, 2 * COARSE))
+            for c in (slice(0, CORE), slice(CORE, 2 * CORE))
         )
         high, low = halves(power - 0.5 * steepness * threshold)
         both = jnp.concatenate([high, low], 1)
         both = dot(finer[...], jnp.concatenate([both, both], 0))
-        return both[:, :COARSE] + both[:, COARSE:]
-
-    def finer_columns(z):
-        z_high, z_low = halves(z)
-        return dot(jnp.concatenate([z_high, z_low], 1), finer_twice) + dot(z_high, finer_t[COARSE:])
-
-    def print_and_drive(condition, r, power):
+        return both[:, :CORE] + both[:, CORE:]
+
+    def print_and_drive(condition, power):
         t = jnp.tanh(power)
-        resist[condition, r] = 0.5 + 0.5 * t
-        return (t + goal[r]) * (1.0 - t * t)
-
-    def coarser_columns(drive):
+        resist[condition] = 0.5 + 0.5 * t
+        return (t + goal[...]) * (1.0 - t * t)
+
+    def coarser_rows(drive):
         high, low = halves(drive)
-        both = dot(high, finer[...])
-        return both[:, :COARSE] + both[:, COARSE:] + dot(low, finer[:, :COARSE])
-
-    def coarser_rows(w):
-        high, low = halves(w)
         both = dot(finer_t[:COARSE], jnp.concatenate([high, low], 1))
-        return both[:, :COARSE] + both[:, COARSE:] + dot(finer_t[COARSE:], high)
+        return both[:, :CORE] + both[:, CORE:] + dot(finer_t[COARSE:], high)
 
     def back_columns(drive, f):
         drive = jnp.concatenate([drive, drive], 1)
@@ -242,13 +235,9 @@
 
     y = [coarse_rows(c) for c in conditions]
     fields = [coarse_field(x) for x in y]
-    z = [finer_rows(f) for f in fields]
-    pieces = [slice(start, start + CHUNK) for start in range(0, CORE, CHUNK)]
-    power = [[finer_columns(z[c][r]) for c in conditions] for r in pieces]
-    drive = [[print_and_drive(c, r, p[c]) for c in conditions] for r, p in zip(pieces, power)]
-    w = [[coarser_columns(d[c]) for c in conditions] for d in drive]
-    w = [jnp.concatenate([x[c] for x in w], 0) for c in conditions]
-    drive = [coarser_rows(x) for x in w]
+    power = [finer_rows(f) for f in fields]
+    drive = [print_and_drive(c, power[c]) for c in conditions]
+    drive = [coarser_rows(x) for x in drive]
     q = [back_columns(drive[c], fields[c]) for c in conditions]
     u = [back_rows(x) for x in q]
     straight = jnp.zeros((BAND, WIDE), jnp.float32)
@@ -258,7 +247,10 @@
         top, bottom = u[i // KERN][:BAND, c], u[i // KERN][BAND:, c]
         straight = straight + (mixed[i, 0] * top + mixed[i, 1] * bottom)
         crossed = crossed + (mixed[i, 0] * bottom - mixed[i, 1] * top)
-    grad[...] = 2.0 * (straight + turn(crossed))
+    total = 2.0 * (straight + turn(crossed))
+    grad[...] = total
+    odd_out[:BAND] = total
+    odd_out[BAND:] = total[: odd_out.shape[0] - BAND]
 
 
 def synthesize(spec, rows, rows_t, side, out):
@@ -271,29 +263,30 @@
     out[...] = both[:, :MARGIN] + both[:, MARGIN:]
 
 
-def beside_kernel(own, even_in, rows, tables, resist, resist_hbm, gradient_hbm, out, sems):
-    rows_t = table_parts(tables)[-1]
+def store_kernel(resist, resist_hbm, sems):
+    for move in copies([(resist, resist_hbm)], sems):
+        move.wait()
+
+
+def beside_kernel(own, even_in, rows, tables, half):
     odd, _ = place()
-    side = jnp.where(odd, 0, 1)
-    first = copies([(resist, resist_hbm)], sems)[0]
-    synthesize(own[...] + even_in[...] * signs((BAND, WIDE)), rows, rows_t, side, out)
-    c = pl.ds(pl.multiple_of(side * MARGIN, MARGIN), MARGIN)
-    second = pltpu.make_async_copy(out, gradient_hbm.at[:, c], sems.at[1])
-    second.start()
-    first.wait()
-    second.wait()
-
-
-def across_kernel(own, odd_in, rows, tables, half_hbm, gradient_hbm, out, sems):
-    rows_t = table_parts(tables)[-1]
+    spec = own[...] + even_in[...] * signs((BAND, WIDE))
+    synthesize(spec, rows, table_parts(tables)[-1].at[:CORE], jnp.where(odd, 0, 1), half)
+
+
+def across_kernel(own, odd_in, rows, tables, half, gradient_hbm, out, sems):
     odd, alone = place()
     side = jnp.where(odd, 1, 0)
-    extra = jnp.where(alone, 0.0, odd_in[...] * signs((BAND, WIDE)))
-    synthesize(own[...] + extra, rows, rows_t, side, out)
-    c = pl.ds(pl.multiple_of(side * MARGIN, MARGIN), MARGIN)
-    move = pltpu.make_async_copy(out, gradient_hbm.at[:, c], sems.at[0])
-    move.start()
-    move.wait()
+
+    def columns(side):
+        return gradient_hbm.at[:, pl.ds(pl.multiple_of(side * MARGIN, MARGIN), MARGIN)]
+
+    moves = copies([(half, columns(1 - side))], sems)
+    extra = jnp.where(alone, 0.0, odd_in[:BAND] * signs((BAND, WIDE)))
+    synthesize(own[...] + extra, rows, table_parts(tables)[-1].at[:CORE], side, out)
+    moves += copies([(out, columns(side))], sems.at[1:])
+    for move in moves:
+        move.wait()
 
 
 def pinned(*arrays):
@@ -366,21 +359,21 @@
         *pinned(condition_index, kernel_weight.T, dose_table, kernel_table, target, tables),
     )
     joined = call(join_kernel, "vv", [small])(own, from_odd)
-    resist, grad = call(
-        window_kernel, "v" * 5, [("v", (CONDS, CORE, CORE), f32), small]
-    )(joined, from_even, goal, mixed, tables)
-    from_odd = lax.ppermute(grad, over, odd)
+    resist, grad, to_odd = call(
+        window_kernel,
+        "v" * 6,
+        [("v", (CONDS, CORE, CORE), f32), small, ("v", (BAND + 8, WIDE), f32)],
+    )(joined, from_even, goal, mixed, rows, tables)
+    from_odd = lax.ppermute(to_odd, over, odd)
     from_even = lax.ppermute(grad, over, even)
-    strip = pltpu.VMEM((CORE, MARGIN), f32)
-    resist, gradient = call(
-        beside_kernel,
-        "v" * 5,
-        [("h", (CONDS, CORE, CORE), f32), ("h", square, f32)],
-        [strip, dma((2,))],
-    )(grad, from_even, rows, tables, resist)
+    resist = call(store_kernel, "v", [("h", (CONDS, CORE, CORE), f32)], [dma((1,))])(resist)
+    half = call(beside_kernel, "vvvv", [("v", (CORE, MARGIN), f32)])(grad, from_even, rows, tables)
     gradient = call(
-        across_kernel, "vvvvh", [("h", square, f32)], [strip, dma((1,))], {4: 0}
-    )(grad, from_odd, rows, tables, gradient)
+        across_kernel,
+        "vvvvv",
+        [("h", square, f32)],
+        [pltpu.VMEM((CORE, MARGIN), f32), dma((2,))],
+    )(grad, from_odd, rows, tables, half)
     return (resist, gradient)
 
 

time: 14.7 us -> 14.3 us (0.973)
  waiting for transfers between devices: 1.3 us -> 0.91 us
    ppermute x1 -> x2, starting transfers between devices: 3 us -> 4.89 us  [local(): from_odd = lax.ppermute(to_odd, over, odd)]
    ppermute x1 -> x0, starting transfers between devices: 1.53 us -> none  [local(): from_odd = lax.ppermute(grad, over, odd)]
    ppermute x1 -> x0, waiting for transfers between devices: 1.29 us -> none  [local(): from_odd = lax.ppermute(grad, over, odd)]
    ppermute x1 -> x2, waiting for transfers between devices: 0.01 us -> 0.52 us  [local(): from_odd = lax.ppermute(to_odd, over, odd)]
    ppermute x1, starting transfers between devices: 0.43 us -> 0.01 us  [local(): from_even = lax.ppermute(grad, over, even)]
    ppermute x1, waiting for transfers between devices: 0.01 us -> 0.4 us  [local(): from_even = lax.ppermute(grad, over, even)]
    pallas_call x3 -> x4, Pallas kernels: 4.04 us -> 4.08 us  [the longest x1 1.78 us: local(): call(window_kernel, 'v' * 6, [('v', (CONDS, CORE, CORE), f32), small, ('v...]
  transfers between devices with their start and end apart: 4 -> 4, of which waited for: 1 -> 2; matrix products, arithmetic and copies ran while one was open for 0% -> 0% of each run, Pallas kernels for 20% -> 22%
where the time goes in v6:
time: 14.3 us; the launch traced here: 14.1 us
  Pallas kernels  7.39 us (52%)
  starting transfers between devices  5.1 us (36%)
  waiting for transfers between devices  0.91 us (6%)
  between operations  0.7 us (5%)
    ppermute x2, starting transfers between devices, local(): from_odd = lax.ppermute(to_odd, over, odd)  4.89 us
    pallas_call x1, Pallas kernels, local(): call(window_kernel, 'v' * 6, [('v', (CONDS, CORE, CORE), f32), small, ('v...  1.78 us
    pallas_call x1, Pallas kernels, local(): call(prepare_kernel, 'v' + 'h' * 6, [('v', (PAIRS, 2, BAND, WIDE), f32),...  1.57 us
    pallas_call x1, Pallas kernels, local(): call(analyze_kernel, 'hh', [small, ('v', (WIDE, MARGIN), f32), ('v', squa...  1.45 us
    pallas_call x1, Pallas kernels, local(): call(across_kernel, 'vvvvv', [('h', square, f32)], [pltpu.VMEM((CORE, MAR...  1.09 us
    pallas_call x1, Pallas kernels, local(): call(store_kernel, 'v', [('h', (CONDS, CORE, CORE), f32)], [dma((1,))])  0.8 us
    ppermute x2, waiting for transfers between devices, local(): from_odd = lax.ppermute(to_odd, over, odd)  0.52 us
    pallas_call x1, Pallas kernels, local(): call(beside_kernel, 'vvvv', [('v', (CORE, MARGIN), f32)])  0.41 us
  transfers between devices with their start and end apart: 4, of which 2 were waited for; matrix products, arithmetic and copies ran while one was open for 0% of the time, Pallas kernels for 22%

profile of v6, /device:TPU:0, one launch (start us, length us, event | category | flops | bytes accessed | tf_op | source)
XLA Modules:
  0.0 14.1 jit_solution(13580990894807289120)
XLA Ops:
  0.6 1.5 %shard_map.95 = (f32[64,128]{1,0:T(8,128)S(1)}, f32[128,128]{1,0:T(8,128)S(1)}, bf16[256,256]{1,0:T(8,128)(2,1)S(1)}) custom-call(f32[256,256]{1,0:T(8,128)} %mask_hbm.1, bf16[256,256]{1,0:T(8,128)(2,1)} %constant.4.clone.rows_hbm), custom_call_target="tpu_custom_call" | custom-call | flops 1000000 | bytes 65536 | tf_op jit(solution)/shard_map/pallas_call | solution.py:336
  2.1 3.0 %collective-permute-start = (f32[64,128]{1,0:T(8,128)S(1)}, f32[64,128]{1,0:T(8,128)S(1)}, u32[]{:S(2)}, u32[]{:S(2)}) collective-permute-start(f32[64,128]{1,0:T(8,128)S(1)} %get-tuple-element.14.odd_out), channel_id=1, source_target_pairs={{1,2},{2,1},{3,4},{4,3},{5,6},{6,5},{7,8},{8,7},{9,10},{10,9},{11,... | collective-permute-start | bytes 98312 | tf_op jit(solution)/shard_map/ppermute | solution.py:342
  5.1 0.3 %shard_map.96 = (f32[64,128]{1,0:T(8,128)S(1)}, f32[64,128]{1,0:T(8,128)S(1)}) custom-call(f32[128,128]{1,0:T(8,128)S(1)} %get-tuple-element.13.rest, f32[64,128]{1,0:T(8,128)S(1)} %get-tuple-element.14.odd_out, bf16[256,256]{1,0:T(8,128)(2,1)S(1)} %get-tuple-element.15.rows), custom_call_target="tpu_custom_call" | custom-call | flops 1000000 | bytes 65536 | tf_op jit(solution)/shard_map/pallas_call | solution.py:343
  5.4 0.2 %collective-permute-start.1 = (f32[64,128]{1,0:T(8,128)S(1)}, f32[64,128]{1,0:T(8,128)S(1)}, u32[]{:S(2)}, u32[]{:S(2)}) collective-permute-start(f32[64,128]{1,0:T(8,128)S(1)} %get-tuple-element.17), channel_id=1, source_target_pairs={{0,1},{1,0},{2,3},{3,2},{4,5},{5,4},{6,7},{7,6},{8,9},{9,8},{10,11... | collective-permute-start | bytes 98312 | tf_op jit(solution)/shard_map/ppermute | solution.py:344
  5.6 1.6 %shard_map.98 = (f32[4,2,64,128]{3,2,1,0:T(8,128)S(1)}, f32[256,256]{1,0:T(8,128)S(1)}, bf16[1536,256]{1,0:T(8,128)(2,1)S(1)}) custom-call(f32[64,128]{1,0:T(8,128)S(1)} %get-tuple-element.16.own.after, s32[2]{0:T(128)} %index_hbm.1, f32[2,4]{1,0:T(2,128)} %bitcast.1, f32[4]{0:T(128)} %dose_hbm.1, f32[4,2,2,64,64]{4,3,2,1,0:T(8,128)} %table_hbm.1, ...), custom_call_target="tpu_custom_call" | custom-call | flops 1000000 | bytes 65536 | tf_op jit(solution)/shard_map/pallas_call | solution.py:345
  7.2 0.0 collective-permute-done.odd_in
  7.2 0.0 collective-permute-done.1.even_in
  7.2 1.8 %shard_map.99 = (f32[2,256,256]{2,1,0:T(8,128)S(1)}, f32[64,128]{1,0:T(8,128)S(1)}, f32[72,128]{1,0:T(8,128)S(1)}) custom-call(f32[64,128]{1,0:T(8,128)S(1)} %shard_map.97.joined, f32[64,128]{1,0:T(8,128)S(1)} %collective-permute-done.1.even_in, f32[256,256]{1,0:T(8,128)S(1)} %get-tuple-element.18.goal, f32[4,2,64,128]{3,2,1,0:T(8,128)S(1)} %get-tuple-element.19.mixed, ...), custom_call_target="tpu_custom_call" | custom-call | flops 1000000 | bytes 65536 | tf_op jit(solution)/shard_map/pallas_call | solution.py:362
  9.0 1.9 %collective-permute-start.2 = (f32[72,128]{1,0:T(8,128)S(1)}, f32[72,128]{1,0:T(8,128)S(1)}, u32[]{:S(2)}, u32[]{:S(2)}) collective-permute-start(f32[72,128]{1,0:T(8,128)S(1)} %get-tuple-element.23), channel_id=1, source_target_pairs={{1,2},{2,1},{3,4},{4,3},{5,6},{6,5},{7,8},{8,7},{9,10},{10,9},{11,... | collective-permute-start | bytes 110600 | tf_op jit(solution)/shard_map/ppermute | solution.py:367
  10.9 0.0 collective-permute-start.3
  10.9 0.8 %shard_map.100 = f32[2,256,256]{2,1,0:T(8,128)} custom-call(f32[2,256,256]{2,1,0:T(8,128)S(1)} %get-tuple-element.21.resist), custom_call_target="tpu_custom_call" | custom-call | flops 1000000 | bytes 65536 | tf_op jit(solution)/shard_map/pallas_call | solution.py:369
  11.7 0.4 %collective-permute-done.3.even_in = f32[64,128]{1,0:T(8,128)S(1)} collective-permute-done((f32[64,128]{1,0:T(8,128)S(1)}, f32[64,128]{1,0:T(8,128)S(1)}, u32[]{:S(2)}, u32[]{:S(2)}) %collective-permute-start.3) | collective-permute-done | bytes 32800 | tf_op jit(solution)/shard_map/ppermute | solution.py:368
  12.1 0.4 %shard_map.101.half = f32[256,128]{1,0:T(8,128)S(1)} custom-call(f32[64,128]{1,0:T(8,128)S(1)} %get-tuple-element.22.own, f32[64,128]{1,0:T(8,128)S(1)} %collective-permute-done.3.even_in, bf16[256,256]{1,0:T(8,128)(2,1)S(1)} %get-tuple-element.15.rows, bf16[1536,256]{1,0:T(8,128)(2,1)S(1)} %get-tuple-element.20.tables), custom_call_target="tpu_custom_call" | custom-call | flops 1000000 | bytes 65536 | tf_op jit(solution)/shard_map/pallas_call | solution.py:370
  12.5 0.5 %collective-permute-done.2.odd_in = f32[72,128]{1,0:T(8,128)S(1)} collective-permute-done((f32[72,128]{1,0:T(8,128)S(1)}, f32[72,128]{1,0:T(8,128)S(1)}, u32[]{:S(2)}, u32[]{:S(2)}) %collective-permute-start.2) | collective-permute-done | bytes 36896 | tf_op jit(solution)/shard_map/ppermute | solution.py:367
  13.0 1.1 %shard_map.102 = f32[256,256]{1,0:T(8,128)} custom-call(f32[64,128]{1,0:T(8,128)S(1)} %get-tuple-element.22.own, f32[72,128]{1,0:T(8,128)S(1)} %collective-permute-done.2.odd_in, bf16[256,256]{1,0:T(8,128)(2,1)S(1)} %get-tuple-element.15.rows, bf16[1536,256]{1,0:T(8,128)(2,1)S(1)} %get-tuple-element.20.tables, f32[256,128]{1,0:T(8,128)S(1)} %shard_map.101.half), custom_call_target="tpu_custom_call" | custom-call | flops 1000000 | bytes 65536 | tf_op jit(solution)/shard_map/pallas_call | solution.py:371
  (1 shorter events, 0.0 us)
Async XLA Ops:
  2.1 5.1 %collective-permute-start = (f32[64,128]{1,0:T(8,128)S(1)}, f32[64,128]{1,0:T(8,128)S(1)}, u32[]{:S(2)}, u32[]{:S(2)}) collective-permute-start(f32[64,128]{1,0:T(8,128)S(1)} %get-tuple-element.14.odd_out), channel_id=1, source_target_pairs={{1,2},{2,1},{3,4},{4,3},{5,6},{6,5},{7,8},{8,7},{9,10},{10,9},{11,... | collective-permute-start | bytes 98312 | tf_op jit(solution)/shard_map/ppermute | solution.py:342
  5.4 1.8 %collective-permute-start.1 = (f32[64,128]{1,0:T(8,128)S(1)}, f32[64,128]{1,0:T(8,128)S(1)}, u32[]{:S(2)}, u32[]{:S(2)}) collective-permute-start(f32[64,128]{1,0:T(8,128)S(1)} %get-tuple-element.17), channel_id=1, source_target_pairs={{0,1},{1,0},{2,3},{3,2},{4,5},{5,4},{6,7},{7,6},{8,9},{9,8},{10,11... | collective-permute-start | bytes 98312 | tf_op jit(solution)/shard_map/ppermute | solution.py:344
  9.0 4.0 %collective-permute-start.2 = (f32[72,128]{1,0:T(8,128)S(1)}, f32[72,128]{1,0:T(8,128)S(1)}, u32[]{:S(2)}, u32[]{:S(2)}) collective-permute-start(f32[72,128]{1,0:T(8,128)S(1)} %get-tuple-element.23), channel_id=1, source_target_pairs={{1,2},{2,1},{3,4},{4,3},{5,6},{6,5},{7,8},{8,7},{9,10},{10,9},{11,... | collective-permute-start | bytes 110600 | tf_op jit(solution)/shard_map/ppermute | solution.py:367
  10.9 1.2 %collective-permute-start.3 = (f32[64,128]{1,0:T(8,128)S(1)}, f32[64,128]{1,0:T(8,128)S(1)}, u32[]{:S(2)}, u32[]{:S(2)}) collective-permute-start(f32[64,128]{1,0:T(8,128)S(1)} %get-tuple-element.22.own), channel_id=1, source_target_pairs={{0,1},{1,0},{2,3},{3,2},{4,5},{5,4},{6,7},{7,6},{8,9},{9,8},{10,11... | collective-permute-start | bytes 98312 | tf_op jit(solution)/shard_map/ppermute | solution.py:368

commit v7 on v6

--- a/solution.py
+++ b/solution.py
@@ -14,8 +14,6 @@
 BAND = 64
 KERN = 2
 TABLE = 4
-TSPLIT = 2
-CSPLIT = 3
 CONDS = 2
 CORE = 256
 PAIRS = CONDS * KERN
@@ -116,7 +114,10 @@
     return lax.dot_general(a, b, (((1,), (1,)), ((), ())), preferred_element_type=jnp.float32)
 
 
-def half_spectrum(z, rows, side):
+def half_spectrum(mask, rows, side):
+    high, low = halves(mask)
+    both = dot(rows[:WIDE], jnp.concatenate([high, low], 1))
+    z = both[:, :MARGIN] + both[:, MARGIN:] + dot(rows[WIDE:], high)
     columns = rows[:, pl.ds(pl.multiple_of(side * MARGIN, MARGIN), MARGIN)]
     both = across_lanes(
         jnp.concatenate(halves(z), 1), jnp.concatenate([columns, columns], 1)
@@ -125,16 +126,30 @@
     return (w[:BAND] + turn(w[BAND:])) * signs((BAND, WIDE))
 
 
-def analyze_kernel(mask_hbm, rows_hbm, odd_out, rest, rows, mask, sems):
-    for move in copies([(mask_hbm, mask), (rows_hbm, rows)], sems):
-        move.wait()
+def analyze_kernel(
+    mask_hbm, rows_hbm, table_hbm, target_hbm, odd_out, rest, rows, table, target, mask, sems
+):
     odd, _ = place()
-    high, low = halves(mask[...])
-    both = dot(rows[...], high)
-    z = both[:WIDE] + both[WIDE:] + dot(rows[:WIDE], low)
-    z_left, z_right = z[:, :MARGIN], z[:, MARGIN:]
-    rest[...] = jnp.where(odd, z_left, z_right)
-    odd_out[...] = half_spectrum(jnp.where(odd, z_right, z_left), rows, jnp.where(odd, 1, 0))
+    side = jnp.where(odd, 1, 0)
+
+    def half(side):
+        return mask_hbm.at[:, pl.ds(pl.multiple_of(side * MARGIN, MARGIN), MARGIN)]
+
+    moves = copies(
+        [
+            (half(side), mask),
+            (rows_hbm, rows),
+            (half(1 - side), rest),
+            (target_hbm, target),
+            *strips(table_hbm, table, TABLE // 2),
+        ],
+        sems,
+    )
+    for move in moves[:2]:
+        move.wait()
+    odd_out[...] = half_spectrum(mask[...], rows, side)
+    for move in moves[2:]:
+        move.wait()
 
 
 def own_kernel(rest, odd_out, rows, even_out, own):
@@ -145,20 +160,10 @@
 
 
 def prepare_kernel(
-    after, index_hbm, weight_hbm, dose_hbm, table_hbm, target_hbm, tables_hbm,
-    mixed, goal, tables, target, table, index, weight, dose, sems,
+    after, table, target, index_hbm, weight_hbm, dose_hbm, mixed, goal, index, weight, dose, sems
 ):
-    moves = copies(
-        [
-            (index_hbm, index),
-            (weight_hbm, weight),
-            (dose_hbm, dose),
-            *strips(table_hbm, table, TABLE // TSPLIT),
-            (target_hbm, target),
-            *strips(tables_hbm, tables, tables.shape[0] // CSPLIT),
-        ],
-        sems,
-    )
+    moves = copies([(index_hbm, index), (weight_hbm, weight), (dose_hbm, dose)], sems)
+    goal[...] = 1.0 - 2.0 * target[...]
     for move in moves:
         move.wait()
     for condition in range(CONDS):
@@ -171,7 +176,6 @@
                 kernel = table[entry, k, part]
                 doubled = jnp.concatenate([kernel, kernel], 1)
                 mixed[condition * KERN + k, part] = doubled * scale
-    goal[...] = 1.0 - 2.0 * target[...]
 
 
 def join_kernel(own, odd_in, joined):
@@ -333,31 +337,27 @@
     small = ("v", (BAND, WIDE), f32)
     square = (CORE, CORE)
     dma, smem = pltpu.SemaphoreType.DMA, pltpu.SMEM
-    to_odd, rest, rows = call(
+    half = ("v", (CORE, MARGIN), f32)
+    to_odd, rest, rows, table, target = call(
         analyze_kernel,
-        "hh",
-        [small, ("v", (WIDE, MARGIN), f32), ("v", square, bf16)],
-        [pltpu.VMEM(square, f32), dma((2,))],
-    )(*pinned(mask, rows_table))
+        "hhhh",
+        [small, half, ("v", square, bf16)] + [("v", x.shape, f32) for x in (kernel_table, target)],
+        [pltpu.VMEM((CORE, MARGIN), f32), dma((6,))],
+    )(*pinned(mask, rows_table, kernel_table, target))
     from_odd = lax.ppermute(to_odd, over, odd)
     to_even, own = call(own_kernel, "vvv", [small, small])(rest, to_odd, rows)
     from_even = lax.ppermute(to_even, over, even)
-    mixed, goal, tables = call(
+    mixed, goal = call(
         prepare_kernel,
-        "v" + "h" * 6,
-        [("v", (PAIRS, 2, BAND, WIDE), f32), ("v", square, f32), ("v", tables.shape, bf16)],
+        "vvvhhh",
+        [("v", (PAIRS, 2, BAND, WIDE), f32), ("v", square, f32)],
         [
-            pltpu.VMEM(square, f32),
-            pltpu.VMEM((TABLE, KERN, 2, BAND, BAND), f32),
             smem((CONDS,), jnp.int32),
             smem((KERN, TABLE), f32),
             smem((TABLE,), f32),
-            dma((4 + TSPLIT + CSPLIT,)),
+            dma((3,)),
         ],
-    )(
-        own,
-        *pinned(condition_index, kernel_weight.T, dose_table, kernel_table, target, tables),
-    )
+    )(own, table, target, *pinned(condition_index, kernel_weight.T, dose_table))
     joined = call(join_kernel, "vv", [small])(own, from_odd)
     resist, grad, to_odd = call(
         window_kernel,
@@ -367,13 +367,13 @@
     from_odd = lax.ppermute(to_odd, over, odd)
     from_even = lax.ppermute(grad, over, even)
     resist = call(store_kernel, "v", [("h", (CONDS, CORE, CORE), f32)], [dma((1,))])(resist)
-    half = call(beside_kernel, "vvvv", [("v", (CORE, MARGIN), f32)])(grad, from_even, rows, tables)
+    made = call(beside_kernel, "vvvv", [half])(grad, from_even, rows, tables)
     gradient = call(
         across_kernel,
         "vvvvv",
         [("h", square, f32)],
         [pltpu.VMEM((CORE, MARGIN), f32), dma((2,))],
-    )(grad, from_odd, rows, tables, half)
+    )(grad, from_odd, rows, tables, made)
     return (resist, gradient)
 
 

time: 14.3 us -> 14.1 us (0.986)
  Pallas kernels: 7.39 us -> 6.83 us
  starting transfers between devices: 5.1 us -> 5.3 us
  waiting for transfers between devices: 0.91 us -> 1.1 us
    pallas_call x3, Pallas kernels: 3.43 us -> 2.74 us  [the longest x1 1.46 us: local(): call(analyze_kernel, 'hhhh', [small, half, ('v', square, bf16)] + [('v',...]
    ppermute x2, starting transfers between devices: 4.89 us -> 5.09 us  [local(): from_odd = lax.ppermute(to_odd, over, odd)]
    ppermute x2, waiting for transfers between devices: 0.52 us -> 0.7 us  [local(): from_odd = lax.ppermute(to_odd, over, odd)]
  transfers between devices with their start and end apart: 4 -> 4, of which waited for: 2 -> 3; matrix products, arithmetic and copies ran while one was open for 0% -> 0% of each run, Pallas kernels for 22% -> 18%
where the time goes in v7:
time: 14.1 us; the launch traced here: 13.9 us
  Pallas kernels  6.83 us (48%)
  starting transfers between devices  5.3 us (38%)
  waiting for transfers between devices  1.1 us (8%)
  between operations  0.7 us (5%)
    ppermute x2, starting transfers between devices, local(): from_odd = lax.ppermute(to_odd, over, odd)  5.09 us
    pallas_call x1, Pallas kernels, local(): call(window_kernel, 'v' * 6, [('v', (CONDS, CORE, CORE), f32), small, ('v...  1.78 us
    pallas_call x1, Pallas kernels, local(): call(analyze_kernel, 'hhhh', [small, half, ('v', square, bf16)] + [('v',...  1.46 us
    pallas_call x1, Pallas kernels, local(): call(across_kernel, 'vvvvv', [('h', square, f32)], [pltpu.VMEM((CORE, MAR...  1.09 us
    pallas_call x1, Pallas kernels, local(): call(prepare_kernel, 'vvvhhh', [('v', (PAIRS, 2, BAND, WIDE), f32), ('v',...  0.87 us
    pallas_call x1, Pallas kernels, local(): call(store_kernel, 'v', [('h', (CONDS, CORE, CORE), f32)], [dma((1,))])  0.8 us
    ppermute x2, waiting for transfers between devices, local(): from_odd = lax.ppermute(to_odd, over, odd)  0.7 us
    pallas_call x1, Pallas kernels, local(): to_even, own = call(own_kernel, 'vvv', [small, small])(rest, to_odd, rows)  0.41 us
  transfers between devices with their start and end apart: 4, of which 3 were waited for; matrix products, arithmetic and copies ran while one was open for 0% of the time, Pallas kernels for 18%

profile of v7, /device:TPU:0, one launch (start us, length us, event | category | flops | bytes accessed | tf_op | source)
XLA Modules:
  0.0 13.9 jit_solution(4041259607346380654)
XLA Ops:
  0.6 1.5 %shard_map.95 = (f32[64,128]{1,0:T(8,128)S(1)}, f32[256,128]{1,0:T(8,128)S(1)}, bf16[256,256]{1,0:T(8,128)(2,1)S(1)}, f32[4,2,2,64,64]{4,3,2,1,0:T(8,128)S(1)}, f32[256,256]{1,0:T(8,128)S(1)}) custom-call(f32[256,256]{1,0:T(8,128)} %mask_hbm.1, bf16[256,256]{1,0:T(8,128)(2,1)} %constant.4.clone.rows_hbm, f32[4,2,2,64,64]{4,3,2,1,0:T(8,128)} %table_hbm.1, ...), custom_call_target="tpu_custom_call" | custom-call | flops 1000000 | bytes 65536 | tf_op jit(solution)/shard_map/pallas_call | solution.py:341
  2.1 0.0 copy-start
  2.1 3.0 %collective-permute-start = (f32[64,128]{1,0:T(8,128)S(1)}, f32[64,128]{1,0:T(8,128)S(1)}, u32[]{:S(2)}, u32[]{:S(2)}) collective-permute-start(f32[64,128]{1,0:T(8,128)S(1)} %get-tuple-element.15.odd_out), channel_id=1, source_target_pairs={{1,2},{2,1},{3,4},{4,3},{5,6},{6,5},{7,8},{8,7},{9,10},{10,9},{11,... | collective-permute-start | bytes 98312 | tf_op jit(solution)/shard_map/ppermute | solution.py:347
  5.1 0.4 %shard_map.96 = (f32[64,128]{1,0:T(8,128)S(1)}, f32[64,128]{1,0:T(8,128)S(1)}) custom-call(f32[256,128]{1,0:T(8,128)S(1)} %get-tuple-element.14.rest, f32[64,128]{1,0:T(8,128)S(1)} %get-tuple-element.15.odd_out, bf16[256,256]{1,0:T(8,128)(2,1)S(1)} %get-tuple-element.16.rows), custom_call_target="tpu_custom_call" | custom-call | flops 1000000 | bytes 65536 | tf_op jit(solution)/shard_map/pallas_call | solution.py:348
  5.5 0.2 %collective-permute-start.1 = (f32[64,128]{1,0:T(8,128)S(1)}, f32[64,128]{1,0:T(8,128)S(1)}, u32[]{:S(2)}, u32[]{:S(2)}) collective-permute-start(f32[64,128]{1,0:T(8,128)S(1)} %get-tuple-element.18), channel_id=1, source_target_pairs={{0,1},{1,0},{2,3},{3,2},{4,5},{5,4},{6,7},{7,6},{8,9},{9,8},{10,11... | collective-permute-start | bytes 98312 | tf_op jit(solution)/shard_map/ppermute | solution.py:349
  5.7 0.9 %shard_map.98 = (f32[4,2,64,128]{3,2,1,0:T(8,128)S(1)}, f32[256,256]{1,0:T(8,128)S(1)}) custom-call(f32[64,128]{1,0:T(8,128)S(1)} %get-tuple-element.17.own.after, f32[4,2,2,64,64]{4,3,2,1,0:T(8,128)S(1)} %get-tuple-element.19.table, f32[256,256]{1,0:T(8,128)S(1)} %get-tuple-element.20.target, s32[2]{0:T(128)} %index_hbm.1, f32[2,4]{1,0:T(2,128)} %bitcast.1, ...), custom_call_target="tpu_custom_call" | custom-call | flops 1000000 | bytes 65536 | tf_op jit(solution)/shard_map/pallas_call | solution.py:350
  6.6 0.4 %collective-permute-done.odd_in = f32[64,128]{1,0:T(8,128)S(1)} collective-permute-done((f32[64,128]{1,0:T(8,128)S(1)}, f32[64,128]{1,0:T(8,128)S(1)}, u32[]{:S(2)}, u32[]{:S(2)}) %collective-permute-start) | collective-permute-done | bytes 32800 | tf_op jit(solution)/shard_map/ppermute | solution.py:347
  7.0 0.0 collective-permute-done.1.even_in
  7.0 0.0 copy-done
  7.0 1.8 %shard_map.99 = (f32[2,256,256]{2,1,0:T(8,128)S(1)}, f32[64,128]{1,0:T(8,128)S(1)}, f32[72,128]{1,0:T(8,128)S(1)}) custom-call(f32[64,128]{1,0:T(8,128)S(1)} %shard_map.97.joined, f32[64,128]{1,0:T(8,128)S(1)} %collective-permute-done.1.even_in, f32[256,256]{1,0:T(8,128)S(1)} %get-tuple-element.21.goal, f32[4,2,64,128]{3,2,1,0:T(8,128)S(1)} %get-tuple-element.22.mixed, ...), custom_call_target="tpu_custom_call" | custom-call | flops 1000000 | bytes 65536 | tf_op jit(solution)/shard_map/pallas_call | solution.py:362
  8.8 2.1 %collective-permute-start.2 = (f32[72,128]{1,0:T(8,128)S(1)}, f32[72,128]{1,0:T(8,128)S(1)}, u32[]{:S(2)}, u32[]{:S(2)}) collective-permute-start(f32[72,128]{1,0:T(8,128)S(1)} %get-tuple-element.25), channel_id=1, source_target_pairs={{1,2},{2,1},{3,4},{4,3},{5,6},{6,5},{7,8},{8,7},{9,10},{10,9},{11,... | collective-permute-start | bytes 110600 | tf_op jit(solution)/shard_map/ppermute | solution.py:367
  10.9 0.0 collective-permute-start.3
  10.9 0.8 %shard_map.100 = f32[2,256,256]{2,1,0:T(8,128)} custom-call(f32[2,256,256]{2,1,0:T(8,128)S(1)} %get-tuple-element.23.resist), custom_call_target="tpu_custom_call" | custom-call | flops 1000000 | bytes 65536 | tf_op jit(solution)/shard_map/pallas_call | solution.py:369
  11.7 0.4 %collective-permute-done.3.even_in = f32[64,128]{1,0:T(8,128)S(1)} collective-permute-done((f32[64,128]{1,0:T(8,128)S(1)}, f32[64,128]{1,0:T(8,128)S(1)}, u32[]{:S(2)}, u32[]{:S(2)}) %collective-permute-start.3) | collective-permute-done | bytes 32800 | tf_op jit(solution)/shard_map/ppermute | solution.py:368
  12.1 0.4 %shard_map.101.half = f32[256,128]{1,0:T(8,128)S(1)} custom-call(f32[64,128]{1,0:T(8,128)S(1)} %get-tuple-element.24.own, f32[64,128]{1,0:T(8,128)S(1)} %collective-permute-done.3.even_in, bf16[256,256]{1,0:T(8,128)(2,1)S(1)} %get-tuple-element.16.rows, bf16[1536,256]{1,0:T(8,128)(2,1)S(1)} %copy-done), custom_call_target="tpu_custom_call" | custom-call | flops 1000000 | bytes 65536 | tf_op jit(solution)/shard_map/pallas_call | solution.py:370
  12.5 0.3 %collective-permute-done.2.odd_in = f32[72,128]{1,0:T(8,128)S(1)} collective-permute-done((f32[72,128]{1,0:T(8,128)S(1)}, f32[72,128]{1,0:T(8,128)S(1)}, u32[]{:S(2)}, u32[]{:S(2)}) %collective-permute-start.2) | collective-permute-done | bytes 36896 | tf_op jit(solution)/shard_map/ppermute | solution.py:367
  12.8 1.1 %shard_map.102 = f32[256,256]{1,0:T(8,128)} custom-call(f32[64,128]{1,0:T(8,128)S(1)} %get-tuple-element.24.own, f32[72,128]{1,0:T(8,128)S(1)} %collective-permute-done.2.odd_in, bf16[256,256]{1,0:T(8,128)(2,1)S(1)} %get-tuple-element.16.rows, bf16[1536,256]{1,0:T(8,128)(2,1)S(1)} %copy-done, f32[256,128]{1,0:T(8,128)S(1)} %shard_map.101.half), custom_call_target="tpu_custom_call" | custom-call | flops 1000000 | bytes 65536 | tf_op jit(solution)/shard_map/pallas_call | solution.py:371
  (1 shorter events, 0.0 us)
Async XLA Ops:
  2.1 4.9 %copy-start = (bf16[1536,256]{1,0:T(8,128)(2,1)S(1)}, bf16[1536,256]{1,0:T(8,128)(2,1)}, u32[]{:S(2)}) copy-start(bf16[1536,256]{1,0:T(8,128)(2,1)} %constant.5.clone.tables) | copy-start | bytes 2359300
  2.1 4.9 %collective-permute-start = (f32[64,128]{1,0:T(8,128)S(1)}, f32[64,128]{1,0:T(8,128)S(1)}, u32[]{:S(2)}, u32[]{:S(2)}) collective-permute-start(f32[64,128]{1,0:T(8,128)S(1)} %get-tuple-element.15.odd_out), channel_id=1, source_target_pairs={{1,2},{2,1},{3,4},{4,3},{5,6},{6,5},{7,8},{8,7},{9,10},{10,9},{11,... | collective-permute-start | bytes 98312 | tf_op jit(solution)/shard_map/ppermute | solution.py:347
  5.5 1.5 %collective-permute-start.1 = (f32[64,128]{1,0:T(8,128)S(1)}, f32[64,128]{1,0:T(8,128)S(1)}, u32[]{:S(2)}, u32[]{:S(2)}) collective-permute-start(f32[64,128]{1,0:T(8,128)S(1)} %get-tuple-element.18), channel_id=1, source_target_pairs={{0,1},{1,0},{2,3},{3,2},{4,5},{5,4},{6,7},{7,6},{8,9},{9,8},{10,11... | collective-permute-start | bytes 98312 | tf_op jit(solution)/shard_map/ppermute | solution.py:349
  8.8 4.0 %collective-permute-start.2 = (f32[72,128]{1,0:T(8,128)S(1)}, f32[72,128]{1,0:T(8,128)S(1)}, u32[]{:S(2)}, u32[]{:S(2)}) collective-permute-start(f32[72,128]{1,0:T(8,128)S(1)} %get-tuple-element.25), channel_id=1, source_target_pairs={{1,2},{2,1},{3,4},{4,3},{5,6},{6,5},{7,8},{8,7},{9,10},{10,9},{11,... | collective-permute-start | bytes 110600 | tf_op jit(solution)/shard_map/ppermute | solution.py:367
  10.9 1.2 %collective-permute-start.3 = (f32[64,128]{1,0:T(8,128)S(1)}, f32[64,128]{1,0:T(8,128)S(1)}, u32[]{:S(2)}, u32[]{:S(2)}) collective-permute-start(f32[64,128]{1,0:T(8,128)S(1)} %get-tuple-element.24.own), channel_id=1, source_target_pairs={{0,1},{1,0},{2,3},{3,2},{4,5},{5,4},{6,7},{7,6},{8,9},{9,8},{10,11... | collective-permute-start | bytes 98312 | tf_op jit(solution)/shard_map/ppermute | solution.py:368

commit v8 on v7

--- a/solution.py
+++ b/solution.py
@@ -200,7 +200,7 @@
         return dot(points_t[...], jnp.concatenate([high, high], 0)) + dot(points_t[:, :WIDE], low)
 
     def coarse_field(y):
-        y = jnp.concatenate([y[:, k * WIDE : (k + 1) * WIDE] for k in range(KERN)], 0)
+        y = jnp.concatenate([y[:, k * WIDE : (k + 1) * WIDE] for k in range(PAIRS)], 0)
         high, low = halves(y)
         return dot(jnp.concatenate([high, low], 1), out_twice) + dot(high, out_low)
 
@@ -238,7 +238,8 @@
         return dot(points[...], jnp.concatenate([high, high], 0)) + dot(points[:, :COARSE], low)
 
     y = [coarse_rows(c) for c in conditions]
-    fields = [coarse_field(x) for x in y]
+    fields = coarse_field(jnp.concatenate(y, 1))
+    fields = [fields[c * KERN * COARSE : (c + 1) * KERN * COARSE] for c in conditions]
     power = [finer_rows(f) for f in fields]
     drive = [print_and_drive(c, power[c]) for c in conditions]
     drive = [coarser_rows(x) for x in drive]
@@ -253,8 +254,7 @@
         crossed = crossed + (mixed[i, 0] * bottom - mixed[i, 1] * top)
     total = 2.0 * (straight + turn(crossed))
     grad[...] = total
-    odd_out[:BAND] = total
-    odd_out[BAND:] = total[: odd_out.shape[0] - BAND]
+    odd_out[...] = total
 
 
 def synthesize(spec, rows, rows_t, side, out):
@@ -286,9 +286,12 @@
         return gradient_hbm.at[:, pl.ds(pl.multiple_of(side * MARGIN, MARGIN), MARGIN)]
 
     moves = copies([(half, columns(1 - side))], sems)
-    extra = jnp.where(alone, 0.0, odd_in[:BAND] * signs((BAND, WIDE)))
-    synthesize(own[...] + extra, rows, table_parts(tables)[-1].at[:CORE], side, out)
-    moves += copies([(out, columns(side))], sems.at[1:])
+    extra = jnp.where(alone, 0.0, odd_in[...] * signs((BAND, WIDE)))
+    rows_t = table_parts(tables)[-1]
+    for i in range(2):
+        r = slice(i * CORE // 2, (i + 1) * CORE // 2)
+        synthesize(own[...] + extra, rows, rows_t.at[r], side, out.at[r])
+        moves += copies([(out.at[r], columns(side).at[r])], sems.at[1 + i :])
     for move in moves:
         move.wait()
 
@@ -362,7 +365,7 @@
     resist, grad, to_odd = call(
         window_kernel,
         "v" * 6,
-        [("v", (CONDS, CORE, CORE), f32), small, ("v", (BAND + 8, WIDE), f32)],
+        [("v", (CONDS, CORE, CORE), f32), small, small],
     )(joined, from_even, goal, mixed, rows, tables)
     from_odd = lax.ppermute(to_odd, over, odd)
     from_even = lax.ppermute(grad, over, even)
@@ -372,7 +375,7 @@
         across_kernel,
         "vvvvv",
         [("h", square, f32)],
-        [pltpu.VMEM((CORE, MARGIN), f32), dma((2,))],
+        [pltpu.VMEM((CORE, MARGIN), f32), dma((3,))],
     )(grad, from_odd, rows, tables, made)
     return (resist, gradient)
 

time: 14.1 us -> 14.2 us (level)
    ppermute x1, waiting for transfers between devices: 0.4 us -> 0.01 us  [local(): from_even = lax.ppermute(grad, over, even)]
    ppermute x2, waiting for transfers between devices: 0.7 us -> 1.08 us  [local(): from_odd = lax.ppermute(to_odd, over, odd)]
    ppermute x1, starting transfers between devices: 0.01 us -> 0.18 us  [local(): from_even = lax.ppermute(grad, over, even)]
  transfers between devices with their start and end apart: 4 -> 4, of which waited for: 3 -> 2; matrix products, arithmetic and copies ran while one was open for 0% -> 0% of each run, Pallas kernels for 18% -> 18%
where the time goes in v8:
time: 14.2 us; the launch traced here: 14 us
  Pallas kernels  6.84 us (48%)
  starting transfers between devices  5.38 us (38%)
  waiting for transfers between devices  1.09 us (8%)
  between operations  0.7 us (5%)
    ppermute x2, starting transfers between devices, local(): from_odd = lax.ppermute(to_odd, over, odd)  4.99 us
    pallas_call x1, Pallas kernels, local(): call(window_kernel, 'v' * 6, [('v', (CONDS, CORE, CORE), f32), small, sma...  1.81 us
    pallas_call x1, Pallas kernels, local(): call(analyze_kernel, 'hhhh', [small, half, ('v', square, bf16)] + [('v',...  1.46 us
    ppermute x2, waiting for transfers between devices, local(): from_odd = lax.ppermute(to_odd, over, odd)  1.08 us
    pallas_call x1, Pallas kernels, local(): call(across_kernel, 'vvvvv', [('h', square, f32)], [pltpu.VMEM((CORE, MAR...  1.07 us
    pallas_call x1, Pallas kernels, local(): call(prepare_kernel, 'vvvhhh', [('v', (PAIRS, 2, BAND, WIDE), f32), ('v',...  0.87 us
    pallas_call x1, Pallas kernels, local(): call(store_kernel, 'v', [('h', (CONDS, CORE, CORE), f32)], [dma((1,))])  0.8 us
    pallas_call x1, Pallas kernels, local(): to_even, own = call(own_kernel, 'vvv', [small, small])(rest, to_odd, rows)  0.41 us
  transfers between devices with their start and end apart: 4, of which 2 were waited for; matrix products, arithmetic and copies ran while one was open for 0% of the time, Pallas kernels for 18%

profile of v8, /device:TPU:0, one launch (start us, length us, event | category | flops | bytes accessed | tf_op | source)
XLA Modules:
  0.0 14.0 jit_solution(11585056805612063697)
XLA Ops:
  0.6 1.5 %shard_map.95 = (f32[64,128]{1,0:T(8,128)S(1)}, f32[256,128]{1,0:T(8,128)S(1)}, bf16[256,256]{1,0:T(8,128)(2,1)S(1)}, f32[4,2,2,64,64]{4,3,2,1,0:T(8,128)S(1)}, f32[256,256]{1,0:T(8,128)S(1)}) custom-call(f32[256,256]{1,0:T(8,128)} %mask_hbm.1, bf16[256,256]{1,0:T(8,128)(2,1)} %constant.4.clone.rows_hbm, f32[4,2,2,64,64]{4,3,2,1,0:T(8,128)} %table_hbm.1, ...), custom_call_target="tpu_custom_call" | custom-call | flops 1000000 | bytes 65536 | tf_op jit(solution)/shard_map/pallas_call | solution.py:344
  2.1 0.0 copy-start
  2.1 3.0 %collective-permute-start = (f32[64,128]{1,0:T(8,128)S(1)}, f32[64,128]{1,0:T(8,128)S(1)}, u32[]{:S(2)}, u32[]{:S(2)}) collective-permute-start(f32[64,128]{1,0:T(8,128)S(1)} %get-tuple-element.15.odd_out), channel_id=1, source_target_pairs={{1,2},{2,1},{3,4},{4,3},{5,6},{6,5},{7,8},{8,7},{9,10},{10,9},{11,... | collective-permute-start | bytes 98312 | tf_op jit(solution)/shard_map/ppermute | solution.py:350
  5.1 0.4 %shard_map.96 = (f32[64,128]{1,0:T(8,128)S(1)}, f32[64,128]{1,0:T(8,128)S(1)}) custom-call(f32[256,128]{1,0:T(8,128)S(1)} %get-tuple-element.14.rest, f32[64,128]{1,0:T(8,128)S(1)} %get-tuple-element.15.odd_out, bf16[256,256]{1,0:T(8,128)(2,1)S(1)} %get-tuple-element.16.rows), custom_call_target="tpu_custom_call" | custom-call | flops 1000000 | bytes 65536 | tf_op jit(solution)/shard_map/pallas_call | solution.py:351
  5.5 0.2 %collective-permute-start.1 = (f32[64,128]{1,0:T(8,128)S(1)}, f32[64,128]{1,0:T(8,128)S(1)}, u32[]{:S(2)}, u32[]{:S(2)}) collective-permute-start(f32[64,128]{1,0:T(8,128)S(1)} %get-tuple-element.18), channel_id=1, source_target_pairs={{0,1},{1,0},{2,3},{3,2},{4,5},{5,4},{6,7},{7,6},{8,9},{9,8},{10,11... | collective-permute-start | bytes 98312 | tf_op jit(solution)/shard_map/ppermute | solution.py:352
  5.7 0.9 %shard_map.98 = (f32[4,2,64,128]{3,2,1,0:T(8,128)S(1)}, f32[256,256]{1,0:T(8,128)S(1)}) custom-call(f32[64,128]{1,0:T(8,128)S(1)} %get-tuple-element.17.own.after, f32[4,2,2,64,64]{4,3,2,1,0:T(8,128)S(1)} %get-tuple-element.19.table, f32[256,256]{1,0:T(8,128)S(1)} %get-tuple-element.20.target, s32[2]{0:T(128)} %index_hbm.1, f32[2,4]{1,0:T(2,128)} %bitcast.1, ...), custom_call_target="tpu_custom_call" | custom-call | flops 1000000 | bytes 65536 | tf_op jit(solution)/shard_map/pallas_call | solution.py:353
  6.6 0.4 %collective-permute-done.odd_in = f32[64,128]{1,0:T(8,128)S(1)} collective-permute-done((f32[64,128]{1,0:T(8,128)S(1)}, f32[64,128]{1,0:T(8,128)S(1)}, u32[]{:S(2)}, u32[]{:S(2)}) %collective-permute-start) | collective-permute-done | bytes 32800 | tf_op jit(solution)/shard_map/ppermute | solution.py:350
  7.0 0.0 collective-permute-done.1.even_in
  7.0 0.0 copy-done
  7.0 1.8 %shard_map.99 = (f32[2,256,256]{2,1,0:T(8,128)S(1)}, f32[64,128]{1,0:T(8,128)S(1)}, f32[64,128]{1,0:T(8,128)S(1)}) custom-call(f32[64,128]{1,0:T(8,128)S(1)} %shard_map.97.joined, f32[64,128]{1,0:T(8,128)S(1)} %collective-permute-done.1.even_in, f32[256,256]{1,0:T(8,128)S(1)} %get-tuple-element.21.goal, f32[4,2,64,128]{3,2,1,0:T(8,128)S(1)} %get-tuple-element.22.mixed, ...), custom_call_target="tpu_custom_call" | custom-call | flops 1000000 | bytes 65536 | tf_op jit(solution)/shard_map/pallas_call | solution.py:365
  8.9 0.2 %collective-permute-start.3 = (f32[64,128]{1,0:T(8,128)S(1)}, f32[64,128]{1,0:T(8,128)S(1)}, u32[]{:S(2)}, u32[]{:S(2)}) collective-permute-start(f32[64,128]{1,0:T(8,128)S(1)} %get-tuple-element.24.own), channel_id=1, source_target_pairs={{0,1},{1,0},{2,3},{3,2},{4,5},{5,4},{6,7},{7,6},{8,9},{9,8},{10,11... | collective-permute-start | bytes 98312 | tf_op jit(solution)/shard_map/ppermute | solution.py:371
  9.0 2.0 %collective-permute-start.2 = (f32[64,128]{1,0:T(8,128)S(1)}, f32[64,128]{1,0:T(8,128)S(1)}, u32[]{:S(2)}, u32[]{:S(2)}) collective-permute-start(f32[64,128]{1,0:T(8,128)S(1)} %get-tuple-element.25), channel_id=1, source_target_pairs={{1,2},{2,1},{3,4},{4,3},{5,6},{6,5},{7,8},{8,7},{9,10},{10,9},{11,... | collective-permute-start | bytes 98312 | tf_op jit(solution)/shard_map/ppermute | solution.py:370
  11.0 0.8 %shard_map.100 = f32[2,256,256]{2,1,0:T(8,128)} custom-call(f32[2,256,256]{2,1,0:T(8,128)S(1)} %get-tuple-element.23.resist), custom_call_target="tpu_custom_call" | custom-call | flops 1000000 | bytes 65536 | tf_op jit(solution)/shard_map/pallas_call | solution.py:372
  11.8 0.0 collective-permute-done.3.even_in
  11.8 0.4 %shard_map.101.half = f32[256,128]{1,0:T(8,128)S(1)} custom-call(f32[64,128]{1,0:T(8,128)S(1)} %get-tuple-element.24.own, f32[64,128]{1,0:T(8,128)S(1)} %collective-permute-done.3.even_in, bf16[256,256]{1,0:T(8,128)(2,1)S(1)} %get-tuple-element.16.rows, bf16[1536,256]{1,0:T(8,128)(2,1)S(1)} %copy-done), custom_call_target="tpu_custom_call" | custom-call | flops 1000000 | bytes 65536 | tf_op jit(solution)/shard_map/pallas_call | solution.py:373
  12.3 0.7 %collective-permute-done.2.odd_in = f32[64,128]{1,0:T(8,128)S(1)} collective-permute-done((f32[64,128]{1,0:T(8,128)S(1)}, f32[64,128]{1,0:T(8,128)S(1)}, u32[]{:S(2)}, u32[]{:S(2)}) %collective-permute-start.2) | collective-permute-done | bytes 32800 | tf_op jit(solution)/shard_map/ppermute | solution.py:370
  12.9 1.1 %shard_map.102 = f32[256,256]{1,0:T(8,128)} custom-call(f32[64,128]{1,0:T(8,128)S(1)} %get-tuple-element.24.own, f32[64,128]{1,0:T(8,128)S(1)} %collective-permute-done.2.odd_in, bf16[256,256]{1,0:T(8,128)(2,1)S(1)} %get-tuple-element.16.rows, bf16[1536,256]{1,0:T(8,128)(2,1)S(1)} %copy-done, f32[256,128]{1,0:T(8,128)S(1)} %shard_map.101.half), custom_call_target="tpu_custom_call" | custom-call | flops 1000000 | bytes 65536 | tf_op jit(solution)/shard_map/pallas_call | solution.py:374
  (1 shorter events, 0.0 us)
Async XLA Ops:
  2.1 4.9 %copy-start = (bf16[1536,256]{1,0:T(8,128)(2,1)S(1)}, bf16[1536,256]{1,0:T(8,128)(2,1)}, u32[]{:S(2)}) copy-start(bf16[1536,256]{1,0:T(8,128)(2,1)} %constant.5.clone.tables) | copy-start | bytes 2359300
  2.1 4.9 %collective-permute-start = (f32[64,128]{1,0:T(8,128)S(1)}, f32[64,128]{1,0:T(8,128)S(1)}, u32[]{:S(2)}, u32[]{:S(2)}) collective-permute-start(f32[64,128]{1,0:T(8,128)S(1)} %get-tuple-element.15.odd_out), channel_id=1, source_target_pairs={{1,2},{2,1},{3,4},{4,3},{5,6},{6,5},{7,8},{8,7},{9,10},{10,9},{11,... | collective-permute-start | bytes 98312 | tf_op jit(solution)/shard_map/ppermute | solution.py:350
  5.5 1.5 %collective-permute-start.1 = (f32[64,128]{1,0:T(8,128)S(1)}, f32[64,128]{1,0:T(8,128)S(1)}, u32[]{:S(2)}, u32[]{:S(2)}) collective-permute-start(f32[64,128]{1,0:T(8,128)S(1)} %get-tuple-element.18), channel_id=1, source_target_pairs={{0,1},{1,0},{2,3},{3,2},{4,5},{5,4},{6,7},{7,6},{8,9},{9,8},{10,11... | collective-permute-start | bytes 98312 | tf_op jit(solution)/shard_map/ppermute | solution.py:352
  8.9 3.0 %collective-permute-start.3 = (f32[64,128]{1,0:T(8,128)S(1)}, f32[64,128]{1,0:T(8,128)S(1)}, u32[]{:S(2)}, u32[]{:S(2)}) collective-permute-start(f32[64,128]{1,0:T(8,128)S(1)} %get-tuple-element.24.own), channel_id=1, source_target_pairs={{0,1},{1,0},{2,3},{3,2},{4,5},{5,4},{6,7},{7,6},{8,9},{9,8},{10,11... | collective-permute-start | bytes 98312 | tf_op jit(solution)/shard_map/ppermute | solution.py:371
  9.0 3.9 %collective-permute-start.2 = (f32[64,128]{1,0:T(8,128)S(1)}, f32[64,128]{1,0:T(8,128)S(1)}, u32[]{:S(2)}, u32[]{:S(2)}) collective-permute-start(f32[64,128]{1,0:T(8,128)S(1)} %get-tuple-element.25), channel_id=1, source_target_pairs={{1,2},{2,1},{3,4},{4,3},{5,6},{6,5},{7,8},{8,7},{9,10},{10,9},{11,... | collective-permute-start | bytes 98312 | tf_op jit(solution)/shard_map/ppermute | solution.py:370

commit v9 on v7

--- a/solution.py
+++ b/solution.py
@@ -114,8 +114,8 @@
     return lax.dot_general(a, b, (((1,), (1,)), ((), ())), preferred_element_type=jnp.float32)
 
 
-def half_spectrum(mask, rows, side):
-    high, low = halves(mask)
+def half_spectrum(window, rows, side):
+    high, low = halves(window[:, pl.ds(pl.multiple_of(side * MARGIN, MARGIN), MARGIN)])
     both = dot(rows[:WIDE], jnp.concatenate([high, low], 1))
     z = both[:, :MARGIN] + both[:, MARGIN:] + dot(rows[WIDE:], high)
     columns = rows[:, pl.ds(pl.multiple_of(side * MARGIN, MARGIN), MARGIN)]
@@ -127,19 +127,13 @@
 
 
 def analyze_kernel(
-    mask_hbm, rows_hbm, table_hbm, target_hbm, odd_out, rest, rows, table, target, mask, sems
+    mask_hbm, rows_hbm, table_hbm, target_hbm, odd_out, mask, rows, table, target, sems
 ):
     odd, _ = place()
-    side = jnp.where(odd, 1, 0)
-
-    def half(side):
-        return mask_hbm.at[:, pl.ds(pl.multiple_of(side * MARGIN, MARGIN), MARGIN)]
-
     moves = copies(
         [
-            (half(side), mask),
+            (mask_hbm, mask),
             (rows_hbm, rows),
-            (half(1 - side), rest),
             (target_hbm, target),
             *strips(table_hbm, table, TABLE // 2),
         ],
@@ -147,14 +141,14 @@
     )
     for move in moves[:2]:
         move.wait()
-    odd_out[...] = half_spectrum(mask[...], rows, side)
+    odd_out[...] = half_spectrum(mask, rows, jnp.where(odd, 1, 0))
     for move in moves[2:]:
         move.wait()
 
 
-def own_kernel(rest, odd_out, rows, even_out, own):
+def own_kernel(mask, odd_out, rows, even_out, own):
     odd, _ = place()
-    even = half_spectrum(rest[...], rows, jnp.where(odd, 0, 1))
+    even = half_spectrum(mask, rows, jnp.where(odd, 0, 1))
     even_out[...] = even
     own[...] = (even + odd_out[...]) * signs((BAND, WIDE))
 
@@ -338,14 +332,14 @@
     square = (CORE, CORE)
     dma, smem = pltpu.SemaphoreType.DMA, pltpu.SMEM
     half = ("v", (CORE, MARGIN), f32)
-    to_odd, rest, rows, table, target = call(
+    to_odd, window, rows, table, target = call(
         analyze_kernel,
         "hhhh",
-        [small, half, ("v", square, bf16)] + [("v", x.shape, f32) for x in (kernel_table, target)],
-        [pltpu.VMEM((CORE, MARGIN), f32), dma((6,))],
+        [small, ("v", square, f32), ("v", square, bf16)] + [("v", x.shape, f32) for x in (kernel_table, target)],
+        [dma((5,))],
     )(*pinned(mask, rows_table, kernel_table, target))
     from_odd = lax.ppermute(to_odd, over, odd)
-    to_even, own = call(own_kernel, "vvv", [small, small])(rest, to_odd, rows)
+    to_even, own = call(own_kernel, "vvv", [small, small])(window, to_odd, rows)
     from_even = lax.ppermute(to_even, over, even)
     mixed, goal = call(
         prepare_kernel,

time: 14.1 us -> 14.1 us (level)
  no operation moved by 1% of the time
where the time goes in v9:
time: 14.1 us; the launch traced here: 13.9 us
  Pallas kernels  6.82 us (48%)
  starting transfers between devices  5.3 us (38%)
  waiting for transfers between devices  1.1 us (8%)
  between operations  0.7 us (5%)
    ppermute x2, starting transfers between devices, local(): from_odd = lax.ppermute(to_odd, over, odd)  5.09 us
    pallas_call x1, Pallas kernels, local(): call(window_kernel, 'v' * 6, [('v', (CONDS, CORE, CORE), f32), small, ('v...  1.78 us
    pallas_call x1, Pallas kernels, local(): call(analyze_kernel, 'hhhh', [small, ('v', square, f32), ('v', square, bf...  1.45 us
    pallas_call x1, Pallas kernels, local(): call(across_kernel, 'vvvvv', [('h', square, f32)], [pltpu.VMEM((CORE, MAR...  1.09 us
    pallas_call x1, Pallas kernels, local(): call(prepare_kernel, 'vvvhhh', [('v', (PAIRS, 2, BAND, WIDE), f32), ('v',...  0.87 us
    pallas_call x1, Pallas kernels, local(): call(store_kernel, 'v', [('h', (CONDS, CORE, CORE), f32)], [dma((1,))])  0.8 us
    ppermute x2, waiting for transfers between devices, local(): from_odd = lax.ppermute(to_odd, over, odd)  0.7 us
    pallas_call x1, Pallas kernels, local(): to_even, own = call(own_kernel, 'vvv', [small, small])(window, to_odd, rows)  0.42 us
  transfers between devices with their start and end apart: 4, of which 3 were waited for; matrix products, arithmetic and copies ran while one was open for 0% of the time, Pallas kernels for 18%

profile of v9, /device:TPU:0, one launch (start us, length us, event | category | flops | bytes accessed | tf_op | source)
XLA Modules:
  0.0 13.9 jit_solution(2077814468096684259)
XLA Ops:
  0.6 1.5 %shard_map.95 = (f32[64,128]{1,0:T(8,128)S(1)}, f32[256,256]{1,0:T(8,128)S(1)}, bf16[256,256]{1,0:T(8,128)(2,1)S(1)}, f32[4,2,2,64,64]{4,3,2,1,0:T(8,128)S(1)}, f32[256,256]{1,0:T(8,128)S(1)}) custom-call(f32[256,256]{1,0:T(8,128)} %mask_hbm.1, bf16[256,256]{1,0:T(8,128)(2,1)} %constant.4.clone.rows_hbm, f32[4,2,2,64,64]{4,3,2,1,0:T(8,128)} %table_hbm.1, ...), custom_call_target="tpu_custom_call" | custom-call | flops 1000000 | bytes 65536 | tf_op jit(solution)/shard_map/pallas_call | solution.py:335
  2.1 0.0 copy-start
  2.1 3.0 %collective-permute-start = (f32[64,128]{1,0:T(8,128)S(1)}, f32[64,128]{1,0:T(8,128)S(1)}, u32[]{:S(2)}, u32[]{:S(2)}) collective-permute-start(f32[64,128]{1,0:T(8,128)S(1)} %get-tuple-element.15.odd_out), channel_id=1, source_target_pairs={{1,2},{2,1},{3,4},{4,3},{5,6},{6,5},{7,8},{8,7},{9,10},{10,9},{11,... | collective-permute-start | bytes 98312 | tf_op jit(solution)/shard_map/ppermute | solution.py:341
  5.1 0.4 %shard_map.96 = (f32[64,128]{1,0:T(8,128)S(1)}, f32[64,128]{1,0:T(8,128)S(1)}) custom-call(f32[256,256]{1,0:T(8,128)S(1)} %get-tuple-element.14.mask, f32[64,128]{1,0:T(8,128)S(1)} %get-tuple-element.15.odd_out, bf16[256,256]{1,0:T(8,128)(2,1)S(1)} %get-tuple-element.16.rows), custom_call_target="tpu_custom_call" | custom-call | flops 1000000 | bytes 65536 | tf_op jit(solution)/shard_map/pallas_call | solution.py:342
  5.5 0.2 %collective-permute-start.1 = (f32[64,128]{1,0:T(8,128)S(1)}, f32[64,128]{1,0:T(8,128)S(1)}, u32[]{:S(2)}, u32[]{:S(2)}) collective-permute-start(f32[64,128]{1,0:T(8,128)S(1)} %get-tuple-element.18), channel_id=1, source_target_pairs={{0,1},{1,0},{2,3},{3,2},{4,5},{5,4},{6,7},{7,6},{8,9},{9,8},{10,11... | collective-permute-start | bytes 98312 | tf_op jit(solution)/shard_map/ppermute | solution.py:343
  5.7 0.9 %shard_map.98 = (f32[4,2,64,128]{3,2,1,0:T(8,128)S(1)}, f32[256,256]{1,0:T(8,128)S(1)}) custom-call(f32[64,128]{1,0:T(8,128)S(1)} %get-tuple-element.17.own.after, f32[4,2,2,64,64]{4,3,2,1,0:T(8,128)S(1)} %get-tuple-element.19.table, f32[256,256]{1,0:T(8,128)S(1)} %get-tuple-element.20.target, s32[2]{0:T(128)} %index_hbm.1, f32[2,4]{1,0:T(2,128)} %bitcast.1, ...), custom_call_target="tpu_custom_call" | custom-call | flops 1000000 | bytes 65536 | tf_op jit(solution)/shard_map/pallas_call | solution.py:344
  6.6 0.4 %collective-permute-done.odd_in = f32[64,128]{1,0:T(8,128)S(1)} collective-permute-done((f32[64,128]{1,0:T(8,128)S(1)}, f32[64,128]{1,0:T(8,128)S(1)}, u32[]{:S(2)}, u32[]{:S(2)}) %collective-permute-start) | collective-permute-done | bytes 32800 | tf_op jit(solution)/shard_map/ppermute | solution.py:341
  7.0 0.0 collective-permute-done.1.even_in
  7.0 0.0 copy-done
  7.0 1.8 %shard_map.99 = (f32[2,256,256]{2,1,0:T(8,128)S(1)}, f32[64,128]{1,0:T(8,128)S(1)}, f32[72,128]{1,0:T(8,128)S(1)}) custom-call(f32[64,128]{1,0:T(8,128)S(1)} %shard_map.97.joined, f32[64,128]{1,0:T(8,128)S(1)} %collective-permute-done.1.even_in, f32[256,256]{1,0:T(8,128)S(1)} %get-tuple-element.21.goal, f32[4,2,64,128]{3,2,1,0:T(8,128)S(1)} %get-tuple-element.22.mixed, ...), custom_call_target="tpu_custom_call" | custom-call | flops 1000000 | bytes 65536 | tf_op jit(solution)/shard_map/pallas_call | solution.py:356
  8.8 2.1 %collective-permute-start.2 = (f32[72,128]{1,0:T(8,128)S(1)}, f32[72,128]{1,0:T(8,128)S(1)}, u32[]{:S(2)}, u32[]{:S(2)}) collective-permute-start(f32[72,128]{1,0:T(8,128)S(1)} %get-tuple-element.25), channel_id=1, source_target_pairs={{1,2},{2,1},{3,4},{4,3},{5,6},{6,5},{7,8},{8,7},{9,10},{10,9},{11,... | collective-permute-start | bytes 110600 | tf_op jit(solution)/shard_map/ppermute | solution.py:361
  10.9 0.0 collective-permute-start.3
  10.9 0.8 %shard_map.100 = f32[2,256,256]{2,1,0:T(8,128)} custom-call(f32[2,256,256]{2,1,0:T(8,128)S(1)} %get-tuple-element.23.resist), custom_call_target="tpu_custom_call" | custom-call | flops 1000000 | bytes 65536 | tf_op jit(solution)/shard_map/pallas_call | solution.py:363
  11.7 0.4 %collective-permute-done.3.even_in = f32[64,128]{1,0:T(8,128)S(1)} collective-permute-done((f32[64,128]{1,0:T(8,128)S(1)}, f32[64,128]{1,0:T(8,128)S(1)}, u32[]{:S(2)}, u32[]{:S(2)}) %collective-permute-start.3) | collective-permute-done | bytes 32800 | tf_op jit(solution)/shard_map/ppermute | solution.py:362
  12.1 0.4 %shard_map.101.half = f32[256,128]{1,0:T(8,128)S(1)} custom-call(f32[64,128]{1,0:T(8,128)S(1)} %get-tuple-element.24.own, f32[64,128]{1,0:T(8,128)S(1)} %collective-permute-done.3.even_in, bf16[256,256]{1,0:T(8,128)(2,1)S(1)} %get-tuple-element.16.rows, bf16[1536,256]{1,0:T(8,128)(2,1)S(1)} %copy-done), custom_call_target="tpu_custom_call" | custom-call | flops 1000000 | bytes 65536 | tf_op jit(solution)/shard_map/pallas_call | solution.py:364
  12.5 0.3 %collective-permute-done.2.odd_in = f32[72,128]{1,0:T(8,128)S(1)} collective-permute-done((f32[72,128]{1,0:T(8,128)S(1)}, f32[72,128]{1,0:T(8,128)S(1)}, u32[]{:S(2)}, u32[]{:S(2)}) %collective-permute-start.2) | collective-permute-done | bytes 36896 | tf_op jit(solution)/shard_map/ppermute | solution.py:361
  12.8 1.1 %shard_map.102 = f32[256,256]{1,0:T(8,128)} custom-call(f32[64,128]{1,0:T(8,128)S(1)} %get-tuple-element.24.own, f32[72,128]{1,0:T(8,128)S(1)} %collective-permute-done.2.odd_in, bf16[256,256]{1,0:T(8,128)(2,1)S(1)} %get-tuple-element.16.rows, bf16[1536,256]{1,0:T(8,128)(2,1)S(1)} %copy-done, f32[256,128]{1,0:T(8,128)S(1)} %shard_map.101.half), custom_call_target="tpu_custom_call" | custom-call | flops 1000000 | bytes 65536 | tf_op jit(solution)/shard_map/pallas_call | solution.py:365
  (1 shorter events, 0.0 us)
Async XLA Ops:
  2.1 4.9 %copy-start = (bf16[1536,256]{1,0:T(8,128)(2,1)S(1)}, bf16[1536,256]{1,0:T(8,128)(2,1)}, u32[]{:S(2)}) copy-start(bf16[1536,256]{1,0:T(8,128)(2,1)} %constant.5.clone.tables) | copy-start | bytes 2359300
  2.1 4.9 %collective-permute-start = (f32[64,128]{1,0:T(8,128)S(1)}, f32[64,128]{1,0:T(8,128)S(1)}, u32[]{:S(2)}, u32[]{:S(2)}) collective-permute-start(f32[64,128]{1,0:T(8,128)S(1)} %get-tuple-element.15.odd_out), channel_id=1, source_target_pairs={{1,2},{2,1},{3,4},{4,3},{5,6},{6,5},{7,8},{8,7},{9,10},{10,9},{11,... | collective-permute-start | bytes 98312 | tf_op jit(solution)/shard_map/ppermute | solution.py:341
  5.5 1.5 %collective-permute-start.1 = (f32[64,128]{1,0:T(8,128)S(1)}, f32[64,128]{1,0:T(8,128)S(1)}, u32[]{:S(2)}, u32[]{:S(2)}) collective-permute-start(f32[64,128]{1,0:T(8,128)S(1)} %get-tuple-element.18), channel_id=1, source_target_pairs={{0,1},{1,0},{2,3},{3,2},{4,5},{5,4},{6,7},{7,6},{8,9},{9,8},{10,11... | collective-permute-start | bytes 98312 | tf_op jit(solution)/shard_map/ppermute | solution.py:343
  8.8 4.0 %collective-permute-start.2 = (f32[72,128]{1,0:T(8,128)S(1)}, f32[72,128]{1,0:T(8,128)S(1)}, u32[]{:S(2)}, u32[]{:S(2)}) collective-permute-start(f32[72,128]{1,0:T(8,128)S(1)} %get-tuple-element.25), channel_id=1, source_target_pairs={{1,2},{2,1},{3,4},{4,3},{5,6},{6,5},{7,8},{8,7},{9,10},{10,9},{11,... | collective-permute-start | bytes 110600 | tf_op jit(solution)/shard_map/ppermute | solution.py:361
  10.9 1.2 %collective-permute-start.3 = (f32[64,128]{1,0:T(8,128)S(1)}, f32[64,128]{1,0:T(8,128)S(1)}, u32[]{:S(2)}, u32[]{:S(2)}) collective-permute-start(f32[64,128]{1,0:T(8,128)S(1)} %get-tuple-element.24.own), channel_id=1, source_target_pairs={{0,1},{1,0},{2,3},{3,2},{4,5},{5,4},{6,7},{7,6},{8,9},{9,8},{10,11... | collective-permute-start | bytes 98312 | tf_op jit(solution)/shard_map/ppermute | solution.py:362

commit v10 on v9

--- a/solution.py
+++ b/solution.py
@@ -127,7 +127,7 @@
 
 
 def analyze_kernel(
-    mask_hbm, rows_hbm, table_hbm, target_hbm, odd_out, mask, rows, table, target, sems
+    mask_hbm, rows_hbm, target_hbm, odd_out, mask, rows, target, sems
 ):
     odd, _ = place()
     moves = copies(
@@ -135,7 +135,6 @@
             (mask_hbm, mask),
             (rows_hbm, rows),
             (target_hbm, target),
-            *strips(table_hbm, table, TABLE // 2),
         ],
         sems,
     )
@@ -154,9 +153,12 @@
 
 
 def prepare_kernel(
-    after, table, target, index_hbm, weight_hbm, dose_hbm, mixed, goal, index, weight, dose, sems
+    after, target, table_hbm, index_hbm, weight_hbm, dose_hbm, mixed, goal, table, index, weight, dose, sems
 ):
-    moves = copies([(index_hbm, index), (weight_hbm, weight), (dose_hbm, dose)], sems)
+    moves = copies(
+        strips(table_hbm, table, TABLE // 2) + [(index_hbm, index), (weight_hbm, weight), (dose_hbm, dose)],
+        sems,
+    )
     goal[...] = 1.0 - 2.0 * target[...]
     for move in moves:
         move.wait()
@@ -332,26 +334,27 @@
     square = (CORE, CORE)
     dma, smem = pltpu.SemaphoreType.DMA, pltpu.SMEM
     half = ("v", (CORE, MARGIN), f32)
-    to_odd, window, rows, table, target = call(
+    to_odd, window, rows, goal = call(
         analyze_kernel,
-        "hhhh",
-        [small, ("v", square, f32), ("v", square, bf16)] + [("v", x.shape, f32) for x in (kernel_table, target)],
-        [dma((5,))],
-    )(*pinned(mask, rows_table, kernel_table, target))
+        "hhh",
+        [small, ("v", square, f32), ("v", square, bf16)] + [("v", x.shape, f32) for x in (target,)],
+        [dma((3,))],
+    )(*pinned(mask, rows_table, target))
     from_odd = lax.ppermute(to_odd, over, odd)
     to_even, own = call(own_kernel, "vvv", [small, small])(window, to_odd, rows)
     from_even = lax.ppermute(to_even, over, even)
     mixed, goal = call(
         prepare_kernel,
-        "vvvhhh",
+        "vvhhhh",
         [("v", (PAIRS, 2, BAND, WIDE), f32), ("v", square, f32)],
         [
+            pltpu.VMEM((TABLE, KERN, 2, BAND, BAND), f32),
             smem((CONDS,), jnp.int32),
             smem((KERN, TABLE), f32),
             smem((TABLE,), f32),
-            dma((3,)),
+            dma((5,)),
         ],
-    )(own, table, target, *pinned(condition_index, kernel_weight.T, dose_table))
+    )(own, goal, *pinned(kernel_table, condition_index, kernel_weight.T, dose_table))
     joined = call(join_kernel, "vv", [small])(own, from_odd)
     resist, grad, to_odd = call(
         window_kernel,

time: 14.1 us -> 14.1 us (level)
  waiting for transfers between devices: 1.1 us -> 0.74 us
  Pallas kernels: 6.82 us -> 7.17 us
    ppermute x2, waiting for transfers between devices: 0.7 us -> 0.34 us  [local(): from_odd = lax.ppermute(to_odd, over, odd)]
    pallas_call x2, Pallas kernels: 2.32 us -> 2.67 us  [the longest x1 1.43 us: local(): call(analyze_kernel, 'hhh', [small, ('v', square, f32), ('v', square, bf1...]
  transfers between devices with their start and end apart: 4 -> 4, of which waited for: 3 -> 2; matrix products, arithmetic and copies ran while one was open for 0% -> 0% of each run, Pallas kernels for 18% -> 21%
where the time goes in v10:
time: 14.1 us; the launch traced here: 13.9 us
  Pallas kernels  7.17 us (51%)
  starting transfers between devices  5.29 us (38%)
  waiting for transfers between devices  0.74 us (5%)
  between operations  0.71 us (5%)
    ppermute x2, starting transfers between devices, local(): from_odd = lax.ppermute(to_odd, over, odd)  5.08 us
    pallas_call x1, Pallas kernels, local(): call(window_kernel, 'v' * 6, [('v', (CONDS, CORE, CORE), f32), small, ('v...  1.78 us
    pallas_call x1, Pallas kernels, local(): call(analyze_kernel, 'hhh', [small, ('v', square, f32), ('v', square, bf1...  1.43 us
    pallas_call x1, Pallas kernels, local(): call(prepare_kernel, 'vvhhhh', [('v', (PAIRS, 2, BAND, WIDE), f32), ('v',...  1.24 us
    pallas_call x1, Pallas kernels, local(): call(across_kernel, 'vvvvv', [('h', square, f32)], [pltpu.VMEM((CORE, MAR...  1.09 us
    pallas_call x1, Pallas kernels, local(): call(store_kernel, 'v', [('h', (CONDS, CORE, CORE), f32)], [dma((1,))])  0.8 us
    pallas_call x1, Pallas kernels, local(): to_even, own = call(own_kernel, 'vvv', [small, small])(window, to_odd, rows)  0.42 us
    pallas_call x1, Pallas kernels, local(): made = call(beside_kernel, 'vvvv', [half])(grad, from_even, rows, tables)  0.41 us
  transfers between devices with their start and end apart: 4, of which 2 were waited for; matrix products, arithmetic and copies ran while one was open for 0% of the time, Pallas kernels for 21%

profile of v10, /device:TPU:0, one launch (start us, length us, event | category | flops | bytes accessed | tf_op | source)
XLA Modules:
  0.0 13.9 jit_solution(4489645587093429102)
XLA Ops:
  0.6 1.4 %shard_map.95 = (f32[64,128]{1,0:T(8,128)S(1)}, f32[256,256]{1,0:T(8,128)S(1)}, bf16[256,256]{1,0:T(8,128)(2,1)S(1)}, f32[256,256]{1,0:T(8,128)S(1)}) custom-call(f32[256,256]{1,0:T(8,128)} %mask_hbm.1, bf16[256,256]{1,0:T(8,128)(2,1)} %constant.4.clone.rows_hbm, f32[256,256]{1,0:T(8,128)} %target_hbm.1), custom_call_target="tpu_custom_call" | custom-call | flops 1000000 | bytes 65536 | tf_op jit(solution)/shard_map/pallas_call | solution.py:337
  2.1 0.0 copy-start
  2.1 3.0 %collective-permute-start = (f32[64,128]{1,0:T(8,128)S(1)}, f32[64,128]{1,0:T(8,128)S(1)}, u32[]{:S(2)}, u32[]{:S(2)}) collective-permute-start(f32[64,128]{1,0:T(8,128)S(1)} %get-tuple-element.14.odd_out), channel_id=1, source_target_pairs={{1,2},{2,1},{3,4},{4,3},{5,6},{6,5},{7,8},{8,7},{9,10},{10,9},{11,... | collective-permute-start | bytes 98312 | tf_op jit(solution)/shard_map/ppermute | solution.py:343
  5.1 0.4 %shard_map.96 = (f32[64,128]{1,0:T(8,128)S(1)}, f32[64,128]{1,0:T(8,128)S(1)}) custom-call(f32[256,256]{1,0:T(8,128)S(1)} %get-tuple-element.13.mask, f32[64,128]{1,0:T(8,128)S(1)} %get-tuple-element.14.odd_out, bf16[256,256]{1,0:T(8,128)(2,1)S(1)} %get-tuple-element.15.rows), custom_call_target="tpu_custom_call" | custom-call | flops 1000000 | bytes 65536 | tf_op jit(solution)/shard_map/pallas_call | solution.py:344
  5.5 0.2 %collective-permute-start.1 = (f32[64,128]{1,0:T(8,128)S(1)}, f32[64,128]{1,0:T(8,128)S(1)}, u32[]{:S(2)}, u32[]{:S(2)}) collective-permute-start(f32[64,128]{1,0:T(8,128)S(1)} %get-tuple-element.17), channel_id=1, source_target_pairs={{0,1},{1,0},{2,3},{3,2},{4,5},{5,4},{6,7},{7,6},{8,9},{9,8},{10,11... | collective-permute-start | bytes 98312 | tf_op jit(solution)/shard_map/ppermute | solution.py:345
  5.7 1.2 %shard_map.98 = (f32[4,2,64,128]{3,2,1,0:T(8,128)S(1)}, f32[256,256]{1,0:T(8,128)S(1)}) custom-call(f32[64,128]{1,0:T(8,128)S(1)} %get-tuple-element.16.own.after, f32[256,256]{1,0:T(8,128)S(1)} %get-tuple-element.18.target, f32[4,2,2,64,64]{4,3,2,1,0:T(8,128)} %table_hbm.1, s32[2]{0:T(128)} %index_hbm.1, f32[2,4]{1,0:T(2,128)} %bitcast.1, f32[4]{0:T(128)} %dose_hbm.1), custom_call_target="tpu_custom_call" | custom-call | flops 1000000 | bytes 65536 | tf_op jit(solution)/shard_map/pallas_call | solution.py:346
  7.0 0.0 collective-permute-done.odd_in
  7.0 0.0 collective-permute-done.1.even_in
  7.0 0.0 copy-done
  7.0 1.8 %shard_map.99 = (f32[2,256,256]{2,1,0:T(8,128)S(1)}, f32[64,128]{1,0:T(8,128)S(1)}, f32[72,128]{1,0:T(8,128)S(1)}) custom-call(f32[64,128]{1,0:T(8,128)S(1)} %shard_map.97.joined, f32[64,128]{1,0:T(8,128)S(1)} %collective-permute-done.1.even_in, f32[256,256]{1,0:T(8,128)S(1)} %get-tuple-element.19.goal, f32[4,2,64,128]{3,2,1,0:T(8,128)S(1)} %get-tuple-element.20.mixed, ...), custom_call_target="tpu_custom_call" | custom-call | flops 1000000 | bytes 65536 | tf_op jit(solution)/shard_map/pallas_call | solution.py:359
  8.8 2.1 %collective-permute-start.2 = (f32[72,128]{1,0:T(8,128)S(1)}, f32[72,128]{1,0:T(8,128)S(1)}, u32[]{:S(2)}, u32[]{:S(2)}) collective-permute-start(f32[72,128]{1,0:T(8,128)S(1)} %get-tuple-element.23), channel_id=1, source_target_pairs={{1,2},{2,1},{3,4},{4,3},{5,6},{6,5},{7,8},{8,7},{9,10},{10,9},{11,... | collective-permute-start | bytes 110600 | tf_op jit(solution)/shard_map/ppermute | solution.py:364
  10.9 0.0 collective-permute-start.3
  10.9 0.8 %shard_map.100 = f32[2,256,256]{2,1,0:T(8,128)} custom-call(f32[2,256,256]{2,1,0:T(8,128)S(1)} %get-tuple-element.21.resist), custom_call_target="tpu_custom_call" | custom-call | flops 1000000 | bytes 65536 | tf_op jit(solution)/shard_map/pallas_call | solution.py:366
  11.7 0.4 %collective-permute-done.3.even_in = f32[64,128]{1,0:T(8,128)S(1)} collective-permute-done((f32[64,128]{1,0:T(8,128)S(1)}, f32[64,128]{1,0:T(8,128)S(1)}, u32[]{:S(2)}, u32[]{:S(2)}) %collective-permute-start.3) | collective-permute-done | bytes 32800 | tf_op jit(solution)/shard_map/ppermute | solution.py:365
  12.1 0.4 %shard_map.101.half = f32[256,128]{1,0:T(8,128)S(1)} custom-call(f32[64,128]{1,0:T(8,128)S(1)} %get-tuple-element.22.own, f32[64,128]{1,0:T(8,128)S(1)} %collective-permute-done.3.even_in, bf16[256,256]{1,0:T(8,128)(2,1)S(1)} %get-tuple-element.15.rows, bf16[1536,256]{1,0:T(8,128)(2,1)S(1)} %copy-done), custom_call_target="tpu_custom_call" | custom-call | flops 1000000 | bytes 65536 | tf_op jit(solution)/shard_map/pallas_call | solution.py:367
  12.5 0.3 %collective-permute-done.2.odd_in = f32[72,128]{1,0:T(8,128)S(1)} collective-permute-done((f32[72,128]{1,0:T(8,128)S(1)}, f32[72,128]{1,0:T(8,128)S(1)}, u32[]{:S(2)}, u32[]{:S(2)}) %collective-permute-start.2) | collective-permute-done | bytes 36896 | tf_op jit(solution)/shard_map/ppermute | solution.py:364
  12.8 1.1 %shard_map.102 = f32[256,256]{1,0:T(8,128)} custom-call(f32[64,128]{1,0:T(8,128)S(1)} %get-tuple-element.22.own, f32[72,128]{1,0:T(8,128)S(1)} %collective-permute-done.2.odd_in, bf16[256,256]{1,0:T(8,128)(2,1)S(1)} %get-tuple-element.15.rows, bf16[1536,256]{1,0:T(8,128)(2,1)S(1)} %copy-done, f32[256,128]{1,0:T(8,128)S(1)} %shard_map.101.half), custom_call_target="tpu_custom_call" | custom-call | flops 1000000 | bytes 65536 | tf_op jit(solution)/shard_map/pallas_call | solution.py:368
  (1 shorter events, 0.0 us)
Async XLA Ops:
  2.1 4.9 %copy-start = (bf16[1536,256]{1,0:T(8,128)(2,1)S(1)}, bf16[1536,256]{1,0:T(8,128)(2,1)}, u32[]{:S(2)}) copy-start(bf16[1536,256]{1,0:T(8,128)(2,1)} %constant.5.clone.tables) | copy-start | bytes 2359300
  2.1 4.9 %collective-permute-start = (f32[64,128]{1,0:T(8,128)S(1)}, f32[64,128]{1,0:T(8,128)S(1)}, u32[]{:S(2)}, u32[]{:S(2)}) collective-permute-start(f32[64,128]{1,0:T(8,128)S(1)} %get-tuple-element.14.odd_out), channel_id=1, source_target_pairs={{1,2},{2,1},{3,4},{4,3},{5,6},{6,5},{7,8},{8,7},{9,10},{10,9},{11,... | collective-permute-start | bytes 98312 | tf_op jit(solution)/shard_map/ppermute | solution.py:343
  5.5 1.5 %collective-permute-start.1 = (f32[64,128]{1,0:T(8,128)S(1)}, f32[64,128]{1,0:T(8,128)S(1)}, u32[]{:S(2)}, u32[]{:S(2)}) collective-permute-start(f32[64,128]{1,0:T(8,128)S(1)} %get-tuple-element.17), channel_id=1, source_target_pairs={{0,1},{1,0},{2,3},{3,2},{4,5},{5,4},{6,7},{7,6},{8,9},{9,8},{10,11... | collective-permute-start | bytes 98312 | tf_op jit(solution)/shard_map/ppermute | solution.py:345
  8.8 4.0 %collective-permute-start.2 = (f32[72,128]{1,0:T(8,128)S(1)}, f32[72,128]{1,0:T(8,128)S(1)}, u32[]{:S(2)}, u32[]{:S(2)}) collective-permute-start(f32[72,128]{1,0:T(8,128)S(1)} %get-tuple-element.23), channel_id=1, source_target_pairs={{1,2},{2,1},{3,4},{4,3},{5,6},{6,5},{7,8},{8,7},{9,10},{10,9},{11,... | collective-permute-start | bytes 110600 | tf_op jit(solution)/shard_map/ppermute | solution.py:364
  10.9 1.2 %collective-permute-start.3 = (f32[64,128]{1,0:T(8,128)S(1)}, f32[64,128]{1,0:T(8,128)S(1)}, u32[]{:S(2)}, u32[]{:S(2)}) collective-permute-start(f32[64,128]{1,0:T(8,128)S(1)} %get-tuple-element.22.own), channel_id=1, source_target_pairs={{0,1},{1,0},{2,3},{3,2},{4,5},{5,4},{6,7},{7,6},{8,9},{9,8},{10,11... | collective-permute-start | bytes 98312 | tf_op jit(solution)/shard_map/ppermute | solution.py:365
